TPU v7x, 256 devices: a whole 4x4x8 slice. The times are simulated.
256 devices in a mesh: ctx: 32 (over z, y_lo, core), tp: 8 (over y_hi, x).
Axes of the slice: x: 4, y: 4 (y_hi: 2, y_lo: 2; y = y_hi * 2 + y_lo), z: 8, core: 2. Of those that a mesh axis runs over, the one named last changes fastest.
Arguments:
- proj: bfloat16 [16384, 3, 4096], P('ctx', None, 'tp'), may hold values from -6 to 6
- short_filter: float32 [3, 3, 4096], P(None, None, 'tp'), may hold values from -3 to 3
- long_filter: float32 [16384, 4096], P(None, ('tp', 'ctx')), may hold values from -1 to 2.5
- out_weight: bfloat16 [4096, 4096], P('tp'), may hold values from -0.125 to 0.125
Outputs:
- block_out: bfloat16 [16384, 4096], P('ctx', 'tp')
All inputs are finite; a program needn't handle non-finite values.
Results may differ from a plain program's by a relative error of at most 0.0064.
Values may be sent and summed in bfloat16 or wider, within the bound.
No kernel may reach another device: no remote copies, remote signals or barrier semaphores. Data moves between devices by JAX's collectives and lax.ppermute only.
A program may use at most 64 MiB of HBM per device.

v0:
```python
import math

import jax
import jax.numpy as jnp
from jax import lax
from jax.sharding import PartitionSpec as P

inner_block = 128
highest = lax.Precision.HIGHEST


def shifted(block, axis, distance):
    devices = range(lax.axis_size(axis))
    route = [(i - distance, i) for i in devices if i - distance in devices]
    return lax.ppermute(block, axis, route)


def cosine_sine(left_index, right_index, modulus):
    angles = (
        2.0
        * math.pi
        / modulus
        * (left_index[:, None] * right_index[None, :] % modulus).astype(jnp.float32)
    )
    return (jnp.cos(angles), jnp.sin(angles))


def fourier_tables(length_rows):
    padded_len = 2 * length_rows
    outer_len = padded_len // inner_block
    outer_index = jnp.arange(outer_len, dtype=jnp.int32)
    inner_index = jnp.arange(inner_block, dtype=jnp.int32)
    outer_pair = cosine_sine(outer_index, outer_index, outer_len)
    turn_pair = cosine_sine(outer_index, inner_index, padded_len)
    inner_pair = cosine_sine(inner_index, inner_index, inner_block)
    return (outer_pair, turn_pair, inner_pair)


def spectrum(signal, tables):
    outer_cos, outer_sin = tables[0]
    turn_cos, turn_sin = tables[1]
    inner_cos, inner_sin = tables[2]
    outer_len = outer_cos.shape[0]
    half_rows = outer_len // 2
    channel_count = signal.shape[1]
    flattened = signal.reshape(half_rows, inner_block * channel_count)
    first_real = jnp.dot(outer_cos[:, :half_rows], flattened, precision=highest).reshape(
        outer_len, inner_block, channel_count
    )
    first_imag = -jnp.dot(outer_sin[:, :half_rows], flattened, precision=highest).reshape(
        outer_len, inner_block, channel_count
    )
    turn_c = turn_cos[:, :, None]
    turn_s = turn_sin[:, :, None]
    mid_real = first_real * turn_c + first_imag * turn_s
    mid_imag = first_imag * turn_c - first_real * turn_s
    out_real = jnp.einsum("kmc,ml->kcl", mid_real, inner_cos, precision=highest) + jnp.einsum(
        "kmc,ml->kcl", mid_imag, inner_sin, precision=highest
    )
    out_imag = jnp.einsum("kmc,ml->kcl", mid_imag, inner_cos, precision=highest) - jnp.einsum(
        "kmc,ml->kcl", mid_real, inner_sin, precision=highest
    )
    return (out_real, out_imag)


def inverse(prod_real, prod_imag, tables):
    outer_cos, outer_sin = tables[0]
    turn_cos, turn_sin = tables[1]
    inner_cos, inner_sin = tables[2]
    outer_len = outer_cos.shape[0]
    half_rows = outer_len // 2
    channel_count = prod_real.shape[1]
    section_real = jnp.einsum("kcl,lm->kcm", prod_real, inner_cos, precision=highest) - jnp.einsum(
        "kcl,lm->kcm", prod_imag, inner_sin, precision=highest
    )
    section_imag = jnp.einsum("kcl,lm->kcm", prod_imag, inner_cos, precision=highest) + jnp.einsum(
        "kcl,lm->kcm", prod_real, inner_sin, precision=highest
    )
    turn_c = turn_cos[:, None, :]
    turn_s = turn_sin[:, None, :]
    back_real = section_real * turn_c - section_imag * turn_s
    back_imag = section_imag * turn_c + section_real * turn_s
    result = jnp.einsum(
        "nk,kcm->cnm", outer_cos[:half_rows], back_real, precision=highest
    ) - jnp.einsum("nk,kcm->cnm", outer_sin[:half_rows], back_imag, precision=highest)
    return result.reshape(channel_count, half_rows * inner_block) / (outer_len * inner_block)


def body(proj, short_filter, long_filter, out_weight):
    local_rows = proj.shape[0]
    tap_count = short_filter.shape[1]
    edge_recv = shifted(proj[local_rows - (tap_count - 1) :], "ctx", 1)
    extended = jnp.concatenate([edge_recv, proj], axis=0)
    featured = jnp.zeros(proj.shape, jnp.float32)
    for tap_index in range(tap_count):
        begin = tap_count - 1 - tap_index
        featured = featured + short_filter[:, tap_index, :][None] * extended[
            begin : begin + local_rows
        ].astype(jnp.float32)
    gated_in = (featured[:, 1, :] * featured[:, 2, :]).astype(jnp.bfloat16)
    signal = lax.all_to_all(gated_in, "ctx", split_axis=1, concat_axis=0, tiled=True)
    tables = fourier_tables(signal.shape[0])
    signal_real, signal_imag = spectrum(signal.astype(jnp.float32), tables)
    filter_real, filter_imag = spectrum(long_filter, tables)
    prod_real = signal_real * filter_real - signal_imag * filter_imag
    prod_imag = signal_real * filter_imag + signal_imag * filter_real
    convolved = inverse(prod_real, prod_imag, tables).astype(jnp.bfloat16)
    returned = lax.all_to_all(convolved, "ctx", split_axis=1, concat_axis=0, tiled=True)
    gated_out = (featured[:, 0, :] * returned.T.astype(jnp.float32)).astype(jnp.bfloat16)
    summed = lax.psum_scatter(
        lax.dot_general(
            out_weight, gated_out, (((0,), (1,)), ((), ())), preferred_element_type=jnp.float32
        ),
        "tp",
        scatter_dimension=0,
        tiled=True,
    )
    return summed.T.astype(jnp.bfloat16)


def solution(mesh):
    placed = (P("ctx", None, "tp"), P(None, None, "tp"), P(None, ("tp", "ctx")), P("tp", None))
    return jax.shard_map(
        body, mesh=mesh, in_specs=placed, out_specs=P("ctx", "tp"), check_vma=False
    )
```

profile of v0, /device:TPU:1, one launch (start us, length us, event | category | flops | bytes accessed | tf_op | source)
XLA Modules:
  0.0 272.6 jit_solution(5721259728283670727)
XLA Ops:
  6.5 0.7 slice.47
  7.3 1.0 copy.23
  8.3 4.6 %collective-permute-start = (bf16[2,3,512]{0,2,1:T(8,128)(2,1)}, bf16[2,3,512]{0,2,1:T(8,128)(2,1)}, u32[]{:S(2)}, u32[]{:S(2)}) collective-permute-start(bf16[2,3,512]{0,2,1:T(8,128)(2,1)} %copy.23), channel_id=1, source_target_pairs={{0,8},{8,16},{16,24},{24,32},{32,40},{40,48},{48,56},{56,64},{64,7... | collective-permute-start | bytes 18440 | tf_op jit(solution)/shard_map/ppermute | solution.py:15
  12.8 1.7 fusion.52
  14.5 1.7 fusion.51
  16.2 0.5 fusion.73
  16.7 0.9 fusion.138
  17.6 6.3 %copy.29 = f32[16384,16]{1,0:T(8,128)} copy(f32[16384,16]{0,1:T(8,128)} %param.6) | data formatting | bytes 2097152 | tf_op args[2]
  23.8 7.9 %reshape.106 = f32[128,2048]{1,0:T(8,128)S(1)} reshape(f32[16384,16]{1,0:T(8,128)} %copy.29) | data formatting | bytes 2097152 | tf_op jit(solution)/shard_map/reshape | solution.py:46
  31.7 0.3 copy.30
  32.0 0.0 copy-start.7
  32.0 3.0 %fusion.30 = f32[256,128,16]{1,0,2:T(8,128)S(1)} fusion(f32[128,16,128]{2,1,0:T(8,128)S(1)} %bitcast.79, f32[256,256]{1,0:T(8,128)} %fusion.52), kind=kOutput, calls=%fused_computation.41 | convolution fusion | flops 805306368 | bytes 3276800 | tf_op jit(solution)/shard_map/dot_general | solution.py:47
  35.0 0.0 copy-done.7
  35.0 2.0 fusion.28
  37.0 0.0 copy-start
  37.0 3.5 %fusion.38 = f32[256,16,128]{2,0,1:T(8,128)} fusion(f32[256,128,16]{1,0,2:T(8,128)S(1)} %fusion.30, f32[256,128,16]{1,0,2:T(8,128)S(1)} %fusion.28, f32[256,128]{1,0:T(8,128)S(1)} %get-tuple-element.12, f32[256,128]{1,0:T(8,128)S(1)} %get-tuple-element.13), kind=kOutput, calls=%fused_computation.50 | convolution fusion | flops 807632896 | bytes 6553600 | tf_op jit(solution)/shard_map/kmc,ml->kcl/dot_general | solution.py:57
  40.6 0.0 copy-done
  40.6 2.6 copy.22
  43.2 0.0 collective-permute-done
  43.2 4.5 %multiply_add_fusion = f32[512,3,512]{0,2,1:T(8,128)S(1)} fusion(bf16[512,3,512]{0,2,1:T(8,128)(2,1)} %copy.22, bf16[2,3,512]{0,2,1:T(8,128)(2,1)} %collective-permute-done, f32[3,512]{1,0:T(4,128)S(1)} %get-tuple-element.10, f32[3,512]{1,0:T(4,128)S(1)} %get-tuple-element.11, f32[3,512]{1,0:T(4,128)S(1)} %bitcast.86), kind=kLoop, calls=%fused_computation.1 | loop fusion | flops 11010048 | bytes 4743168 | tf_op jit(solution)/shard_map/add | solution.py:97
  47.7 0.0 copy-start.2
  47.7 1.7 copy-done.2
  49.4 0.9 fusion.21
  50.3 9.1 %all-to-all-start = ((bf16[512,32,16]{0,2,1:T(8,128)(2,1)}), bf16[512,32,16]{0,2,1:T(8,128)(2,1)S(1)}, u32[]{:S(2)}, u32[]{:S(2)}) async-start(bf16[512,32,16]{0,2,1:T(8,128)(2,1)} %bitcast.2), calls=%async_computation | async-start | bytes 1048576 | tf_op jit(solution)/shard_map/all_to_all | solution.py:101
  59.4 0.6 reduce-scatter.2.cloned.1.call-start
  60.0 0.0 copy-start.1
  60.0 0.0 copy-start.3
  60.0 3.9 %fusion.39 = f32[256,16,128]{2,0,1:T(8,128)S(1)} fusion(f32[256,128,16]{1,0,2:T(8,128)S(1)} %fusion.30, f32[256,128,16]{1,0,2:T(8,128)} %copy-done, f32[256,128]{1,0:T(8,128)S(1)} %get-tuple-element.12, f32[256,128]{1,0:T(8,128)S(1)} %get-tuple-element.13), kind=kOutput, calls=%fused_computation.51 | convolution fusion | flops 807632896 | bytes 6553600 | tf_op jit(solution)/shard_map/kmc,ml->kcl/dot_general | solution.py:60
  63.9 0.0 copy-done.1
  63.9 0.0 copy-done.3
  63.9 3.6 %convolution_add_fusion.1 = f32[256,16,128]{2,0,1:T(8,128)} fusion(f32[256,16,128]{2,0,1:T(8,128)S(1)} %copy-done.3, f32[256,128,16]{1,0,2:T(8,128)S(1)} %fusion.30, f32[256,128,16]{1,0,2:T(8,128)S(1)} %copy-done.1, f32[256,128]{1,0:T(8,128)S(1)} %get-tuple-element.12, f32[256,128]{1,0:T(8,128)S(1)} %get-tuple-element.13), kind=kOutput, calls=%fused_computation.22 | convolution fusion | flops 808157184 | bytes 8650752 | tf_op jit(solution)/shard_map/kmc,ml->kcl/dot_general | solution.py:57
  67.6 3.5 %convolution_subtract_fusion.1 = f32[256,16,128]{2,0,1:T(8,128)} fusion(f32[256,16,128]{2,0,1:T(8,128)S(1)} %fusion.39, f32[256,128,16]{1,0,2:T(8,128)S(1)} %fusion.30, f32[256,128,16]{1,0,2:T(8,128)S(1)} %copy-done.1, f32[256,128]{1,0:T(8,128)S(1)} %get-tuple-element.12, f32[256,128]{1,0:T(8,128)S(1)} %get-tuple-element.13), kind=kOutput, calls=%fused_computation.20 | convolution fusion | flops 808157184 | bytes 8650752 | tf_op jit(solution)/shard_map/kmc,ml->kcl/dot_general | solution.py:60
  71.1 4.9 %all-to-all-done = bf16[512,32,16]{0,2,1:T(8,128)(2,1)S(1)} async-done(((bf16[512,32,16]{0,2,1:T(8,128)(2,1)}), bf16[512,32,16]{0,2,1:T(8,128)(2,1)S(1)}, u32[]{:S(2)}, u32[]{:S(2)}) %all-to-all-start) | async-done | bytes 524320 | tf_op jit(solution)/shard_map/all_to_all | solution.py:101
  76.0 3.1 %copy.25 = bf16[32,512,16]{2,1,0:T(8,128)(2,1)} copy(bf16[32,512,16]{1,2,0:T(8,128)(2,1)S(1)} %bitcast.84) | data formatting | bytes 1048576 | tf_op jit(solution)/shard_map/all_to_all | solution.py:101
  79.0 8.4 %reshape.105 = bf16[128,2048]{1,0:T(8,128)(2,1)S(1)} reshape(bf16[32,512,16]{2,1,0:T(8,128)(2,1)} %copy.25) | data formatting | bytes 1048576 | tf_op jit(solution)/shard_map/reshape | solution.py:46
  87.4 0.0 copy-start.8
  87.4 0.3 copy.26
  87.7 0.0 copy-done.6
  87.7 1.0 fusion.34
  88.7 0.0 copy-done.8
  88.7 1.0 fusion.32
  89.7 2.3 fusion.36
  92.0 2.2 fusion.37
  94.2 0.0 copy-start.4
  94.3 0.0 copy-start.5
  94.3 2.3 convolution_add_fusion.2
  96.6 0.0 copy-done.4
  96.6 0.0 copy-done.5
  96.6 2.8 %multiply_add_fusion.1 = (f32[256,16,128]{2,0,1:T(8,128)S(1)}, f32[256,16,128]{2,0,1:T(8,128)S(1)}) fusion(f32[256,16,128]{2,0,1:T(8,128)S(1)} %copy-done.4, f32[256,16,128]{2,0,1:T(8,128)S(1)} %convolution_add_fusion.2, f32[256,16,128]{2,0,1:T(8,128)S(1)} %copy-done.5, f32[256,16,128]{2,0,1:T(8,128)S(1)} %fusion.37, f32[256,128,16]{1,0,2:T(8,128)S(1)} %fusion.34, ...), kind=kOutput, calls=%fused_computation.10 | convolution fusion | flops 811302912 | bytes 17039360 | tf_op jit(solution)/shard_map/kmc,ml->kcl/dot_general | solution.py:60
  99.4 2.4 fusion.65
  101.8 2.1 fusion.63
  103.9 2.1 convolution_subtract_fusion
  106.0 2.1 convolution_add_fusion
  108.1 3.6 %fusion = f32[16,128,128]{2,1,0:T(8,128)S(1)} fusion(f32[256,16,128]{2,0,1:T(8,128)S(1)} %convolution_subtract_fusion, f32[256,16,128]{2,0,1:T(8,128)S(1)} %convolution_add_fusion, f32[256,128]{1,0:T(8,128)S(1)} %get-tuple-element.12, f32[256,128]{1,0:T(8,128)S(1)} %get-tuple-element.13, f32[256,256]{1,0:T(8,128)S(1)} %copy-done.8), kind=kOutput, calls=%fused_computation.2 | convolution fusion | flops 806879232 | bytes 5636096 | tf_op jit(solution)/shard_map/nk,kcm->cnm/dot_general | solution.py:85
  111.7 3.8 %fusion.18 = bf16[16,128,128]{1,2,0:T(8,128)(2,1)S(1)} fusion(f32[16,128,128]{2,1,0:T(8,128)S(1)} %fusion, f32[256,16,128]{2,0,1:T(8,128)S(1)} %convolution_add_fusion, f32[256,16,128]{2,0,1:T(8,128)S(1)} %convolution_subtract_fusion, f32[256,128]{1,0:T(8,128)S(1)} %get-tuple-element.12, f32[256,128]{1,0:T(8,128)S(1)} %get-tuple-element.13, ...), kind=kOutput, calls=%fused_computation.29 | convolution fusion | flops 807665664 | bytes 6160384 | tf_op jit(solution)/shard_map/nk,kcm->cnm/dot_general | solution.py:83
  115.5 0.3 copy.35
  115.8 0.3 convert_element_type.135
  116.1 0.3 copy.36
  116.4 21.0 %all_to_all.23 = bf16[16,32,512]{2,0,1:T(8,128)(2,1)S(1)} all-to-all(bf16[16,32,512]{2,0,1:T(8,128)(2,1)S(1)} %copy.36), channel_id=1, replica_groups=mesh['ctx'=32,'tp'=8] {'ctx'}, dimensions={1} | all-to-all | bytes 1048576 | tf_op jit(solution)/shard_map/all_to_all | solution.py:108
  137.4 1.4 fusion.23
  138.7 7.8 %convolution_bitcast_fusion = f32[4096,512]{0,1:T(8,128)} fusion(bf16[512,512]{0,1:T(8,128)(2,1)S(1)} %fusion.23, bf16[512,4096]{1,0:T(8,128)(2,1)} %param.7), kind=kOutput, calls=%fused_computation | convolution fusion | flops 2147483648 | bytes 13107200 | tf_op jit(solution)/shard_map/dot_general | solution.py:111
  146.6 0.0 reduce-scatter.2.cloned.1.call-update
  146.6 116.9 %reduce-scatter.2.cloned.1.call-done = f32[512,512]{0,1:T(8,128)} async-done(((f32[4096,512]{0,1:T(8,128)}), f32[512,512]{0,1:T(8,128)}) %reduce-scatter.2.cloned.1.call-update) | async-done | bytes 1048592 | tf_op jit(solution)/shard_map/reduce_scatter | solution.py:110
  263.4 2.1 convert_bitcast_fusion
  (3 shorter events, 0.0 us)
Async XLA Ops:
  8.3 34.9 %collective-permute-start = (bf16[2,3,512]{0,2,1:T(8,128)(2,1)}, bf16[2,3,512]{0,2,1:T(8,128)(2,1)}, u32[]{:S(2)}, u32[]{:S(2)}) collective-permute-start(bf16[2,3,512]{0,2,1:T(8,128)(2,1)} %copy.23), channel_id=1, source_target_pairs={{0,8},{8,16},{16,24},{24,32},{32,40},{40,48},{48,56},{56,64},{64,7... | collective-permute-start | bytes 18440 | tf_op jit(solution)/shard_map/ppermute | solution.py:15
  32.0 3.0 %copy-start.7 = (f32[256,256]{1,0:T(8,128)S(1)}, f32[256,256]{1,0:T(8,128)}, u32[]{:S(2)}) copy-start(f32[256,256]{1,0:T(8,128)} %fusion.51) | copy-start | bytes 786436
  37.0 3.5 %copy-start = (f32[256,128,16]{1,0,2:T(8,128)}, f32[256,128,16]{1,0,2:T(8,128)S(1)}, u32[]{:S(2)}) copy-start(f32[256,128,16]{1,0,2:T(8,128)S(1)} %fusion.28) | copy-start | bytes 6291460
  47.7 1.7 copy-start.2
  50.3 25.6 %all-to-all-start = ((bf16[512,32,16]{0,2,1:T(8,128)(2,1)}), bf16[512,32,16]{0,2,1:T(8,128)(2,1)S(1)}, u32[]{:S(2)}, u32[]{:S(2)}) async-start(bf16[512,32,16]{0,2,1:T(8,128)(2,1)} %bitcast.2), calls=%async_computation | async-start | bytes 1048576 | tf_op jit(solution)/shard_map/all_to_all | solution.py:101
  59.4 204.0 %reduce-scatter.2.cloned.1.call-start = ((), (), s32[]{:S(2)}) async-start(), calls=%async_computation.3 | async-start | bytes 9437184 | tf_op jit(solution)/shard_map/reduce_scatter | solution.py:110
  60.0 4.0 %copy-start.1 = (f32[256,128,16]{1,0,2:T(8,128)S(1)}, f32[256,128,16]{1,0,2:T(8,128)}, u32[]{:S(2)}) copy-start(f32[256,128,16]{1,0,2:T(8,128)} %copy-done) | copy-start | bytes 6291460
  60.0 4.0 %copy-start.3 = (f32[256,16,128]{2,0,1:T(8,128)S(1)}, f32[256,16,128]{2,0,1:T(8,128)}, u32[]{:S(2)}) copy-start(f32[256,16,128]{2,0,1:T(8,128)} %fusion.38) | copy-start | bytes 6291460
  79.0 8.7 %copy-start.6 = (f32[256,256]{1,0:T(8,128)S(1)}, f32[256,256]{1,0:T(8,128)}, u32[]{:S(2)}) copy-start(f32[256,256]{1,0:T(8,128)} %fusion.52) | copy-start | bytes 786436
  87.4 1.3 copy-start.8
  94.2 2.3 copy-start.4
  94.3 2.3 copy-start.5
Sparse Core Ops, SparseCore 0:
  146.7 116.6 reduce-scatter.1
where the time goes:
time: 276 us; the launch traced here: 273 us
  waiting for transfers between devices  122 us (44%)
  matrix products  55 us (20%)
  local copies, waits for them, and re-layouts  34 us (12%)
  blocking collectives  21 us (8%)
  starting transfers between devices  14.2 us (5%)
  between operations  14 us (5%)
  other arithmetic  12.8 us (5%)
    reduce_scatter x1, waiting for transfers between devices, body(): lax.psum_scatter(lax.dot_general(out_weight, gated_out, (((0,), (1,)), ((...  117 us
    all_to_all x1, blocking collectives, body(): lax.all_to_all(convolved, 'ctx', split_axis=1, concat_axis=0, tiled=True)  21 us
    reshape x2, local copies, waits for them, and re-layouts, spectrum(): flattened = signal.reshape(half_rows, inner_block * channel_count)  16.2 us
    unnamed x22, local copies, waits for them, and re-layouts  10.6 us
    all_to_all x1, starting transfers between devices, body(): lax.all_to_all(gated_in, 'ctx', split_axis=1, concat_axis=0, tiled=True)  9.08 us
    dot_general x1, matrix products, body(): lax.dot_general(out_weight, gated_out, (((0,), (1,)), ((), ())), preferre...  7.82 us
    dot_general x2, matrix products, spectrum(): jnp.einsum('kmc,ml->kcl', mid_real, inner_sin, precision=highest)  6.29 us
    dot_general x2, matrix products, spectrum(): jnp.einsum('kmc,ml->kcl', mid_imag, inner_cos, precision=highest)  6.16 us
  transfers between devices with their start and end apart: 3, of which 2 were waited for; matrix products, arithmetic and copies ran while one was open for 15% of the time, Pallas kernels for 0%

commit v1 on v0

v1 whole, which is shorter than its diff:
```python
import functools

import jax
import jax.numpy as jnp
import numpy as np
from jax import lax
from jax.experimental import pallas as pl
from jax.experimental.pallas import tpu as pltpu
from jax.sharding import Mesh, PartitionSpec as P

CTX = ("z", "yl", "core")
SIDE = 128
LENGTH = SIDE * SIDE
f32, bf16 = jnp.float32, jnp.bfloat16


def halves(table):
    high = table.astype(bf16)
    low = (table - high.astype(np.float64)).astype(bf16)
    return np.stack([high, low])


def tables():
    i = np.arange(SIDE)
    first = 2 * np.pi * np.outer(i + 0.25, i) / SIDE
    turn = 2 * np.pi * np.outer(i + 0.25, i) / LENGTH
    second = 2 * np.pi * np.outer(i, i) / SIDE
    c1, s1, c2, s2 = np.cos(first), np.sin(first), np.cos(second), np.sin(second)
    fwd1 = np.concatenate([c1, s1], 0)
    fwd2 = np.block([[c2, s2], [-s2, c2]])
    inv1 = np.block([[c2, -s2], [s2, c2]])
    inv2 = np.concatenate([c1.T, s1.T], 1) / LENGTH
    twist = np.stack([np.cos(turn), np.sin(turn)]).astype(np.float32)
    return halves(fwd1), halves(fwd2), halves(inv1), halves(inv2), twist


def split(x):
    high = x.astype(bf16)
    return high, (x - high.astype(f32)).astype(bf16)


def mm(a, b):
    return jnp.dot(a, b, preferred_element_type=f32)


def left3(tab, x):
    high, low = split(x)
    return mm(tab[0], high) + (mm(tab[1], high) + mm(tab[0], low))


def right3(x, tab):
    high, low = split(x)
    return mm(high, tab[0]) + (mm(low, tab[0]) + mm(high, tab[1]))


def forward(first, twist, tab2):
    spectra = []
    tc, ts = twist[0], twist[1]
    for w in range(first.shape[1] // SIDE):
        re, im = first[:SIDE, w * SIDE : (w + 1) * SIDE], first[SIDE:, w * SIDE : (w + 1) * SIDE]
        turned = jnp.concatenate([re * tc - im * ts, re * ts + im * tc], 1)
        spectra.append(right3(turned, tab2))
    return spectra


def filter_kernel(h_ref, fwd1_ref, fwd2_ref, twist_ref, out_ref, rows):
    channels = h_ref.shape[0]
    for n in range(SIDE):
        rows[n * channels : (n + 1) * channels, :] = h_ref[:, n * SIDE : (n + 1) * SIDE]

    def step(p, carry):
        pair = [rows[pl.ds(2 * p + w, SIDE, stride=channels), :] for w in range(2)]
        first = left3(fwd1_ref, jnp.concatenate(pair, 1))
        for w, spectrum in enumerate(forward(first, twist_ref, fwd2_ref)):
            out_ref[2 * p + w] = spectrum
        return carry

    lax.fori_loop(0, channels // 2, step, 0)


def conv_kernel(u_ref, h_ref, fwd1_ref, fwd2_ref, inv1_ref, inv2_ref, twist_ref, out_ref, rows, back):
    blocks, channels, local = u_ref.shape
    per = local // SIDE
    for i in range(blocks):
        for q in range(per):
            n = i * per + q
            rows[n * channels : (n + 1) * channels, :] = u_ref[i, :, q * SIDE : (q + 1) * SIDE].astype(f32)

    def step(p, carry):
        pair = jnp.concatenate([rows[pl.ds(2 * p + w, SIDE, stride=channels), :] for w in range(2)], 1).astype(bf16)
        first = mm(fwd1_ref[0], pair) + mm(fwd1_ref[1], pair)
        tc, ts = twist_ref[0], twist_ref[1]
        turned = []
        for w, s in enumerate(forward(first, twist_ref, fwd2_ref)):
            h = h_ref[2 * p + w]
            sr, si, hr, hi = s[:, :SIDE], s[:, SIDE:], h[:, :SIDE], h[:, SIDE:]
            product = jnp.concatenate([sr * hr - si * hi, sr * hi + si * hr], 1)
            b = right3(product, inv1_ref)
            br, bi = b[:, :SIDE], b[:, SIDE:]
            turned.append(jnp.concatenate([br * tc + bi * ts, bi * tc - br * ts], 0))
        y = left3(inv2_ref, jnp.concatenate(turned, 1))
        for w in range(2):
            back[pl.ds(2 * p + w, SIDE, stride=channels), :] = y[:, w * SIDE : (w + 1) * SIDE]
        return carry

    lax.fori_loop(0, channels // 2, step, 0)
    for i in range(blocks):
        for q in range(per):
            n = i * per + q
            out_ref[i, :, q * SIDE : (q + 1) * SIDE] = back[n * channels : (n + 1) * channels, :].astype(bf16)


def featured(x_ref, edge_ref, taps_ref, ext, s):
    tokens = x_ref.shape[1]
    count = taps_ref.shape[1]
    ext[8 : 8 + tokens, :] = x_ref[s].astype(f32)
    ext[8 - (count - 1) : 8, :] = edge_ref[s].astype(f32)
    total = taps_ref[s, 0:1, :] * ext[8 : 8 + tokens, :]
    for j in range(1, count):
        total = total + taps_ref[s, j : j + 1, :] * ext[8 - j : 8 - j + tokens, :]
    return total


def gate_in_kernel(x_ref, edge_ref, taps_ref, out_ref, ext):
    product = featured(x_ref, edge_ref, taps_ref, ext, 1) * featured(x_ref, edge_ref, taps_ref, ext, 2)
    out_ref[...] = product.T.astype(bf16)


def gate_out_kernel(x_ref, edge_ref, taps_ref, conv_ref, out_ref, ext):
    conv = conv_ref[...].astype(f32).T
    out_ref[...] = (featured(x_ref, edge_ref, taps_ref, ext, 0) * conv).astype(bf16)


def ring(axis, shift):
    size = lax.axis_size(axis)
    return [(i, (i + shift) % size) for i in range(size)]


def call(kernel, shape, dtype, scratch, flops, *args):
    moved = sum(a.size * a.dtype.itemsize for a in args)
    return pl.pallas_call(
        kernel,
        out_shape=jax.ShapeDtypeStruct(shape, dtype),
        scratch_shapes=scratch,
        cost_estimate=pl.CostEstimate(flops=flops, bytes_accessed=moved, transcendentals=0),
    )(*args)


def body(proj, short_filter, long_filter, out_weight):
    tokens, streams, width = proj.shape
    count = short_filter.shape[1]
    ctx = lax.axis_size(CTX)
    mine = width // ctx
    fwd1, fwd2, inv1, inv2, twist = [jnp.asarray(t) for t in tables()]

    streams_first = jnp.transpose(proj, (1, 0, 2))
    edge = lax.ppermute(
        streams_first[:, tokens - (count - 1) :, :], CTX, [(i, i + 1) for i in range(ctx - 1)]
    )

    nx, ny = lax.axis_size("x"), lax.axis_size("yh")
    x, yh = lax.axis_index("x"), lax.axis_index("yh")
    cols = out_weight.shape[1] // (nx * ny)

    def columns(shift, other):
        to = (x + shift) % nx
        row = (yh + other) % ny
        return lax.dynamic_slice_in_dim(out_weight, (row * nx + to) * cols, cols, 1)

    shifts = (2, 1, 3)
    weight_own, weight_other = {0: columns(0, 0)}, {0: columns(0, 1)}
    for s in shifts:
        both = jnp.concatenate([columns(s, 0), columns(s, 1)], 0)
        got = lax.ppermute(both, "x", ring("x", s))
        weight_own[s], weight_other[s] = got[:width], got[width:]

    ext = [pltpu.VMEM((tokens + 8, width), f32)]
    gated_in = call(gate_in_kernel, (width, tokens), bf16, ext, 0, streams_first, edge, short_filter)
    signal = lax.all_to_all(gated_in.reshape(ctx, mine, tokens), CTX, 0, 0)
    rows = [pltpu.VMEM((SIDE * mine, SIDE), f32)]
    spectrum = call(
        filter_kernel, (mine, SIDE, 2 * SIDE), f32, rows, 10**9, long_filter.T, fwd1, fwd2, twist
    )
    convolved = call(
        conv_kernel, (ctx, mine, tokens), bf16, rows * 2, 3 * 10**9,
        signal, spectrum, fwd1, fwd2, inv1, inv2, twist,
    )
    returned = lax.all_to_all(convolved, CTX, 0, 0).reshape(width, tokens)
    gated_out = call(
        gate_out_kernel, (tokens, width), bf16, ext, 0, streams_first, edge, short_filter, returned
    )
    pieces = {0: gated_out}
    for s in shifts:
        pieces[s] = lax.ppermute(gated_out, "x", ring("x", s))

    def project(weights):
        total = mm(pieces[0], weights[0])
        for s in (1, 3, 2):
            total = total + mm(pieces[s], weights[s])
        return total

    theirs = lax.ppermute(project(weight_other).astype(bf16), "yh", ring("yh", 1))
    return (project(weight_own) + theirs.astype(f32)).astype(bf16)


def solution(mesh):
    axes = Mesh(mesh.devices.reshape(8, 2, 2, 2, 4), ("z", "yl", "core", "yh", "x"))
    tp = ("yh", "x")
    placed = (P(CTX, None, tp), P(None, None, tp), P(None, tp + CTX), P(tp, None))
    return jax.shard_map(body, mesh=axes, in_specs=placed, out_specs=P(CTX, tp), check_vma=False)
```

time: 276 us -> 153 us (0.55)
  waiting for transfers between devices: 122 us -> 75.5 us
  matrix products: 55 us -> 12.7 us
  local copies, waits for them, and re-layouts: 34 us -> 4.99 us
  Pallas kernels: 0 us -> 25.2 us
  blocking collectives: 21 us -> 0 us
  starting transfers between devices: 14.2 us -> 31.6 us
  between operations: 14 us -> 0.18 us
  other arithmetic: 12.8 us -> 2.16 us
    reduce_scatter x1 -> x0, waiting for transfers between devices: 117 us -> none  [body(): lax.psum_scatter(lax.dot_general(out_weight, gated_out, (((0,), (1,)), ((...]
    ppermute x1 -> x8, waiting for transfers between devices: 0.01 us -> 56.2 us  [the longest x3 24.6 us: body(): pieces[s] = lax.ppermute(gated_out, 'x', ring('x', s))]
    dot_general x19 -> x8, matrix products: 55 us -> 12.7 us  [mm(): return jnp.dot(a, b, preferred_element_type=f32)]
    pallas_call x0 -> x4, Pallas kernels: none -> 25.2 us  [call(): pl.pallas_call(kernel, out_shape=jax.ShapeDtypeStruct(shape, dtype), scra...]
    all_to_all x1 -> x0, blocking collectives: 21 us -> none  [body(): lax.all_to_all(convolved, 'ctx', split_axis=1, concat_axis=0, tiled=True)]
    reshape x2 -> x0, local copies, waits for them, and re-layouts: 16.2 us -> none  [spectrum(): flattened = signal.reshape(half_rows, inner_block * channel_count)]
    all_to_all x1 -> x2, waiting for transfers between devices: 4.85 us -> 19.2 us  [the longest x1 10.7 us: body(): returned = lax.all_to_all(convolved, CTX, 0, 0).reshape(width, tokens)]
    ppermute x1 -> x8, starting transfers between devices: 4.57 us -> 14.9 us  [the longest x1 4.58 us: body(): lax.ppermute(streams_first[:, tokens - (count - 1):, :], CTX, [(i, i + 1)...]
  transfers between devices with their start and end apart: 3 -> 10, of which waited for: 2 -> 8; matrix products, arithmetic and copies ran while one was open for 15% -> 8% of each run, Pallas kernels for 0% -> 7%
where the time goes in v1:
time: 153 us; the launch traced here: 152 us
  waiting for transfers between devices  75.5 us (49%)
  starting transfers between devices  31.6 us (21%)
  Pallas kernels  25.2 us (16%)
  matrix products  12.7 us (8%)
  local copies, waits for them, and re-layouts  4.99 us (3%)
  other arithmetic  2.16 us (1%)
    pallas_call x4, Pallas kernels, call(): pl.pallas_call(kernel, out_shape=jax.ShapeDtypeStruct(shape, dtype), scra...  25.2 us
    ppermute x3, waiting for transfers between devices, body(): pieces[s] = lax.ppermute(gated_out, 'x', ring('x', s))  24.6 us
    ppermute x3, waiting for transfers between devices, body(): got = lax.ppermute(both, 'x', ring('x', s))  23.8 us
    dot_general x8, matrix products, mm(): return jnp.dot(a, b, preferred_element_type=f32)  12.7 us
    all_to_all x1, starting transfers between devices, body(): signal = lax.all_to_all(gated_in.reshape(ctx, mine, tokens), CTX, 0, 0)  11.8 us
    all_to_all x1, waiting for transfers between devices, body(): returned = lax.all_to_all(convolved, CTX, 0, 0).reshape(width, tokens)  10.7 us
    all_to_all x1, waiting for transfers between devices, body(): signal = lax.all_to_all(gated_in.reshape(ctx, mine, tokens), CTX, 0, 0)  8.57 us
    ppermute x1, waiting for transfers between devices, body(): lax.ppermute(project(weight_other).astype(bf16), 'yh', ring('yh', 1))  7.1 us
  transfers between devices with their start and end apart: 10, of which 8 were waited for; matrix products, arithmetic and copies ran while one was open for 8% of the time, Pallas kernels for 7%

profile of v1, /device:TPU:1, one launch (start us, length us, event | category | flops | bytes accessed | tf_op | source)
XLA Modules:
  0.0 152.2 jit_solution(16788381448777367562)
XLA Ops:
  0.0 0.7 slice.28
  0.8 4.6 %collective-permute-start = (bf16[3,2,512]{2,1,0:T(2,128)(2,1)S(1)}, bf16[3,2,512]{2,1,0:T(2,128)(2,1)S(1)}, u32[]{:S(2)}, u32[]{:S(2)}) collective-permute-start(bf16[3,2,512]{2,1,0:T(2,128)(2,1)S(1)} %slice.28), channel_id=1, source_target_pairs={{0,8},{8,16},{16,24},{24,32},{32,40},{40,48},{48,56},{56,64},{64,7... | collective-permute-start | bytes 18440 | tf_op jit(solution)/shard_map/ppermute | solution.py:157
  5.3 0.8 collective-permute-done.edge_ref
  6.1 0.0 copy-start.3
  6.1 0.6 copy-done.3
  6.7 3.2 %shard_map.91 = bf16[512,512]{1,0:T(8,128)(2,1)} custom-call(bf16[3,512,512]{2,1,0:T(8,128)(2,1)} %bitcast.13, bf16[3,2,512]{2,1,0:T(2,128)(2,1)} %copy-done.3, f32[3,3,512]{2,1,0:T(4,128)} %taps_ref.3), custom_call_target="tpu_custom_call" | custom-call | bytes 1597440 | tf_op jit(solution)/shard_map/pallas_call | solution.py:141
  9.9 11.8 %all-to-all-start = ((bf16[32,16,512]{2,1,0:T(8,128)(2,1)}), bf16[32,16,512]{2,1,0:T(8,128)(2,1)S(1)}, u32[]{:S(2)}, u32[]{:S(2)}) async-start(bf16[32,16,512]{2,1,0:T(8,128)(2,1)} %bitcast.15), calls=%async_computation | async-start | bytes 1048576 | tf_op jit(solution)/shard_map/all_to_all | solution.py:179
  21.7 8.0 %shard_map.92.h_ref = f32[16,128,256]{2,1,0:T(8,128)} custom-call(f32[16,16384]{1,0:T(8,128)} %bitcast.17, bf16[2,256,128]{2,1,0:T(8,128)(2,1)} %constant.85.clone.fwd1_ref, bf16[2,256,256]{2,1,0:T(8,128)(2,1)} %constant.86.clone.fwd2_ref, f32[2,128,128]{2,1,0:T(8,128)} %constant.89.clone.twist_ref), custom_call_target="tpu_custom_call" | custom-call | flops 1000000000 | bytes 1572864 | tf_op jit(solution)/shard_map/pallas_call | solution.py:141
  29.7 8.6 %all-to-all-done.u_ref = bf16[32,16,512]{2,1,0:T(8,128)(2,1)S(1)} async-done(((bf16[32,16,512]{2,1,0:T(8,128)(2,1)}), bf16[32,16,512]{2,1,0:T(8,128)(2,1)S(1)}, u32[]{:S(2)}, u32[]{:S(2)}) %all-to-all-start) | async-done | bytes 524320 | tf_op jit(solution)/shard_map/all_to_all | solution.py:179
  38.3 0.0 copy-start.2
  38.3 0.8 copy-done.2
  39.0 11.1 %shard_map.93 = bf16[32,16,512]{2,1,0:T(8,128)(2,1)} custom-call(bf16[32,16,512]{2,1,0:T(8,128)(2,1)} %copy-done.2, f32[16,128,256]{2,1,0:T(8,128)} %shard_map.92.h_ref, bf16[2,256,128]{2,1,0:T(8,128)(2,1)} %constant.85.clone.fwd1_ref, bf16[2,256,256]{2,1,0:T(8,128)(2,1)} %constant.86.clone.fwd2_ref, bf16[2,256,256]{2,1,0:T(8,128)(2,1)} %constant.87.clone.inv1_ref, ...), custom_call_target="tpu_custom_call" | custom-call | flops 3000000000 | bytes 3538944 | tf_op jit(solution)/shard_map/pallas_call | solution.py:141
  50.1 4.9 %all-to-all-start.1 = ((bf16[32,16,512]{2,1,0:T(8,128)(2,1)}), bf16[32,16,512]{2,1,0:T(8,128)(2,1)S(1)}, u32[]{:S(2)}, u32[]{:S(2)}) async-start(bf16[32,16,512]{2,1,0:T(8,128)(2,1)} %shard_map.93), calls=%async_computation.1 | async-start | bytes 1048576 | tf_op jit(solution)/shard_map/all_to_all | solution.py:188
  55.1 2.1 %constant_dynamic-slice_fusion.5 = (bf16[512,512]{1,0:T(8,128)(2,1)S(1)}, bf16[512,512]{1,0:T(8,128)(2,1)S(1)}, bf16[512,512]{1,0:T(8,128)(2,1)S(1)}, bf16[512,5...) fusion(bf16[512,4096]{1,0:T(8,128)(2,1)} %param.12, s32[]{:T(128)S(6)} %select_n.75, ...), kind=kLoop, calls=%fused_computation.32 | loop fusion | bytes 6291480 | tf_op jit(solution)/shard_map/dynamic_slice | solution.py:168
  57.2 1.0 pad_maximum_fusion.1
  58.2 2.5 %collective-permute-start.4 = (bf16[1024,512]{1,0:T(8,128)(2,1)}, bf16[1024,512]{1,0:T(8,128)(2,1)}, u32[]{:S(2)}, u32[]{:S(2)}) collective-permute-start(bf16[1024,512]{1,0:T(8,128)(2,1)} %pad_maximum_fusion.1), channel_id=1, source_target_pairs={{0,3},{1,0},{2,1},{3,2},{4,7},{5,4},{6,5},{7,6},{8,11},{9,8},{10,9... | collective-permute-start | bytes 3145736 | tf_op jit(solution)/shard_map/ppermute | solution.py:174
  60.7 0.1 pad_maximum_fusion.2
  60.8 0.6 collective-permute-start.6
  61.4 10.7 %all-to-all-done.1 = bf16[32,16,512]{2,1,0:T(8,128)(2,1)S(1)} async-done(((bf16[32,16,512]{2,1,0:T(8,128)(2,1)}), bf16[32,16,512]{2,1,0:T(8,128)(2,1)S(1)}, u32[]{:S(2)}, u32[]{:S(2)}) %all-to-all-start.1) | async-done | bytes 524320 | tf_op jit(solution)/shard_map/all_to_all | solution.py:188
  72.0 0.0 copy-start.1
  72.0 0.8 copy-done.1
  72.8 2.9 %shard_map.94 = bf16[512,512]{1,0:T(8,128)(2,1)} custom-call(bf16[3,512,512]{2,1,0:T(8,128)(2,1)} %bitcast.14, bf16[3,2,512]{2,1,0:T(2,128)(2,1)} %copy-done.3, f32[3,3,512]{2,1,0:T(4,128)} %taps_ref.3, bf16[512,512]{1,0:T(8,128)(2,1)} %bitcast.16), custom_call_target="tpu_custom_call" | custom-call | bytes 2121728 | tf_op jit(solution)/shard_map/pallas_call | solution.py:141
  75.7 0.0 copy-start
  75.7 2.5 %collective-permute-start.3 = (bf16[512,512]{1,0:T(8,128)(2,1)}, bf16[512,512]{1,0:T(8,128)(2,1)S(1)}, u32[]{:S(2)}, u32[]{:S(2)}) collective-permute-start(bf16[512,512]{1,0:T(8,128)(2,1)} %shard_map.94), channel_id=1, source_target_pairs={{0,3},{1,0},{2,1},{3,2},{4,7},{5,4},{6,5},{7,6},{8,11},{9,8},{10,9... | collective-permute-start | bytes 1572872 | tf_op jit(solution)/shard_map/ppermute | solution.py:194
  78.2 1.1 pad_maximum_fusion
  79.3 0.0 collective-permute-start.2
  79.3 0.0 copy-done
  79.3 1.7 %collective-permute-start.5 = (bf16[512,512]{1,0:T(8,128)(2,1)S(1)}, bf16[512,512]{1,0:T(8,128)(2,1)S(1)}, u32[]{:S(2)}, u32[]{:S(2)}) collective-permute-start(bf16[512,512]{1,0:T(8,128)(2,1)S(1)} %copy-done), channel_id=1, source_target_pairs={{0,2},{1,3},{2,0},{3,1},{4,6},{5,7},{6,4},{7,5},{8,10},{9,11},{10,... | collective-permute-start | bytes 1572872 | tf_op jit(solution)/shard_map/ppermute | solution.py:194
  81.0 23.8 %collective-permute-done.4 = bf16[1024,512]{1,0:T(8,128)(2,1)} collective-permute-done((bf16[1024,512]{1,0:T(8,128)(2,1)}, bf16[1024,512]{1,0:T(8,128)(2,1)}, u32[]{:S(2)}, u32[]{:S(2)}) %collective-permute-start.4) | collective-permute-done | bytes 1048608 | tf_op jit(solution)/shard_map/ppermute | solution.py:174
  104.8 0.0 collective-permute-start.1
  104.8 12.8 %collective-permute-done.3 = bf16[512,512]{1,0:T(8,128)(2,1)S(1)} collective-permute-done((bf16[512,512]{1,0:T(8,128)(2,1)}, bf16[512,512]{1,0:T(8,128)(2,1)S(1)}, u32[]{:S(2)}, u32[]{:S(2)}) %collective-permute-start.3) | collective-permute-done | bytes 524320 | tf_op jit(solution)/shard_map/ppermute | solution.py:194
  117.6 1.5 fusion.9
  119.0 0.0 collective-permute-done.6
  119.0 1.2 collective-permute-done.5
  120.2 1.5 fusion.7
  121.7 0.0 collective-permute-done.2
  121.7 10.6 %collective-permute-done.1 = bf16[512,512]{1,0:T(8,128)(2,1)S(1)} collective-permute-done((bf16[512,512]{1,0:T(8,128)(2,1)S(1)}, bf16[512,512]{1,0:T(8,128)(2,1)S(1)}, u32[]{:S(2)}, u32[]{:S(2)}) %collective-permute-start.1) | collective-permute-done | bytes 524320 | tf_op jit(solution)/shard_map/ppermute | solution.py:194
  132.3 1.5 fusion.11
  133.8 1.5 fusion.6
  135.3 3.0 %collective-permute-start.7 = (bf16[512,512]{1,0:T(8,128)(2,1)S(1)}, bf16[512,512]{1,0:T(8,128)(2,1)S(1)}, u32[]{:S(2)}, u32[]{:S(2)}) collective-permute-start(bf16[512,512]{1,0:T(8,128)(2,1)S(1)} %fusion.6), channel_id=1, source_target_pairs={{0,4},{4,0},{1,5},{5,1},{2,6},{6,2},{3,7},{7,3},{8,12},{12,8},{9,1... | collective-permute-start | bytes 1572872 | tf_op jit(solution)/shard_map/ppermute | solution.py:202
  138.3 1.5 fusion.15
  139.8 1.5 fusion.13
  141.3 1.5 fusion.17
  142.8 7.1 %collective-permute-done.7 = bf16[512,512]{1,0:T(8,128)(2,1)S(1)} collective-permute-done((bf16[512,512]{1,0:T(8,128)(2,1)S(1)}, bf16[512,512]{1,0:T(8,128)(2,1)S(1)}, u32[]{:S(2)}, u32[]{:S(2)}) %collective-permute-start.7) | collective-permute-done | bytes 524320 | tf_op jit(solution)/shard_map/ppermute | solution.py:202
  149.9 2.4 %fusion.5 = bf16[512,512]{1,0:T(8,128)(2,1)} fusion(f32[512,512]{1,0:T(8,128)S(1)} %fusion.13, f32[512,512]{1,0:T(8,128)S(1)} %fusion.15, f32[512,512]{1,0:T(8,128)S(1)} %fusion.17, bf16[512,512]{1,0:T(8,128)(2,1)S(1)} %copy-done, bf16[512,512]{1,0:T(8,128)(2,1)S(1)} %collective-permute-done.7, bf16[512,4096]{1,0:T(8,128)(2,1)} %param.12, s32[]{:T(128)S(6)} %select_n.73), kind=kOutput, calls=%fused_computation.7 | convolution fusion | flops 270008320 | bytes 5242884 | tf_op jit(solution)/shard_map/dot_general | solution.py:43
Async XLA Ops:
  0.8 5.3 %collective-permute-start = (bf16[3,2,512]{2,1,0:T(2,128)(2,1)S(1)}, bf16[3,2,512]{2,1,0:T(2,128)(2,1)S(1)}, u32[]{:S(2)}, u32[]{:S(2)}) collective-permute-start(bf16[3,2,512]{2,1,0:T(2,128)(2,1)S(1)} %slice.28), channel_id=1, source_target_pairs={{0,8},{8,16},{16,24},{24,32},{32,40},{40,48},{48,56},{56,64},{64,7... | collective-permute-start | bytes 18440 | tf_op jit(solution)/shard_map/ppermute | solution.py:157
  6.1 0.6 copy-start.3
  9.9 28.4 %all-to-all-start = ((bf16[32,16,512]{2,1,0:T(8,128)(2,1)}), bf16[32,16,512]{2,1,0:T(8,128)(2,1)S(1)}, u32[]{:S(2)}, u32[]{:S(2)}) async-start(bf16[32,16,512]{2,1,0:T(8,128)(2,1)} %bitcast.15), calls=%async_computation | async-start | bytes 1048576 | tf_op jit(solution)/shard_map/all_to_all | solution.py:179
  38.3 0.8 copy-start.2
  50.1 21.9 %all-to-all-start.1 = ((bf16[32,16,512]{2,1,0:T(8,128)(2,1)}), bf16[32,16,512]{2,1,0:T(8,128)(2,1)S(1)}, u32[]{:S(2)}, u32[]{:S(2)}) async-start(bf16[32,16,512]{2,1,0:T(8,128)(2,1)} %shard_map.93), calls=%async_computation.1 | async-start | bytes 1048576 | tf_op jit(solution)/shard_map/all_to_all | solution.py:188
  58.2 46.6 %collective-permute-start.4 = (bf16[1024,512]{1,0:T(8,128)(2,1)}, bf16[1024,512]{1,0:T(8,128)(2,1)}, u32[]{:S(2)}, u32[]{:S(2)}) collective-permute-start(bf16[1024,512]{1,0:T(8,128)(2,1)} %pad_maximum_fusion.1), channel_id=1, source_target_pairs={{0,3},{1,0},{2,1},{3,2},{4,7},{5,4},{6,5},{7,6},{8,11},{9,8},{10,9... | collective-permute-start | bytes 3145736 | tf_op jit(solution)/shard_map/ppermute | solution.py:174
  60.8 58.3 %collective-permute-start.6 = (bf16[1024,512]{1,0:T(8,128)(2,1)S(1)}, bf16[1024,512]{1,0:T(8,128)(2,1)}, u32[]{:S(2)}, u32[]{:S(2)}) collective-permute-start(bf16[1024,512]{1,0:T(8,128)(2,1)S(1)} %pad_maximum_fusion.2), channel_id=1, source_target_pairs={{0,2},{1,3},{2,0},{3,1},{4,6},{5,7},{6,4},{7,5},{8,10},{9,11},{10,... | collective-permute-start | bytes 3145736 | tf_op jit(solution)/shard_map/ppermute | solution.py:174
  72.0 0.8 copy-start.1
  75.7 3.5 %copy-start = (bf16[512,512]{1,0:T(8,128)(2,1)S(1)}, bf16[512,512]{1,0:T(8,128)(2,1)}, u32[]{:S(2)}) copy-start(bf16[512,512]{1,0:T(8,128)(2,1)} %shard_map.94) | copy-start | bytes 1572868
  75.7 41.8 %collective-permute-start.3 = (bf16[512,512]{1,0:T(8,128)(2,1)}, bf16[512,512]{1,0:T(8,128)(2,1)S(1)}, u32[]{:S(2)}, u32[]{:S(2)}) collective-permute-start(bf16[512,512]{1,0:T(8,128)(2,1)} %shard_map.94), channel_id=1, source_target_pairs={{0,3},{1,0},{2,1},{3,2},{4,7},{5,4},{6,5},{7,6},{8,11},{9,8},{10,9... | collective-permute-start | bytes 1572872 | tf_op jit(solution)/shard_map/ppermute | solution.py:194
  79.3 42.5 %collective-permute-start.2 = (bf16[1024,512]{1,0:T(8,128)(2,1)}, bf16[1024,512]{1,0:T(8,128)(2,1)}, u32[]{:S(2)}, u32[]{:S(2)}) collective-permute-start(bf16[1024,512]{1,0:T(8,128)(2,1)} %pad_maximum_fusion), channel_id=1, source_target_pairs={{0,1},{1,2},{2,3},{3,0},{4,5},{5,6},{6,7},{7,4},{8,9},{9,10},{10,1... | collective-permute-start | bytes 3145736 | tf_op jit(solution)/shard_map/ppermute | solution.py:174
  79.3 41.0 %collective-permute-start.5 = (bf16[512,512]{1,0:T(8,128)(2,1)S(1)}, bf16[512,512]{1,0:T(8,128)(2,1)S(1)}, u32[]{:S(2)}, u32[]{:S(2)}) collective-permute-start(bf16[512,512]{1,0:T(8,128)(2,1)S(1)} %copy-done), channel_id=1, source_target_pairs={{0,2},{1,3},{2,0},{3,1},{4,6},{5,7},{6,4},{7,5},{8,10},{9,11},{10,... | collective-permute-start | bytes 1572872 | tf_op jit(solution)/shard_map/ppermute | solution.py:194
  104.8 27.6 %collective-permute-start.1 = (bf16[512,512]{1,0:T(8,128)(2,1)S(1)}, bf16[512,512]{1,0:T(8,128)(2,1)S(1)}, u32[]{:S(2)}, u32[]{:S(2)}) collective-permute-start(bf16[512,512]{1,0:T(8,128)(2,1)S(1)} %copy-done), channel_id=1, source_target_pairs={{0,1},{1,2},{2,3},{3,0},{4,5},{5,6},{6,7},{7,4},{8,9},{9,10},{10,1... | collective-permute-start | bytes 1572872 | tf_op jit(solution)/shard_map/ppermute | solution.py:194
  135.3 14.5 %collective-permute-start.7 = (bf16[512,512]{1,0:T(8,128)(2,1)S(1)}, bf16[512,512]{1,0:T(8,128)(2,1)S(1)}, u32[]{:S(2)}, u32[]{:S(2)}) collective-permute-start(bf16[512,512]{1,0:T(8,128)(2,1)S(1)} %fusion.6), channel_id=1, source_target_pairs={{0,4},{4,0},{1,5},{5,1},{2,6},{6,2},{3,7},{7,3},{8,12},{12,8},{9,1... | collective-permute-start | bytes 1572872 | tf_op jit(solution)/shard_map/ppermute | solution.py:202

commit v2 on v1

v2 whole, which is shorter than its diff:
```python
import jax
import jax.numpy as jnp
import numpy as np
from jax import lax
from jax.experimental import pallas as pl
from jax.experimental.pallas import tpu as pltpu
from jax.sharding import Mesh, PartitionSpec as P


CTX = ("z", "yl", "core")
SIDE = 128
LENGTH = SIDE * SIDE
WIDE = 4
EDGE = 8
LIMIT = 16 * 2**20
FULL = 60 * 1024 * 2**10
f32, bf16 = jnp.float32, jnp.bfloat16


def halves(table):
    high = table.astype(bf16)
    low = (table - high.astype(np.float64)).astype(bf16)
    return np.stack([high, low])


def tables():
    i = np.arange(SIDE)
    first = 2 * np.pi * np.outer(i + 0.25, i) / SIDE
    turn = 2 * np.pi * np.outer(i + 0.25, i) / LENGTH
    second = 2 * np.pi * np.outer(i, i) / SIDE
    c1, s1, c2, s2 = np.cos(first), np.sin(first), np.cos(second), np.sin(second)
    fwd1 = np.concatenate([c1, s1], 0)
    fwd2 = np.block([[c2, s2], [-s2, c2]])
    inv1 = np.block([[c2, -s2], [s2, c2]])
    inv2 = np.concatenate([c1.T, s1.T], 1) / LENGTH
    twist = np.stack([np.cos(turn), np.sin(turn)]).astype(np.float32)
    return halves(fwd1), halves(fwd2), halves(inv1), halves(inv2), twist


def split(x):
    high = x.astype(bf16)
    return high, (x - high.astype(f32)).astype(bf16)


def mm(a, b):
    return jnp.dot(a, b, preferred_element_type=f32)


def left3(tab, x):
    high, low = split(x)
    return mm(tab[0], high) + (mm(tab[1], high) + mm(tab[0], low))


def right3(x, tab):
    high, low = split(x)
    return mm(high, tab[0]) + (mm(low, tab[0]) + mm(high, tab[1]))


def stacked(first, twist):
    tc, ts = twist[0], twist[1]
    turned = []
    for w in range(first.shape[1] // SIDE):
        re, im = first[:SIDE, w * SIDE : (w + 1) * SIDE], first[SIDE:, w * SIDE : (w + 1) * SIDE]
        turned.append(jnp.concatenate([re * tc - im * ts, re * ts + im * tc], 1))
    return jnp.concatenate(turned, 0)


def filter_kernel(h_ref, fwd1_ref, fwd2_ref, twist_ref, out_ref, rows):
    channels = h_ref.shape[0]
    for n in range(SIDE):
        rows[n * channels : (n + 1) * channels, :] = h_ref[:, n * SIDE : (n + 1) * SIDE]

    def step(p, carry):
        group = [rows[pl.ds(WIDE * p + w, SIDE, stride=channels), :] for w in range(WIDE)]
        first = left3(fwd1_ref, jnp.concatenate(group, 1))
        spectra = right3(stacked(first, twist_ref), fwd2_ref)
        for w in range(WIDE):
            out_ref[WIDE * p + w] = spectra[w * SIDE : (w + 1) * SIDE]
        return carry

    lax.fori_loop(0, channels // WIDE, step, 0)


def fetch(sources, targets, sem):
    copies = [pltpu.make_async_copy(a, b, sem.at[i]) for i, (a, b) in enumerate(zip(sources, targets))]
    for c in copies:
        c.start()
    return copies


def conv_kernel(u_ref, *refs):
    sources, out_ref, rows, back, held, sem = refs[:6], refs[6], refs[7], refs[8], refs[9:15], refs[15]
    h_ref, fwd1_ref, fwd2_ref, inv1_ref, inv2_ref, twist_ref = held
    copies = fetch(sources, held, sem)
    blocks, channels, local = u_ref.shape
    per = local // SIDE
    for i in range(blocks):
        for q in range(per):
            n = i * per + q
            rows[n * channels : (n + 1) * channels, :] = u_ref[i, :, q * SIDE : (q + 1) * SIDE].astype(f32)
    for c in copies:
        c.wait()

    def step(p, carry):
        group = [rows[pl.ds(WIDE * p + w, SIDE, stride=channels), :] for w in range(WIDE)]
        group = jnp.concatenate(group, 1).astype(bf16)
        first = mm(fwd1_ref[0], group) + mm(fwd1_ref[1], group)
        spectra = right3(stacked(first, twist_ref), fwd2_ref)
        products = []
        for w in range(WIDE):
            s, h = spectra[w * SIDE : (w + 1) * SIDE], h_ref[WIDE * p + w]
            sr, si, hr, hi = s[:, :SIDE], s[:, SIDE:], h[:, :SIDE], h[:, SIDE:]
            products.append(jnp.concatenate([sr * hr - si * hi, sr * hi + si * hr], 1))
        b = right3(jnp.concatenate(products, 0), inv1_ref)
        tc, ts = twist_ref[0], twist_ref[1]
        turned = []
        for w in range(WIDE):
            br, bi = b[w * SIDE : (w + 1) * SIDE, :SIDE], b[w * SIDE : (w + 1) * SIDE, SIDE:]
            turned.append(jnp.concatenate([br * tc + bi * ts, bi * tc - br * ts], 0))
        y = left3(inv2_ref, jnp.concatenate(turned, 1))
        for w in range(WIDE):
            back[pl.ds(WIDE * p + w, SIDE, stride=channels), :] = y[:, w * SIDE : (w + 1) * SIDE]
        return carry

    lax.fori_loop(0, channels // WIDE, step, 0)
    for i in range(blocks):
        for q in range(per):
            n = i * per + q
            out_ref[i, :, q * SIDE : (q + 1) * SIDE] = back[n * channels : (n + 1) * channels, :].astype(bf16)


def featured(x, edge_ref, taps_ref, ext, s):
    tokens = x.shape[0]
    ext[EDGE : EDGE + tokens, :] = x.astype(f32)
    ext[:EDGE, :] = edge_ref[s].astype(f32)
    total = taps_ref[s, 0:1, :] * ext[EDGE : EDGE + tokens, :]
    for j in range(1, taps_ref.shape[1]):
        total = total + taps_ref[s, j : j + 1, :] * ext[EDGE - j : EDGE - j + tokens, :]
    return total


def gate_in_kernel(edge_ref, x_hbm, taps_hbm, out_ref, ext, keys, values, taps, sem):
    copies = fetch((taps_hbm, x_hbm.at[1], x_hbm.at[2]), (taps, keys, values), sem)
    copies[0].wait()
    copies[1].wait()
    key = featured(keys[...], edge_ref, taps, ext, 1)
    copies[2].wait()
    out_ref[...] = (key * featured(values[...], edge_ref, taps, ext, 2)).T.astype(bf16)


def query_kernel(x_ref, edge_ref, taps_ref, out_ref, ext):
    out_ref[...] = featured(x_ref[0], edge_ref, taps_ref, ext, 0)


def gate_out_kernel(query_ref, conv_ref, upper_ref, lower_ref):
    gated = (query_ref[...] * conv_ref[...].astype(f32).T).astype(bf16)
    half = upper_ref.shape[0]
    upper_ref[...] = gated[:half]
    lower_ref[...] = gated[half:]


def block_columns(nx, ny, shift, other, cols):
    x, yh = lax.axis_index("x"), lax.axis_index("yh")
    block = ((yh + other) % ny) * nx + (x + shift) % nx
    return pl.ds(pl.multiple_of(block * cols, cols), cols)


def columns_kernel(nx, ny, weight_ref, *rest):
    outs, sem = rest[:nx], rest[nx]
    cols = outs[0].shape[2]
    half = weight_ref.shape[0] // 2
    first = pl.multiple_of(lax.axis_index("core") * half, half)
    sources = []
    for s in range(nx):
        for o in range(ny):
            at = block_columns(nx, ny, s, o, cols)
            sources.append(weight_ref.at[pl.ds(first, half), at] if s else weight_ref.at[:, at])
    for c in fetch(sources, [out.at[o] for out in outs for o in range(ny)], sem):
        c.wait()


def stage_kernel(*refs):
    count = len(refs) // 2
    for c in fetch(refs[:count], refs[count : 2 * count], refs[2 * count]):
        c.wait()


def project_rows(other, at, pieces, weights):
    width = pieces[0].shape[1]
    half = width // 2
    core = lax.axis_index("core")
    mine = pl.ds(pl.multiple_of(core * half, half), half)
    rest = pl.ds(pl.multiple_of((1 - core) * half, half), half)
    total = mm(pieces[0][at, :], weights[0][other])
    for s, piece in enumerate(pieces[1:]):
        total = total + mm(piece[at, mine], weights[1 + 2 * s][other])
        total = total + mm(piece[at, rest], weights[2 + 2 * s][other])
    return total


def project_other_kernel(*refs):
    pieces, weights, out_ref = refs[:4], refs[4:11], refs[11]
    step = 128

    def rows(r, carry):
        at = pl.ds(pl.multiple_of(r * step, step), step)
        out_ref[at, :] = project_rows(1, at, pieces, weights).astype(out_ref.dtype)
        return carry

    lax.fori_loop(0, out_ref.shape[0] // step, rows, 0)


def project_own_kernel(*refs):
    pieces, weights, out_ref = refs[:8], refs[8:15], refs[15]
    step = 128
    tokens = pieces[0].shape[0]
    for part in range(2):

        def rows(r, carry):
            start = pl.multiple_of(r * step, step)
            sums = project_rows(0, pl.ds(start, step), pieces[4 * part : 4 * part + 4], weights)
            out_ref[pl.ds(part * tokens + start, step), :] = sums
            return carry

        lax.fori_loop(0, tokens // step, rows, 0)


def finish_kernel(own_ref, first_ref, second_ref, out_ref):
    tokens = first_ref.shape[0]
    for part, came in enumerate((first_ref, second_ref)):
        at = slice(part * tokens, (part + 1) * tokens)
        out_ref[at, :] = (own_ref[at, :] + came[...].astype(f32)).astype(out_ref.dtype)


def ring(axis, shift):
    size = lax.axis_size(axis)
    return [(i, (i + shift) % size) for i in range(size)]


VM = pl.BlockSpec(memory_space=pltpu.VMEM)
HBM = pl.BlockSpec(memory_space=pltpu.HBM)


def held(*arrays):
    return [pltpu.VMEM(a.shape, a.dtype) for a in arrays] + [pltpu.SemaphoreType.DMA((len(arrays),))]


def call(kernel, outs, scratch, flops, *args, specs=None, limit=LIMIT):
    moved = sum(a.size * a.dtype.itemsize for a in args)
    shapes = [jax.ShapeDtypeStruct(*o) for o in outs]
    result = pl.pallas_call(
        kernel,
        out_shape=shapes,
        in_specs=specs or [VM] * len(args),
        out_specs=[VM] * len(shapes),
        scratch_shapes=scratch,
        compiler_params=pltpu.CompilerParams(vmem_limit_bytes=limit),
        cost_estimate=pl.CostEstimate(flops=flops, bytes_accessed=moved, transcendentals=0),
    )(*args)
    return result if len(shapes) > 1 else result[0]


def body(proj, short_filter, long_filter, out_weight):
    tokens, _, width = proj.shape
    ctx = lax.axis_size(CTX)
    mine = width // ctx
    nx, ny = lax.axis_size("x"), lax.axis_size("yh")
    cols = out_weight.shape[1] // (nx * ny)
    fwd1, fwd2, inv1, inv2, twist = [jnp.asarray(t) for t in tables()]

    streams_first = jnp.transpose(proj, (1, 0, 2))
    edge = lax.ppermute(streams_first[:, tokens - EDGE :, :], CTX, [(i, i + 1) for i in range(ctx - 1)])
    ext = [pltpu.VMEM((tokens + EDGE, width), f32)]
    gated_in = call(
        gate_in_kernel, [((width, tokens), bf16)],
        ext + held(streams_first[1], streams_first[2], short_filter), 0,
        edge, streams_first, short_filter, specs=[VM, HBM, HBM], limit=FULL,
    )
    gated_in, out_weight = lax.optimization_barrier((gated_in, out_weight))
    signal = lax.all_to_all(gated_in.reshape(ctx, mine, tokens), CTX, 0, 0)

    def columns(*refs):
        columns_kernel(nx, ny, *refs)

    blocks = call(
        columns, [((ny, width if s == 0 else width // 2, cols), bf16) for s in range(nx)],
        [pltpu.SemaphoreType.DMA((ny * nx,))], 0, out_weight, specs=[HBM], limit=FULL,
    )
    weights = [blocks[0]]
    for s in range(1, nx):
        came = lax.ppermute(blocks[s], "x", ring("x", s))
        weights += [came, lax.ppermute(came, "core", ring("core", 1))]

    rows = [pltpu.VMEM((SIDE * mine, SIDE), f32)]
    spectrum = call(filter_kernel, [((mine, SIDE, 2 * SIDE), f32)], rows, 10**9, long_filter.T, fwd1, fwd2, twist)
    convolved = call(
        conv_kernel, [((ctx, mine, tokens), bf16)],
        rows * 2 + held(spectrum, fwd1, fwd2, inv1, inv2, twist), 3 * 10**9,
        signal, spectrum, fwd1, fwd2, inv1, inv2, twist, specs=[VM] + [HBM] * 6, limit=FULL,
    )
    returned = lax.all_to_all(convolved, CTX, 0, 0).reshape(width, tokens)
    query = call(query_kernel, [((tokens, width), f32)], ext, 0, streams_first, edge, short_filter)
    half = tokens // 2
    upper, lower = call(gate_out_kernel, [((half, width), bf16)] * 2, [], 0, query, returned)

    def send(block, shift):
        return lax.ppermute(block, "x", ring("x", shift))

    left_upper, right_lower = send(upper, 1), send(lower, -1)
    right_upper, left_lower = send(upper, -1), send(lower, 1)
    far_upper, far_lower = send(left_upper, 1), send(right_lower, -1)
    pieces = [(upper, left_upper, far_upper, right_upper), (lower, left_lower, far_lower, right_lower)]

    weights = call(
        stage_kernel, [(w.shape, bf16) for w in weights], [pltpu.SemaphoreType.DMA((len(weights),))], 0,
        *weights, specs=[HBM] * len(weights),
    )
    theirs = []
    for part in range(2):
        sums = call(project_other_kernel, [((half, cols), bf16)], [], 10**9, *pieces[part], *weights)
        theirs.append(lax.ppermute(sums, "yh", ring("yh", 1)))
    own = call(project_own_kernel, [((tokens, cols), f32)], [], 2 * 10**9, *pieces[0], *pieces[1], *weights)
    return call(finish_kernel, [((tokens, cols), bf16)], [], 0, own, *theirs)


def solution(mesh):
    axes = Mesh(mesh.devices.reshape(8, 2, 2, 2, 4), ("z", "yl", "core", "yh", "x"))
    tp = ("yh", "x")
    placed = (P(CTX, None, tp), P(None, None, tp), P(None, tp + CTX), P(tp, None))
    return jax.shard_map(body, mesh=axes, in_specs=placed, out_specs=P(CTX, tp), check_vma=False)
```

time: 153 us -> 122 us (0.80); the launches traced: 152 us -> 119 us
  waiting for transfers between devices: 75.5 us -> 44.9 us
  matrix products: 12.7 us -> 0 us
  starting transfers between devices: 31.6 us -> 42.5 us
  other arithmetic: 2.16 us -> 0 us
  Pallas kernels: 25.2 us -> 27 us
    ppermute x8 -> x15, waiting for transfers between devices: 56.2 us -> 33 us  [the longest x3 20.1 us: body(): came = lax.ppermute(blocks[s], 'x', ring('x', s))]
    dot_general x8 -> x0, matrix products: 12.7 us -> none  [mm(): return jnp.dot(a, b, preferred_element_type=f32)]
    ppermute x8 -> x15, starting transfers between devices: 14.9 us -> 25.7 us  [the longest x6 7.5 us: send(): return lax.ppermute(block, 'x', ring('x', shift))]
    all_to_all x1, waiting for transfers between devices: 10.7 us -> 0.01 us  [body(): returned = lax.all_to_all(convolved, CTX, 0, 0).reshape(width, tokens)]
    all_to_all x1, waiting for transfers between devices: 8.57 us -> 12 us  [body(): signal = lax.all_to_all(gated_in.reshape(ctx, mine, tokens), CTX, 0, 0)]
    concatenate x3 -> x0, other arithmetic: 2.16 us -> none  [body(): both = jnp.concatenate([columns(s, 0), columns(s, 1)], 0)]
    dynamic_slice x1 -> x0, local copies, waits for them, and re-layouts: 2.07 us -> none  [columns(): return lax.dynamic_slice_in_dim(out_weight, (row * nx + to) * cols, cols, 1)]
    pallas_call x4 -> x11, Pallas kernels: 25.2 us -> 27 us  [call(): pl.pallas_call(kernel, out_shape=shapes, in_specs=specs or [VM] * len(arg...]
  transfers between devices with their start and end apart: 10 -> 17, of which waited for: 8 -> 9; matrix products, arithmetic and copies ran while one was open for 8% -> 0% of each run, Pallas kernels for 7% -> 11%
where the time goes in v2:
time: 122 us; the launch traced here: 119 us
  waiting for transfers between devices  44.9 us (37%)
  starting transfers between devices  42.5 us (35%)
  Pallas kernels  27 us (22%)
  local copies, waits for them, and re-layouts  4.88 us (4%)
    pallas_call x11, Pallas kernels, call(): pl.pallas_call(kernel, out_shape=shapes, in_specs=specs or [VM] * len(arg...  27 us
    ppermute x3, waiting for transfers between devices, body(): came = lax.ppermute(blocks[s], 'x', ring('x', s))  20.1 us
    all_to_all x1, waiting for transfers between devices, body(): signal = lax.all_to_all(gated_in.reshape(ctx, mine, tokens), CTX, 0, 0)  12 us
    all_to_all x1, starting transfers between devices, body(): signal = lax.all_to_all(gated_in.reshape(ctx, mine, tokens), CTX, 0, 0)  11.9 us
    ppermute x6, waiting for transfers between devices, send(): return lax.ppermute(block, 'x', ring('x', shift))  7.65 us
    ppermute x6, starting transfers between devices, send(): return lax.ppermute(block, 'x', ring('x', shift))  7.5 us
    ppermute x2, starting transfers between devices, body(): theirs.append(lax.ppermute(sums, 'yh', ring('yh', 1)))  6.02 us
    all_to_all x1, starting transfers between devices, body(): returned = lax.all_to_all(convolved, CTX, 0, 0).reshape(width, tokens)  4.88 us
  transfers between devices with their start and end apart: 17, of which 9 were waited for; matrix products, arithmetic and copies ran while one was open for 0% of the time, Pallas kernels for 11%

profile of v2, /device:TPU:1, one launch (start us, length us, event | category | flops | bytes accessed | tf_op | source)
XLA Modules:
  0.0 119.5 jit_solution(4705232600326380842)
XLA Ops:
  0.0 0.0 copy-start.7
  0.0 0.0 copy-start.6
  0.0 0.0 copy-start.5
  0.0 0.9 slice.4
  0.9 4.6 %collective-permute-start = (bf16[3,8,512]{2,1,0:T(8,128)(2,1)S(1)}, bf16[3,8,512]{2,1,0:T(8,128)(2,1)S(1)}, u32[]{:S(2)}, u32[]{:S(2)}) collective-permute-start(bf16[3,8,512]{2,1,0:T(8,128)(2,1)S(1)} %slice.4), channel_id=1, source_target_pairs={{0,8},{8,16},{16,24},{24,32},{32,40},{40,48},{48,56},{56,64},{64,7... | collective-permute-start | bytes 73736 | tf_op jit(solution)/shard_map/ppermute | solution.py:272
  5.5 0.9 collective-permute-done.edge_ref
  6.4 0.6 copy-done.3
  7.0 3.8 %shard_map.92 = bf16[512,512]{1,0:T(8,128)(2,1)} custom-call(bf16[3,8,512]{2,1,0:T(8,128)(2,1)} %copy-done.3, bf16[3,512,512]{2,1,0:T(8,128)(2,1)} %bitcast.5, f32[3,3,512]{2,1,0:T(4,128)} %taps_hbm.1), custom_call_target="tpu_custom_call" | custom-call | bytes 1615872 | tf_op jit(solution)/shard_map/pallas_call | solution.py:251
  10.8 11.9 %all-to-all-start = ((bf16[32,16,512]{2,1,0:T(8,128)(2,1)}), bf16[32,16,512]{2,1,0:T(8,128)(2,1)S(1)}, u32[]{:S(2)}, u32[]{:S(2)}) async-start(bf16[32,16,512]{2,1,0:T(8,128)(2,1)} %bitcast.9), calls=%async_computation | async-start | bytes 1048576 | tf_op jit(solution)/shard_map/all_to_all | solution.py:280
  22.6 0.0 copy-done.7
  22.6 0.0 copy-done.6
  22.7 0.0 copy-done.8
  22.7 0.0 copy-done.5
  22.7 3.2 %shard_map.93.refs_0_ = f32[16,128,256]{2,1,0:T(8,128)S(1)} custom-call(f32[16,16384]{1,0:T(8,128)S(1)} %bitcast.8, bf16[2,256,128]{2,1,0:T(8,128)(2,1)S(1)} %copy-done.7, bf16[2,256,256]{2,1,0:T(8,128)(2,1)S(1)} %copy-done.6, f32[2,128,128]{2,1,0:T(8,128)S(1)} %copy-done.8), custom_call_target="tpu_custom_call" | custom-call | flops 1000000000 | bytes 1572864 | tf_op jit(solution)/shard_map/pallas_call | solution.py:251
  25.9 0.0 copy-start.9
  25.9 1.4 %copy-done.9 = f32[16,128,256]{2,1,0:T(8,128)} copy-done((f32[16,128,256]{2,1,0:T(8,128)}, f32[16,128,256]{2,1,0:T(8,128)S(1)}, u32[]{:S(2)}) %copy-start.9) | copy-done | bytes 2097176
  27.2 12.0 %all-to-all-done.u_ref = bf16[32,16,512]{2,1,0:T(8,128)(2,1)S(1)} async-done(((bf16[32,16,512]{2,1,0:T(8,128)(2,1)}), bf16[32,16,512]{2,1,0:T(8,128)(2,1)S(1)}, u32[]{:S(2)}, u32[]{:S(2)}) %all-to-all-start) | async-done | bytes 524320 | tf_op jit(solution)/shard_map/all_to_all | solution.py:280
  39.2 0.8 copy-done.10
  40.0 9.8 %shard_map.94 = bf16[32,16,512]{2,1,0:T(8,128)(2,1)} custom-call(bf16[32,16,512]{2,1,0:T(8,128)(2,1)} %copy-done.10, f32[16,128,256]{2,1,0:T(8,128)} %copy-done.9, bf16[2,256,128]{2,1,0:T(8,128)(2,1)} %constant.10.clone.fwd1_ref.refs_1_, bf16[2,256,256]{2,1,0:T(8,128)(2,1)} %constant.11.clone.fwd2_ref.refs_2_, bf16[2,256,256]{2,1,0:T(8,128)(2,1)} %constant.12.clone.refs_3_, ...), custom_call_target="tpu_custom_call" | custom-call | flops 3000000000 | bytes 3538944 | tf_op jit(solution)/shard_map/pallas_call | solution.py:251
  49.8 4.9 %all-to-all-start.1 = ((bf16[32,16,512]{2,1,0:T(8,128)(2,1)}), bf16[32,16,512]{2,1,0:T(8,128)(2,1)S(1)}, u32[]{:S(2)}, u32[]{:S(2)}) async-start(bf16[32,16,512]{2,1,0:T(8,128)(2,1)} %shard_map.94), calls=%async_computation.1 | async-start | bytes 1048576 | tf_op jit(solution)/shard_map/all_to_all | solution.py:301
  54.7 0.0 copy-start
  54.7 0.0 copy-start.2
  54.7 0.0 copy-start.4
  54.7 3.4 %shard_map.96 = (bf16[2,512,512]{2,1,0:T(8,128)(2,1)}, bf16[2,256,512]{2,1,0:T(8,128)(2,1)}, bf16[2,256,512]{2,1,0:T(8,128)(2,1)}, bf16[2,256,512]{2,1,0:T(8,128)(2,1)}) custom-call(bf16[512,4096]{1,0:T(8,128)(2,1)} %refs_0_), custom_call_target="tpu_custom_call" | custom-call | bytes 4194304 | tf_op jit(solution)/shard_map/pallas_call | solution.py:251
  58.1 2.8 %collective-permute-start.9 = (bf16[2,256,512]{2,1,0:T(8,128)(2,1)}, bf16[2,256,512]{2,1,0:T(8,128)(2,1)S(1)}, u32[]{:S(2)}, u32[]{:S(2)}) collective-permute-start(bf16[2,256,512]{2,1,0:T(8,128)(2,1)} %get-tuple-element.26), channel_id=1, source_target_pairs={{0,2},{1,3},{2,0},{3,1},{4,6},{5,7},{6,4},{7,5},{8,10},{9,11},{10,... | collective-permute-start | bytes 1572872 | tf_op jit(solution)/shard_map/ppermute | solution.py:291
  60.9 0.9 collective-permute-start.11
  61.8 0.6 collective-permute-start.7
  62.4 10.7 %collective-permute-done.9.refs_3_ = bf16[2,256,512]{2,1,0:T(8,128)(2,1)S(1)} collective-permute-done((bf16[2,256,512]{2,1,0:T(8,128)(2,1)}, bf16[2,256,512]{2,1,0:T(8,128)(2,1)S(1)}, u32[]{:S(2)}, u32[]{:S(2)}) %collective-permute-start.9) | collective-permute-done | bytes 524320 | tf_op jit(solution)/shard_map/ppermute | solution.py:291
  73.0 2.0 %collective-permute-start.10 = (bf16[2,256,512]{2,1,0:T(8,128)(2,1)S(1)}, bf16[2,256,512]{2,1,0:T(8,128)(2,1)}, u32[]{:S(2)}, u32[]{:S(2)}) collective-permute-start(bf16[2,256,512]{2,1,0:T(8,128)(2,1)S(1)} %collective-permute-done.9.refs_3_), channel_id=1, source_target_pairs={{0,8},{8,0},{1,9},{9,1},{2,10},{10,2},{3,11},{11,3},{4,12},{12,4},... | collective-permute-start | bytes 1572872 | tf_op jit(solution)/shard_map/ppermute | solution.py:292
  75.1 9.4 %collective-permute-done.11.refs_5_ = bf16[2,256,512]{2,1,0:T(8,128)(2,1)} collective-permute-done((bf16[2,256,512]{2,1,0:T(8,128)(2,1)}, bf16[2,256,512]{2,1,0:T(8,128)(2,1)}, u32[]{:S(2)}, u32[]{:S(2)}) %collective-permute-start.11) | collective-permute-done | bytes 524320 | tf_op jit(solution)/shard_map/ppermute | solution.py:291
  84.5 1.2 %collective-permute-start.12 = (bf16[2,256,512]{2,1,0:T(8,128)(2,1)}, bf16[2,256,512]{2,1,0:T(8,128)(2,1)}, u32[]{:S(2)}, u32[]{:S(2)}) collective-permute-start(bf16[2,256,512]{2,1,0:T(8,128)(2,1)} %collective-permute-done.11.refs_5_), channel_id=1, source_target_pairs={{0,8},{8,0},{1,9},{9,1},{2,10},{10,2},{3,11},{11,3},{4,12},{12,4},... | collective-permute-start | bytes 1572872 | tf_op jit(solution)/shard_map/ppermute | solution.py:292
  85.7 0.0 copy-done
  85.7 0.0 copy-done.2
  85.7 0.0 copy-done.4
  85.7 0.6 shard_map.91.query_ref
  86.3 0.0 collective-permute-done.7.refs_1_
  86.3 0.1 collective-permute-start.8
  86.4 0.0 all-to-all-done.1
  86.4 0.2 shard_map.95
  86.7 2.4 %collective-permute-start.5 = (bf16[256,512]{1,0:T(8,128)(2,1)S(1)}, bf16[256,512]{1,0:T(8,128)(2,1)S(1)}, u32[]{:S(2)}, u32[]{:S(2)}) collective-permute-start(bf16[256,512]{1,0:T(8,128)(2,1)S(1)} %get-tuple-element.22.refs_4_.refs_0_), channel_id=1, source_target_pairs={{0,3},{1,0},{2,1},{3,2},{4,7},{5,4},{6,5},{7,6},{8,11},{9,8},{10,9... | collective-permute-start | bytes 786440 | tf_op jit(solution)/shard_map/ppermute | solution.py:307
  89.1 0.0 collective-permute-start.1
  89.1 0.0 collective-permute-done.10.refs_4_
  89.1 0.2 collective-permute-start.4
  89.3 5.0 %collective-permute-done.5.refs_7_.refs_3_ = bf16[256,512]{1,0:T(8,128)(2,1)S(1)} collective-permute-done((bf16[256,512]{1,0:T(8,128)(2,1)S(1)}, bf16[256,512]{1,0:T(8,128)(2,1)S(1)}, u32[]{:S(2)}, u32[]{:S(2)}) %collective-permute-start.5) | collective-permute-done | bytes 262176 | tf_op jit(solution)/shard_map/ppermute | solution.py:307
  94.3 3.4 %collective-permute-start.6 = (bf16[256,512]{1,0:T(8,128)(2,1)S(1)}, bf16[256,512]{1,0:T(8,128)(2,1)S(1)}, u32[]{:S(2)}, u32[]{:S(2)}) collective-permute-start(bf16[256,512]{1,0:T(8,128)(2,1)S(1)} %collective-permute-done.5.refs_7_.refs_3_), channel_id=1, source_target_pairs={{0,3},{1,0},{2,1},{3,2},{4,7},{5,4},{6,5},{7,6},{8,11},{9,8},{10,9... | collective-permute-start | bytes 786440 | tf_op jit(solution)/shard_map/ppermute | solution.py:307
  97.7 0.0 collective-permute-done.12.refs_6_
  97.7 0.0 collective-permute-start.3
  97.7 0.0 collective-permute-done.1.refs_1_
  97.7 1.4 %collective-permute-start.2 = (bf16[256,512]{1,0:T(8,128)(2,1)S(1)}, bf16[256,512]{1,0:T(8,128)(2,1)S(1)}, u32[]{:S(2)}, u32[]{:S(2)}) collective-permute-start(bf16[256,512]{1,0:T(8,128)(2,1)S(1)} %collective-permute-done.1.refs_1_), channel_id=1, source_target_pairs={{0,1},{1,2},{2,3},{3,0},{4,5},{5,6},{6,7},{7,4},{8,9},{9,10},{10,1... | collective-permute-start | bytes 786440 | tf_op jit(solution)/shard_map/ppermute | solution.py:307
  99.2 0.0 collective-permute-done.8.refs_2_
  99.2 1.2 %copy-done.1 = bf16[2,512,512]{2,1,0:T(8,128)(2,1)S(1)} copy-done((bf16[2,512,512]{2,1,0:T(8,128)(2,1)S(1)}, bf16[2,512,512]{2,1,0:T(8,128)(2,1)}, u32[]{:S(2)}) %copy-start.1) | copy-done | bytes 1048600
  100.4 1.7 %shard_map.97 = (bf16[2,512,512]{2,1,0:T(8,128)(2,1)S(1)}, bf16[2,256,512]{2,1,0:T(8,128)(2,1)S(1)}, bf16[2,256,512]{2,1,0:T(8,128)(2,1)S(1)}, bf16[2,256,512]{2...) custom-call(bf16[2,512,512]{2,1,0:T(8,128)(2,1)S(1)} %copy-done.1, ...), custom_call_target="tpu_custom_call" | custom-call | bytes 4194304 | tf_op jit(solution)/shard_map/pallas_call | solution.py:251
  102.1 1.0 collective-permute-done.4.refs_5_.refs_1_
  103.0 0.0 collective-permute-done.6.refs_6_.refs_2_
  103.0 0.9 shard_map.100
  103.9 3.0 %collective-permute-start.14 = (bf16[256,512]{1,0:T(8,128)(2,1)S(1)}, bf16[256,512]{1,0:T(8,128)(2,1)S(1)}, u32[]{:S(2)}, u32[]{:S(2)}) collective-permute-start(bf16[256,512]{1,0:T(8,128)(2,1)S(1)} %shard_map.100), channel_id=1, source_target_pairs={{0,4},{4,0},{1,5},{5,1},{2,6},{6,2},{3,7},{7,3},{8,12},{12,8},{9,1... | collective-permute-start | bytes 786440 | tf_op jit(solution)/shard_map/ppermute | solution.py:321
  106.9 0.7 collective-permute-done.3.refs_3_
  107.6 1.0 collective-permute-done.2.refs_2_
  108.6 0.9 shard_map.99
  109.5 3.0 %collective-permute-start.13 = (bf16[256,512]{1,0:T(8,128)(2,1)S(1)}, bf16[256,512]{1,0:T(8,128)(2,1)S(1)}, u32[]{:S(2)}, u32[]{:S(2)}) collective-permute-start(bf16[256,512]{1,0:T(8,128)(2,1)S(1)} %shard_map.99), channel_id=1, source_target_pairs={{0,4},{4,0},{1,5},{5,1},{2,6},{6,2},{3,7},{7,3},{8,12},{12,8},{9,1... | collective-permute-start | bytes 786440 | tf_op jit(solution)/shard_map/ppermute | solution.py:321
  112.5 1.8 %shard_map.98.own_ref = f32[512,512]{1,0:T(8,128)S(1)} custom-call(bf16[256,512]{1,0:T(8,128)(2,1)S(1)} %get-tuple-element.21.refs_0_, bf16[256,512]{1,0:T(8,128)(2,1)S(1)} %collective-permute-done.1.refs_1_, bf16[256,512]{1,0:T(8,128)(2,1)S(1)} %collective-permute-done.2.refs_2_, bf16[256,512]{1,0:T(8,128)(2,1)S(1)} %collective-permute-done.3.refs_3_, ...), custom_call_target="tpu_custom_call" | custom-call | flops 2000000000 | bytes 6291456 | tf_op jit(solution)/shard_map/pallas_call | solution.py:251
  114.3 0.0 collective-permute-done.14.second_ref
  114.3 4.3 %collective-permute-done.13.first_ref = bf16[256,512]{1,0:T(8,128)(2,1)S(1)} collective-permute-done((bf16[256,512]{1,0:T(8,128)(2,1)S(1)}, bf16[256,512]{1,0:T(8,128)(2,1)S(1)}, u32[]{:S(2)}, u32[]{:S(2)}) %collective-permute-start.13) | collective-permute-done | bytes 262176 | tf_op jit(solution)/shard_map/ppermute | solution.py:321
  118.6 0.9 shard_map.101
  (4 shorter events, 0.0 us)
Async XLA Ops:
  0.0 22.6 %copy-start.7 = (bf16[2,256,128]{2,1,0:T(8,128)(2,1)S(1)}, bf16[2,256,128]{2,1,0:T(8,128)(2,1)}, u32[]{:S(2)}) copy-start(bf16[2,256,128]{2,1,0:T(8,128)(2,1)} %constant.10.clone.fwd1_ref.refs_1_) | copy-start | bytes 393220
  0.0 22.6 %copy-start.6 = (bf16[2,256,256]{2,1,0:T(8,128)(2,1)S(1)}, bf16[2,256,256]{2,1,0:T(8,128)(2,1)}, u32[]{:S(2)}) copy-start(bf16[2,256,256]{2,1,0:T(8,128)(2,1)} %constant.11.clone.fwd2_ref.refs_2_) | copy-start | bytes 786436
  0.0 22.7 %copy-start.8 = (f32[2,128,128]{2,1,0:T(8,128)S(1)}, f32[2,128,128]{2,1,0:T(8,128)}, u32[]{:S(2)}) copy-start(f32[2,128,128]{2,1,0:T(8,128)} %constant.14.clone.twist_ref.refs_5_) | copy-start | bytes 393220
  0.0 22.7 %copy-start.5 = (f32[16384,16]{0,1:T(8,128)S(1)}, f32[16384,16]{0,1:T(8,128)}, u32[]{:S(2)}) copy-start(f32[16384,16]{0,1:T(8,128)} %param.11) | copy-start | bytes 3145732
  0.9 5.5 %collective-permute-start = (bf16[3,8,512]{2,1,0:T(8,128)(2,1)S(1)}, bf16[3,8,512]{2,1,0:T(8,128)(2,1)S(1)}, u32[]{:S(2)}, u32[]{:S(2)}) collective-permute-start(bf16[3,8,512]{2,1,0:T(8,128)(2,1)S(1)} %slice.4), channel_id=1, source_target_pairs={{0,8},{8,16},{16,24},{24,32},{32,40},{40,48},{48,56},{56,64},{64,7... | collective-permute-start | bytes 73736 | tf_op jit(solution)/shard_map/ppermute | solution.py:272
  6.4 0.6 copy-start.3
  10.8 28.4 %all-to-all-start = ((bf16[32,16,512]{2,1,0:T(8,128)(2,1)}), bf16[32,16,512]{2,1,0:T(8,128)(2,1)S(1)}, u32[]{:S(2)}, u32[]{:S(2)}) async-start(bf16[32,16,512]{2,1,0:T(8,128)(2,1)} %bitcast.9), calls=%async_computation | async-start | bytes 1048576 | tf_op jit(solution)/shard_map/all_to_all | solution.py:280
  25.9 1.4 %copy-start.9 = (f32[16,128,256]{2,1,0:T(8,128)}, f32[16,128,256]{2,1,0:T(8,128)S(1)}, u32[]{:S(2)}) copy-start(f32[16,128,256]{2,1,0:T(8,128)S(1)} %shard_map.93.refs_0_) | copy-start | bytes 6291460
  39.2 0.8 copy-start.10
  49.8 36.7 %all-to-all-start.1 = ((bf16[32,16,512]{2,1,0:T(8,128)(2,1)}), bf16[32,16,512]{2,1,0:T(8,128)(2,1)S(1)}, u32[]{:S(2)}, u32[]{:S(2)}) async-start(bf16[32,16,512]{2,1,0:T(8,128)(2,1)} %shard_map.94), calls=%async_computation.1 | async-start | bytes 1048576 | tf_op jit(solution)/shard_map/all_to_all | solution.py:301
  54.7 31.0 %copy-start = (bf16[512,3,512]{2,0,1:T(8,128)(2,1)S(1)}, bf16[512,3,512]{2,0,1:T(8,128)(2,1)}, u32[]{:S(2)}) copy-start(bf16[512,3,512]{2,0,1:T(8,128)(2,1)} %param.9) | copy-start | bytes 4718596
  54.7 31.0 %copy-start.2 = (f32[3,3,512]{2,1,0:T(4,128)S(1)}, f32[3,3,512]{2,1,0:T(4,128)}, u32[]{:S(2)}) copy-start(f32[3,3,512]{2,1,0:T(4,128)} %taps_hbm.1) | copy-start | bytes 55300
  54.7 31.0 %copy-start.4 = (bf16[3,8,512]{2,1,0:T(8,128)(2,1)S(1)}, bf16[3,8,512]{2,1,0:T(8,128)(2,1)}, u32[]{:S(2)}) copy-start(bf16[3,8,512]{2,1,0:T(8,128)(2,1)} %copy-done.3) | copy-start | bytes 73732
  58.1 15.0 %collective-permute-start.9 = (bf16[2,256,512]{2,1,0:T(8,128)(2,1)}, bf16[2,256,512]{2,1,0:T(8,128)(2,1)S(1)}, u32[]{:S(2)}, u32[]{:S(2)}) collective-permute-start(bf16[2,256,512]{2,1,0:T(8,128)(2,1)} %get-tuple-element.26), channel_id=1, source_target_pairs={{0,2},{1,3},{2,0},{3,1},{4,6},{5,7},{6,4},{7,5},{8,10},{9,11},{10,... | collective-permute-start | bytes 1572872 | tf_op jit(solution)/shard_map/ppermute | solution.py:291
  60.9 23.6 %collective-permute-start.11 = (bf16[2,256,512]{2,1,0:T(8,128)(2,1)}, bf16[2,256,512]{2,1,0:T(8,128)(2,1)}, u32[]{:S(2)}, u32[]{:S(2)}) collective-permute-start(bf16[2,256,512]{2,1,0:T(8,128)(2,1)} %get-tuple-element.27), channel_id=1, source_target_pairs={{0,3},{1,0},{2,1},{3,2},{4,7},{5,4},{6,5},{7,6},{8,11},{9,8},{10,9... | collective-permute-start | bytes 1572872 | tf_op jit(solution)/shard_map/ppermute | solution.py:291
  61.8 24.6 %collective-permute-start.7 = (bf16[2,256,512]{2,1,0:T(8,128)(2,1)}, bf16[2,256,512]{2,1,0:T(8,128)(2,1)}, u32[]{:S(2)}, u32[]{:S(2)}) collective-permute-start(bf16[2,256,512]{2,1,0:T(8,128)(2,1)} %get-tuple-element.25), channel_id=1, source_target_pairs={{0,1},{1,2},{2,3},{3,0},{4,5},{5,6},{6,7},{7,4},{8,9},{9,10},{10,1... | collective-permute-start | bytes 1572872 | tf_op jit(solution)/shard_map/ppermute | solution.py:291
  73.0 16.0 %collective-permute-start.10 = (bf16[2,256,512]{2,1,0:T(8,128)(2,1)S(1)}, bf16[2,256,512]{2,1,0:T(8,128)(2,1)}, u32[]{:S(2)}, u32[]{:S(2)}) collective-permute-start(bf16[2,256,512]{2,1,0:T(8,128)(2,1)S(1)} %collective-permute-done.9.refs_3_), channel_id=1, source_target_pairs={{0,8},{8,0},{1,9},{9,1},{2,10},{10,2},{3,11},{11,3},{4,12},{12,4},... | collective-permute-start | bytes 1572872 | tf_op jit(solution)/shard_map/ppermute | solution.py:292
  84.5 13.2 %collective-permute-start.12 = (bf16[2,256,512]{2,1,0:T(8,128)(2,1)}, bf16[2,256,512]{2,1,0:T(8,128)(2,1)}, u32[]{:S(2)}, u32[]{:S(2)}) collective-permute-start(bf16[2,256,512]{2,1,0:T(8,128)(2,1)} %collective-permute-done.11.refs_5_), channel_id=1, source_target_pairs={{0,8},{8,0},{1,9},{9,1},{2,10},{10,2},{3,11},{11,3},{4,12},{12,4},... | collective-permute-start | bytes 1572872 | tf_op jit(solution)/shard_map/ppermute | solution.py:292
  86.3 12.8 %collective-permute-start.8 = (bf16[2,256,512]{2,1,0:T(8,128)(2,1)}, bf16[2,256,512]{2,1,0:T(8,128)(2,1)S(1)}, u32[]{:S(2)}, u32[]{:S(2)}) collective-permute-start(bf16[2,256,512]{2,1,0:T(8,128)(2,1)} %collective-permute-done.7.refs_1_), channel_id=1, source_target_pairs={{0,8},{8,0},{1,9},{9,1},{2,10},{10,2},{3,11},{11,3},{4,12},{12,4},... | collective-permute-start | bytes 1572872 | tf_op jit(solution)/shard_map/ppermute | solution.py:292
  86.7 7.6 %collective-permute-start.5 = (bf16[256,512]{1,0:T(8,128)(2,1)S(1)}, bf16[256,512]{1,0:T(8,128)(2,1)S(1)}, u32[]{:S(2)}, u32[]{:S(2)}) collective-permute-start(bf16[256,512]{1,0:T(8,128)(2,1)S(1)} %get-tuple-element.22.refs_4_.refs_0_), channel_id=1, source_target_pairs={{0,3},{1,0},{2,1},{3,2},{4,7},{5,4},{6,5},{7,6},{8,11},{9,8},{10,9... | collective-permute-start | bytes 786440 | tf_op jit(solution)/shard_map/ppermute | solution.py:307
  89.1 8.6 %collective-permute-start.1 = (bf16[256,512]{1,0:T(8,128)(2,1)S(1)}, bf16[256,512]{1,0:T(8,128)(2,1)S(1)}, u32[]{:S(2)}, u32[]{:S(2)}) collective-permute-start(bf16[256,512]{1,0:T(8,128)(2,1)S(1)} %get-tuple-element.21.refs_0_), channel_id=1, source_target_pairs={{0,1},{1,2},{2,3},{3,0},{4,5},{5,6},{6,7},{7,4},{8,9},{9,10},{10,1... | collective-permute-start | bytes 786440 | tf_op jit(solution)/shard_map/ppermute | solution.py:307
  89.1 13.9 %collective-permute-start.4 = (bf16[256,512]{1,0:T(8,128)(2,1)S(1)}, bf16[256,512]{1,0:T(8,128)(2,1)S(1)}, u32[]{:S(2)}, u32[]{:S(2)}) collective-permute-start(bf16[256,512]{1,0:T(8,128)(2,1)S(1)} %get-tuple-element.22.refs_4_.refs_0_), channel_id=1, source_target_pairs={{0,1},{1,2},{2,3},{3,0},{4,5},{5,6},{6,7},{7,4},{8,9},{9,10},{10,1... | collective-permute-start | bytes 786440 | tf_op jit(solution)/shard_map/ppermute | solution.py:307
  94.3 8.7 %collective-permute-start.6 = (bf16[256,512]{1,0:T(8,128)(2,1)S(1)}, bf16[256,512]{1,0:T(8,128)(2,1)S(1)}, u32[]{:S(2)}, u32[]{:S(2)}) collective-permute-start(bf16[256,512]{1,0:T(8,128)(2,1)S(1)} %collective-permute-done.5.refs_7_.refs_3_), channel_id=1, source_target_pairs={{0,3},{1,0},{2,1},{3,2},{4,7},{5,4},{6,5},{7,6},{8,11},{9,8},{10,9... | collective-permute-start | bytes 786440 | tf_op jit(solution)/shard_map/ppermute | solution.py:307
  97.7 9.9 %collective-permute-start.3 = (bf16[256,512]{1,0:T(8,128)(2,1)S(1)}, bf16[256,512]{1,0:T(8,128)(2,1)S(1)}, u32[]{:S(2)}, u32[]{:S(2)}) collective-permute-start(bf16[256,512]{1,0:T(8,128)(2,1)S(1)} %get-tuple-element.21.refs_0_), channel_id=1, source_target_pairs={{0,3},{1,0},{2,1},{3,2},{4,7},{5,4},{6,5},{7,6},{8,11},{9,8},{10,9... | collective-permute-start | bytes 786440 | tf_op jit(solution)/shard_map/ppermute | solution.py:307
  97.7 10.9 %collective-permute-start.2 = (bf16[256,512]{1,0:T(8,128)(2,1)S(1)}, bf16[256,512]{1,0:T(8,128)(2,1)S(1)}, u32[]{:S(2)}, u32[]{:S(2)}) collective-permute-start(bf16[256,512]{1,0:T(8,128)(2,1)S(1)} %collective-permute-done.1.refs_1_), channel_id=1, source_target_pairs={{0,1},{1,2},{2,3},{3,0},{4,5},{5,6},{6,7},{7,4},{8,9},{9,10},{10,1... | collective-permute-start | bytes 786440 | tf_op jit(solution)/shard_map/ppermute | solution.py:307
  99.2 1.2 %copy-start.1 = (bf16[2,512,512]{2,1,0:T(8,128)(2,1)S(1)}, bf16[2,512,512]{2,1,0:T(8,128)(2,1)}, u32[]{:S(2)}) copy-start(bf16[2,512,512]{2,1,0:T(8,128)(2,1)} %get-tuple-element.24.refs_0_) | copy-start | bytes 3145732
  103.9 10.4 %collective-permute-start.14 = (bf16[256,512]{1,0:T(8,128)(2,1)S(1)}, bf16[256,512]{1,0:T(8,128)(2,1)S(1)}, u32[]{:S(2)}, u32[]{:S(2)}) collective-permute-start(bf16[256,512]{1,0:T(8,128)(2,1)S(1)} %shard_map.100), channel_id=1, source_target_pairs={{0,4},{4,0},{1,5},{5,1},{2,6},{6,2},{3,7},{7,3},{8,12},{12,8},{9,1... | collective-permute-start | bytes 786440 | tf_op jit(solution)/shard_map/ppermute | solution.py:321
  109.5 9.1 %collective-permute-start.13 = (bf16[256,512]{1,0:T(8,128)(2,1)S(1)}, bf16[256,512]{1,0:T(8,128)(2,1)S(1)}, u32[]{:S(2)}, u32[]{:S(2)}) collective-permute-start(bf16[256,512]{1,0:T(8,128)(2,1)S(1)} %shard_map.99), channel_id=1, source_target_pairs={{0,4},{4,0},{1,5},{5,1},{2,6},{6,2},{3,7},{7,3},{8,12},{12,8},{9,1... | collective-permute-start | bytes 786440 | tf_op jit(solution)/shard_map/ppermute | solution.py:321

commit v3 on v2

--- a/solution.py
+++ b/solution.py
@@ -10,10 +10,8 @@
 CTX = ("z", "yl", "core")
 SIDE = 128
 LENGTH = SIDE * SIDE
-WIDE = 4
 EDGE = 8
 LIMIT = 16 * 2**20
-FULL = 60 * 1024 * 2**10
 f32, bf16 = jnp.float32, jnp.bfloat16
 
 
@@ -31,10 +29,9 @@
     c1, s1, c2, s2 = np.cos(first), np.sin(first), np.cos(second), np.sin(second)
     fwd1 = np.concatenate([c1, s1], 0)
     fwd2 = np.block([[c2, s2], [-s2, c2]])
-    inv1 = np.block([[c2, -s2], [s2, c2]])
     inv2 = np.concatenate([c1.T, s1.T], 1) / LENGTH
     twist = np.stack([np.cos(turn), np.sin(turn)]).astype(np.float32)
-    return halves(fwd1), halves(fwd2), halves(inv1), halves(inv2), twist
+    return halves(fwd1), halves(fwd2), halves(inv2), twist
 
 
 def split(x):
@@ -70,15 +67,10 @@
     for n in range(SIDE):
         rows[n * channels : (n + 1) * channels, :] = h_ref[:, n * SIDE : (n + 1) * SIDE]
 
-    def step(p, carry):
-        group = [rows[pl.ds(WIDE * p + w, SIDE, stride=channels), :] for w in range(WIDE)]
-        first = left3(fwd1_ref, jnp.concatenate(group, 1))
-        spectra = right3(stacked(first, twist_ref), fwd2_ref)
-        for w in range(WIDE):
-            out_ref[WIDE * p + w] = spectra[w * SIDE : (w + 1) * SIDE]
-        return carry
-
-    lax.fori_loop(0, channels // WIDE, step, 0)
+    group = jnp.concatenate([rows[pl.ds(w, SIDE, stride=channels), :] for w in range(channels)], 1)
+    spectra = right3(stacked(left3(fwd1_ref, group), twist_ref), fwd2_ref)
+    for w in range(channels):
+        out_ref[w] = spectra[w * SIDE : (w + 1) * SIDE]
 
 
 def fetch(sources, targets, sem):
@@ -89,8 +81,9 @@
 
 
 def conv_kernel(u_ref, *refs):
-    sources, out_ref, rows, back, held, sem = refs[:6], refs[6], refs[7], refs[8], refs[9:15], refs[15]
-    h_ref, fwd1_ref, fwd2_ref, inv1_ref, inv2_ref, twist_ref = held
+    sources, out_hbm, rows, back, out_ref = refs[:5], refs[5], refs[6], refs[7], refs[8]
+    held, sem, out_sem = refs[9:14], refs[14], refs[15]
+    fwd1_ref, twist_ref, fwd2_ref, h_ref, inv2_ref = held
     copies = fetch(sources, held, sem)
     blocks, channels, local = u_ref.shape
     per = local // SIDE
@@ -98,35 +91,38 @@
         for q in range(per):
             n = i * per + q
             rows[n * channels : (n + 1) * channels, :] = u_ref[i, :, q * SIDE : (q + 1) * SIDE].astype(f32)
-    for c in copies:
-        c.wait()
-
-    def step(p, carry):
-        group = [rows[pl.ds(WIDE * p + w, SIDE, stride=channels), :] for w in range(WIDE)]
-        group = jnp.concatenate(group, 1).astype(bf16)
-        first = mm(fwd1_ref[0], group) + mm(fwd1_ref[1], group)
-        spectra = right3(stacked(first, twist_ref), fwd2_ref)
-        products = []
-        for w in range(WIDE):
-            s, h = spectra[w * SIDE : (w + 1) * SIDE], h_ref[WIDE * p + w]
-            sr, si, hr, hi = s[:, :SIDE], s[:, SIDE:], h[:, :SIDE], h[:, SIDE:]
-            products.append(jnp.concatenate([sr * hr - si * hi, sr * hi + si * hr], 1))
-        b = right3(jnp.concatenate(products, 0), inv1_ref)
-        tc, ts = twist_ref[0], twist_ref[1]
-        turned = []
-        for w in range(WIDE):
-            br, bi = b[w * SIDE : (w + 1) * SIDE, :SIDE], b[w * SIDE : (w + 1) * SIDE, SIDE:]
-            turned.append(jnp.concatenate([br * tc + bi * ts, bi * tc - br * ts], 0))
-        y = left3(inv2_ref, jnp.concatenate(turned, 1))
-        for w in range(WIDE):
-            back[pl.ds(WIDE * p + w, SIDE, stride=channels), :] = y[:, w * SIDE : (w + 1) * SIDE]
-        return carry
-
-    lax.fori_loop(0, channels // WIDE, step, 0)
+    group = jnp.concatenate([rows[pl.ds(w, SIDE, stride=channels), :] for w in range(channels)], 1).astype(bf16)
+    for c in copies[:3]:
+        c.wait()
+    first = mm(fwd1_ref[0], group) + mm(fwd1_ref[1], group)
+    spectra = right3(stacked(first, twist_ref), fwd2_ref)
+    for c in copies[3:]:
+        c.wait()
+    products = []
+    for w in range(channels):
+        s, h = spectra[w * SIDE : (w + 1) * SIDE], h_ref[w]
+        sr, si, hr, hi = s[:, :SIDE], s[:, SIDE:], h[:, :SIDE], h[:, SIDE:]
+        products.append(jnp.concatenate([sr * hr - si * hi, -(sr * hi + si * hr)], 1))
+    b = right3(jnp.concatenate(products, 0), fwd2_ref)
+    tc, ts = twist_ref[0], twist_ref[1]
+    turned = []
+    for w in range(channels):
+        br, bi = b[w * SIDE : (w + 1) * SIDE, :SIDE], b[w * SIDE : (w + 1) * SIDE, SIDE:]
+        turned.append(jnp.concatenate([br * tc - bi * ts, -(bi * tc + br * ts)], 0))
+    y = left3(inv2_ref, jnp.concatenate(turned, 1))
+    for w in range(channels):
+        back[pl.ds(w, SIDE, stride=channels), :] = y[:, w * SIDE : (w + 1) * SIDE]
+    outs = []
     for i in range(blocks):
         for q in range(per):
             n = i * per + q
             out_ref[i, :, q * SIDE : (q + 1) * SIDE] = back[n * channels : (n + 1) * channels, :].astype(bf16)
+        if (i + 1) % (blocks // 4) == 0:
+            at = pl.ds(i + 1 - blocks // 4, blocks // 4)
+            outs.append(pltpu.make_async_copy(out_ref.at[at], out_hbm.at[at], out_sem.at[len(outs)]))
+            outs[-1].start()
+    for c in outs:
+        c.wait()
 
 
 def featured(x, edge_ref, taps_ref, ext, s):
@@ -245,19 +241,39 @@
     return [pltpu.VMEM(a.shape, a.dtype) for a in arrays] + [pltpu.SemaphoreType.DMA((len(arrays),))]
 
 
-def call(kernel, outs, scratch, flops, *args, specs=None, limit=LIMIT):
+def call(kernel, outs, scratch, flops, *args, specs=None, outs_at=VM):
+    specs = specs or [VM] * len(args)
+    args = [pltpu.with_memory_space_constraint(a, pltpu.HBM) if s is HBM else a for a, s in zip(args, specs)]
     moved = sum(a.size * a.dtype.itemsize for a in args)
     shapes = [jax.ShapeDtypeStruct(*o) for o in outs]
     result = pl.pallas_call(
         kernel,
         out_shape=shapes,
-        in_specs=specs or [VM] * len(args),
-        out_specs=[VM] * len(shapes),
+        in_specs=specs,
+        out_specs=[outs_at] * len(shapes),
         scratch_shapes=scratch,
-        compiler_params=pltpu.CompilerParams(vmem_limit_bytes=limit),
+        compiler_params=pltpu.CompilerParams(vmem_limit_bytes=LIMIT),
         cost_estimate=pl.CostEstimate(flops=flops, bytes_accessed=moved, transcendentals=0),
     )(*args)
     return result if len(shapes) > 1 else result[0]
+
+
+def transform(long_filter, fwd1, fwd2, twist):
+    mine = long_filter.shape[1]
+    rows = [pltpu.VMEM((SIDE * mine, SIDE), f32)]
+    return call(filter_kernel, [((mine, SIDE, 2 * SIDE), f32)], rows, 10**9, long_filter.T, fwd1, fwd2, twist)
+
+
+def convolve(signal, spectrum, fwd1, fwd2, inv2, twist):
+    mine = signal.shape[1]
+    rows = [pltpu.VMEM((SIDE * mine, SIDE), f32)] * 2
+    inside = [pltpu.VMEM(signal.shape, bf16)]
+    kept = held(fwd1, twist, fwd2, spectrum, inv2)[:-1]
+    sems = [pltpu.SemaphoreType.DMA((5,)), pltpu.SemaphoreType.DMA((4,))]
+    return call(
+        conv_kernel, [(signal.shape, bf16)], rows + inside + kept + sems, 3 * 10**9,
+        signal, fwd1, twist, fwd2, spectrum, inv2, specs=[VM] + [HBM] * 5, outs_at=HBM,
+    )
 
 
 def body(proj, short_filter, long_filter, out_weight):
@@ -266,7 +282,7 @@
     mine = width // ctx
     nx, ny = lax.axis_size("x"), lax.axis_size("yh")
     cols = out_weight.shape[1] // (nx * ny)
-    fwd1, fwd2, inv1, inv2, twist = [jnp.asarray(t) for t in tables()]
+    fwd1, fwd2, inv2, twist = [jnp.asarray(t) for t in tables()]
 
     streams_first = jnp.transpose(proj, (1, 0, 2))
     edge = lax.ppermute(streams_first[:, tokens - EDGE :, :], CTX, [(i, i + 1) for i in range(ctx - 1)])
@@ -274,7 +290,7 @@
     gated_in = call(
         gate_in_kernel, [((width, tokens), bf16)],
         ext + held(streams_first[1], streams_first[2], short_filter), 0,
-        edge, streams_first, short_filter, specs=[VM, HBM, HBM], limit=FULL,
+        edge, streams_first, short_filter, specs=[VM, HBM, HBM],
     )
     gated_in, out_weight = lax.optimization_barrier((gated_in, out_weight))
     signal = lax.all_to_all(gated_in.reshape(ctx, mine, tokens), CTX, 0, 0)
@@ -284,20 +300,15 @@
 
     blocks = call(
         columns, [((ny, width if s == 0 else width // 2, cols), bf16) for s in range(nx)],
-        [pltpu.SemaphoreType.DMA((ny * nx,))], 0, out_weight, specs=[HBM], limit=FULL,
+        [pltpu.SemaphoreType.DMA((ny * nx,))], 0, out_weight, specs=[HBM],
     )
     weights = [blocks[0]]
     for s in range(1, nx):
         came = lax.ppermute(blocks[s], "x", ring("x", s))
         weights += [came, lax.ppermute(came, "core", ring("core", 1))]
 
-    rows = [pltpu.VMEM((SIDE * mine, SIDE), f32)]
-    spectrum = call(filter_kernel, [((mine, SIDE, 2 * SIDE), f32)], rows, 10**9, long_filter.T, fwd1, fwd2, twist)
-    convolved = call(
-        conv_kernel, [((ctx, mine, tokens), bf16)],
-        rows * 2 + held(spectrum, fwd1, fwd2, inv1, inv2, twist), 3 * 10**9,
-        signal, spectrum, fwd1, fwd2, inv1, inv2, twist, specs=[VM] + [HBM] * 6, limit=FULL,
-    )
+    spectrum = transform(long_filter, fwd1, fwd2, twist)
+    convolved = convolve(signal, spectrum, fwd1, fwd2, inv2, twist)
     returned = lax.all_to_all(convolved, CTX, 0, 0).reshape(width, tokens)
     query = call(query_kernel, [((tokens, width), f32)], ext, 0, streams_first, edge, short_filter)
     half = tokens // 2

time: 122 us -> 115 us (0.943)
  Pallas kernels: 27 us -> 21.4 us
  local copies, waits for them, and re-layouts: 4.88 us -> 2.26 us
  waiting for transfers between devices: 44.9 us -> 46.3 us
    pallas_call x11, Pallas kernels: 27 us -> 21.4 us  [call(): pl.pallas_call(kernel, out_shape=shapes, in_specs=specs, out_specs=[outs_...]
    unnamed x22, local copies, waits for them, and re-layouts: 4.02 us -> 1.4 us
  transfers between devices with their start and end apart: 17 -> 17, of which waited for: 9 -> 9; matrix products, arithmetic and copies ran while one was open for 0% -> 0% of each run, Pallas kernels for 11% -> 9%
where the time goes in v3:
time: 115 us; the launch traced here: 113 us
  waiting for transfers between devices  46.3 us (40%)
  starting transfers between devices  42.5 us (37%)
  Pallas kernels  21.4 us (19%)
  local copies, waits for them, and re-layouts  2.26 us (2%)
    pallas_call x11, Pallas kernels, call(): pl.pallas_call(kernel, out_shape=shapes, in_specs=specs, out_specs=[outs_...  21.4 us
    ppermute x3, waiting for transfers between devices, body(): came = lax.ppermute(blocks[s], 'x', ring('x', s))  19.8 us
    all_to_all x1, waiting for transfers between devices, body(): signal = lax.all_to_all(gated_in.reshape(ctx, mine, tokens), CTX, 0, 0)  12.9 us
    all_to_all x1, starting transfers between devices, body(): signal = lax.all_to_all(gated_in.reshape(ctx, mine, tokens), CTX, 0, 0)  11.9 us
    ppermute x6, waiting for transfers between devices, send(): return lax.ppermute(block, 'x', ring('x', shift))  8.34 us
    ppermute x6, starting transfers between devices, send(): return lax.ppermute(block, 'x', ring('x', shift))  7.51 us
    ppermute x2, starting transfers between devices, body(): theirs.append(lax.ppermute(sums, 'yh', ring('yh', 1)))  6.01 us
    all_to_all x1, starting transfers between devices, body(): returned = lax.all_to_all(convolved, CTX, 0, 0).reshape(width, tokens)  4.89 us
  transfers between devices with their start and end apart: 17, of which 9 were waited for; matrix products, arithmetic and copies ran while one was open for 0% of the time, Pallas kernels for 9%

profile of v3, /device:TPU:1, one launch (start us, length us, event | category | flops | bytes accessed | tf_op | source)
XLA Modules:
  0.0 112.6 jit_solution(1845644364813300086)
XLA Ops:
  0.0 0.0 copy-start.5
  0.0 0.0 copy-start.3
  0.0 0.9 slice.4
  0.9 4.6 %collective-permute-start = (bf16[3,8,512]{2,1,0:T(8,128)(2,1)S(1)}, bf16[3,8,512]{2,1,0:T(8,128)(2,1)S(1)}, u32[]{:S(2)}, u32[]{:S(2)}) collective-permute-start(bf16[3,8,512]{2,1,0:T(8,128)(2,1)S(1)} %slice.4), channel_id=1, source_target_pairs={{0,8},{8,16},{16,24},{24,32},{32,40},{40,48},{48,56},{56,64},{64,7... | collective-permute-start | bytes 73736 | tf_op jit(solution)/shard_map/ppermute | solution.py:288
  5.5 0.9 collective-permute-done.edge_ref
  6.4 3.0 %shard_map.83 = bf16[512,512]{1,0:T(8,128)(2,1)} custom-call(bf16[3,8,512]{2,1,0:T(8,128)(2,1)S(1)} %collective-permute-done.edge_ref, bf16[3,512,512]{2,1,0:T(8,128)(2,1)} %bitcast.5, f32[3,3,512]{2,1,0:T(4,128)} %taps_hbm.1), custom_call_target="tpu_custom_call" | custom-call | bytes 1615872 | tf_op jit(solution)/shard_map/pallas_call | solution.py:249
  9.4 11.9 %all-to-all-start = ((bf16[32,16,512]{2,1,0:T(8,128)(2,1)}), bf16[32,16,512]{2,1,0:T(8,128)(2,1)S(1)}, u32[]{:S(2)}, u32[]{:S(2)}) async-start(bf16[32,16,512]{2,1,0:T(8,128)(2,1)} %bitcast.1), calls=%async_computation | async-start | bytes 1048576 | tf_op jit(solution)/shard_map/all_to_all | solution.py:296
  21.3 0.0 copy-done.5
  21.3 0.0 copy-done.6
  21.3 0.0 copy-done.4
  21.3 0.0 copy-done.3
  21.3 2.2 %shard_map.84.refs_3_ = f32[16,128,256]{2,1,0:T(8,128)S(1)} custom-call(f32[16,16384]{1,0:T(8,128)S(1)} %bitcast.8, bf16[2,256,128]{2,1,0:T(8,128)(2,1)S(1)} %copy-done.6, bf16[2,256,256]{2,1,0:T(8,128)(2,1)S(1)} %copy-done.4, f32[2,128,128]{2,1,0:T(8,128)S(1)} %copy-done.5), custom_call_target="tpu_custom_call" | custom-call | flops 1000000000 | bytes 1572864 | tf_op jit(solution)/shard_map/pallas_call | solution.py:249
  23.5 0.0 copy-start.7
  23.5 1.4 %copy-done.7 = f32[16,128,256]{2,1,0:T(8,128)} copy-done((f32[16,128,256]{2,1,0:T(8,128)}, f32[16,128,256]{2,1,0:T(8,128)S(1)}, u32[]{:S(2)}) %copy-start.7) | copy-done | bytes 2097176
  24.9 12.9 %all-to-all-done.u_ref = bf16[32,16,512]{2,1,0:T(8,128)(2,1)S(1)} async-done(((bf16[32,16,512]{2,1,0:T(8,128)(2,1)}), bf16[32,16,512]{2,1,0:T(8,128)(2,1)S(1)}, u32[]{:S(2)}, u32[]{:S(2)}) %all-to-all-start) | async-done | bytes 524320 | tf_op jit(solution)/shard_map/all_to_all | solution.py:296
  37.8 6.8 %shard_map.85 = bf16[32,16,512]{2,1,0:T(8,128)(2,1)} custom-call(bf16[32,16,512]{2,1,0:T(8,128)(2,1)S(1)} %all-to-all-done.u_ref, bf16[2,256,128]{2,1,0:T(8,128)(2,1)} %constant.8.clone.fwd1_ref.refs_0_, f32[2,128,128]{2,1,0:T(8,128)} %constant.11.clone.twist_ref.refs_1_, bf16[2,256,256]{2,1,0:T(8,128)(2,1)} %constant.9.clone.fwd2_ref.refs_2_, ...), custom_call_target="tpu_custom_call" | custom-call | flops 3000000000 | bytes 3276800 | tf_op jit(solution)/shard_map/pallas_call | solution.py:249
  44.7 4.9 %all-to-all-start.1 = ((bf16[32,16,512]{2,1,0:T(8,128)(2,1)}), bf16[32,16,512]{2,1,0:T(8,128)(2,1)S(1)}, u32[]{:S(2)}, u32[]{:S(2)}) async-start(bf16[32,16,512]{2,1,0:T(8,128)(2,1)} %shard_map.85), calls=%async_computation.1 | async-start | bytes 1048576 | tf_op jit(solution)/shard_map/all_to_all | solution.py:312
  49.5 0.0 copy-start
  49.6 0.0 copy-start.2
  49.6 1.9 %shard_map.87 = (bf16[2,512,512]{2,1,0:T(8,128)(2,1)S(1)}, bf16[2,256,512]{2,1,0:T(8,128)(2,1)S(1)}, bf16[2,256,512]{2,1,0:T(8,128)(2,1)S(1)}, bf16[2,256,512]{2,1,0:T(8,128)(2,1)S(1)}) custom-call(bf16[512,4096]{1,0:T(8,128)(2,1)} %refs_0_.1), custom_call_target="tpu_custom_call" | custom-call | bytes 4194304 | tf_op jit(solution)/shard_map/pallas_call | solution.py:249
  51.5 0.0 copy-start.1
  51.5 2.8 %collective-permute-start.9 = (bf16[2,256,512]{2,1,0:T(8,128)(2,1)S(1)}, bf16[2,256,512]{2,1,0:T(8,128)(2,1)S(1)}, u32[]{:S(2)}, u32[]{:S(2)}) collective-permute-start(bf16[2,256,512]{2,1,0:T(8,128)(2,1)S(1)} %get-tuple-element.26), channel_id=1, source_target_pairs={{0,2},{1,3},{2,0},{3,1},{4,6},{5,7},{6,4},{7,5},{8,10},{9,11},{10,... | collective-permute-start | bytes 1572872 | tf_op jit(solution)/shard_map/ppermute | solution.py:307
  54.3 0.9 collective-permute-start.11
  55.2 0.6 collective-permute-start.7
  55.8 10.5 %collective-permute-done.9.refs_3_ = bf16[2,256,512]{2,1,0:T(8,128)(2,1)S(1)} collective-permute-done((bf16[2,256,512]{2,1,0:T(8,128)(2,1)S(1)}, bf16[2,256,512]{2,1,0:T(8,128)(2,1)S(1)}, u32[]{:S(2)}, u32[]{:S(2)}) %collective-permute-start.9) | collective-permute-done | bytes 524320 | tf_op jit(solution)/shard_map/ppermute | solution.py:307
  66.2 2.0 %collective-permute-start.10 = (bf16[2,256,512]{2,1,0:T(8,128)(2,1)S(1)}, bf16[2,256,512]{2,1,0:T(8,128)(2,1)}, u32[]{:S(2)}, u32[]{:S(2)}) collective-permute-start(bf16[2,256,512]{2,1,0:T(8,128)(2,1)S(1)} %collective-permute-done.9.refs_3_), channel_id=1, source_target_pairs={{0,8},{8,0},{1,9},{9,1},{2,10},{10,2},{3,11},{11,3},{4,12},{12,4},... | collective-permute-start | bytes 1572872 | tf_op jit(solution)/shard_map/ppermute | solution.py:308
  68.3 9.3 %collective-permute-done.11.refs_5_ = bf16[2,256,512]{2,1,0:T(8,128)(2,1)S(1)} collective-permute-done((bf16[2,256,512]{2,1,0:T(8,128)(2,1)S(1)}, bf16[2,256,512]{2,1,0:T(8,128)(2,1)S(1)}, u32[]{:S(2)}, u32[]{:S(2)}) %collective-permute-start.11) | collective-permute-done | bytes 524320 | tf_op jit(solution)/shard_map/ppermute | solution.py:307
  77.6 1.2 %collective-permute-start.12 = (bf16[2,256,512]{2,1,0:T(8,128)(2,1)S(1)}, bf16[2,256,512]{2,1,0:T(8,128)(2,1)}, u32[]{:S(2)}, u32[]{:S(2)}) collective-permute-start(bf16[2,256,512]{2,1,0:T(8,128)(2,1)S(1)} %collective-permute-done.11.refs_5_), channel_id=1, source_target_pairs={{0,8},{8,0},{1,9},{9,1},{2,10},{10,2},{3,11},{11,3},{4,12},{12,4},... | collective-permute-start | bytes 1572872 | tf_op jit(solution)/shard_map/ppermute | solution.py:308
  78.8 0.0 copy-done
  78.8 0.0 copy-done.2
  78.8 0.6 shard_map.82.query_ref
  79.4 0.0 collective-permute-done.7.refs_1_
  79.4 0.0 copy-done.1
  79.4 0.0 copy-start.10
  79.4 0.1 collective-permute-start.8
  79.5 0.0 all-to-all-done.1
  79.5 0.2 shard_map.86
  79.8 0.0 copy-done.8
  79.8 0.0 copy-done.9
  79.8 2.4 %collective-permute-start.5 = (bf16[256,512]{1,0:T(8,128)(2,1)S(1)}, bf16[256,512]{1,0:T(8,128)(2,1)S(1)}, u32[]{:S(2)}, u32[]{:S(2)}) collective-permute-start(bf16[256,512]{1,0:T(8,128)(2,1)S(1)} %get-tuple-element.22.refs_4_.refs_0_), channel_id=1, source_target_pairs={{0,3},{1,0},{2,1},{3,2},{4,7},{5,4},{6,5},{7,6},{8,11},{9,8},{10,9... | collective-permute-start | bytes 786440 | tf_op jit(solution)/shard_map/ppermute | solution.py:318
  82.2 0.0 collective-permute-start.1
  82.2 0.0 collective-permute-done.10.refs_4_
  82.2 0.2 collective-permute-start.4
  82.4 5.0 %collective-permute-done.5.refs_7_.refs_3_ = bf16[256,512]{1,0:T(8,128)(2,1)S(1)} collective-permute-done((bf16[256,512]{1,0:T(8,128)(2,1)S(1)}, bf16[256,512]{1,0:T(8,128)(2,1)S(1)}, u32[]{:S(2)}, u32[]{:S(2)}) %collective-permute-start.5) | collective-permute-done | bytes 262176 | tf_op jit(solution)/shard_map/ppermute | solution.py:318
  87.4 3.4 %collective-permute-start.6 = (bf16[256,512]{1,0:T(8,128)(2,1)S(1)}, bf16[256,512]{1,0:T(8,128)(2,1)S(1)}, u32[]{:S(2)}, u32[]{:S(2)}) collective-permute-start(bf16[256,512]{1,0:T(8,128)(2,1)S(1)} %collective-permute-done.5.refs_7_.refs_3_), channel_id=1, source_target_pairs={{0,3},{1,0},{2,1},{3,2},{4,7},{5,4},{6,5},{7,6},{8,11},{9,8},{10,9... | collective-permute-start | bytes 786440 | tf_op jit(solution)/shard_map/ppermute | solution.py:318
  90.8 0.0 collective-permute-done.12.refs_6_
  90.8 0.0 collective-permute-start.3
  90.8 0.0 collective-permute-done.1.refs_1_
  90.8 1.4 %collective-permute-start.2 = (bf16[256,512]{1,0:T(8,128)(2,1)S(1)}, bf16[256,512]{1,0:T(8,128)(2,1)S(1)}, u32[]{:S(2)}, u32[]{:S(2)}) collective-permute-start(bf16[256,512]{1,0:T(8,128)(2,1)S(1)} %collective-permute-done.1.refs_1_), channel_id=1, source_target_pairs={{0,1},{1,2},{2,3},{3,0},{4,5},{5,6},{6,7},{7,4},{8,9},{9,10},{10,1... | collective-permute-start | bytes 786440 | tf_op jit(solution)/shard_map/ppermute | solution.py:318
  92.3 0.0 collective-permute-done.8.refs_2_
  92.3 0.0 copy-done.10
  92.3 2.2 %shard_map.88 = (bf16[2,512,512]{2,1,0:T(8,128)(2,1)S(1)}, bf16[2,256,512]{2,1,0:T(8,128)(2,1)S(1)}, bf16[2,256,512]{2,1,0:T(8,128)(2,1)S(1)}, bf16[2,256,512]{2...) custom-call(bf16[2,512,512]{2,1,0:T(8,128)(2,1)} %copy-done.1, ...), custom_call_target="tpu_custom_call" | custom-call | bytes 4194304 | tf_op jit(solution)/shard_map/pallas_call | solution.py:249
  94.5 1.6 %collective-permute-done.4.refs_5_.refs_1_ = bf16[256,512]{1,0:T(8,128)(2,1)S(1)} collective-permute-done((bf16[256,512]{1,0:T(8,128)(2,1)S(1)}, bf16[256,512]{1,0:T(8,128)(2,1)S(1)}, u32[]{:S(2)}, u32[]{:S(2)}) %collective-permute-start.4) | collective-permute-done | bytes 262176 | tf_op jit(solution)/shard_map/ppermute | solution.py:318
  96.1 0.0 collective-permute-done.6.refs_6_.refs_2_
  96.1 0.9 shard_map.91
  97.0 3.0 %collective-permute-start.14 = (bf16[256,512]{1,0:T(8,128)(2,1)S(1)}, bf16[256,512]{1,0:T(8,128)(2,1)S(1)}, u32[]{:S(2)}, u32[]{:S(2)}) collective-permute-start(bf16[256,512]{1,0:T(8,128)(2,1)S(1)} %shard_map.91), channel_id=1, source_target_pairs={{0,4},{4,0},{1,5},{5,1},{2,6},{6,2},{3,7},{7,3},{8,12},{12,8},{9,1... | collective-permute-start | bytes 786440 | tf_op jit(solution)/shard_map/ppermute | solution.py:332
  100.0 0.7 collective-permute-done.3.refs_3_
  100.7 1.0 collective-permute-done.2.refs_2_
  101.8 0.9 shard_map.90
  102.7 3.0 %collective-permute-start.13 = (bf16[256,512]{1,0:T(8,128)(2,1)S(1)}, bf16[256,512]{1,0:T(8,128)(2,1)S(1)}, u32[]{:S(2)}, u32[]{:S(2)}) collective-permute-start(bf16[256,512]{1,0:T(8,128)(2,1)S(1)} %shard_map.90), channel_id=1, source_target_pairs={{0,4},{4,0},{1,5},{5,1},{2,6},{6,2},{3,7},{7,3},{8,12},{12,8},{9,1... | collective-permute-start | bytes 786440 | tf_op jit(solution)/shard_map/ppermute | solution.py:332
  105.7 1.8 %shard_map.89.own_ref = f32[512,512]{1,0:T(8,128)S(1)} custom-call(bf16[256,512]{1,0:T(8,128)(2,1)S(1)} %get-tuple-element.21.refs_0_, bf16[256,512]{1,0:T(8,128)(2,1)S(1)} %collective-permute-done.1.refs_1_, bf16[256,512]{1,0:T(8,128)(2,1)S(1)} %collective-permute-done.2.refs_2_, bf16[256,512]{1,0:T(8,128)(2,1)S(1)} %collective-permute-done.3.refs_3_, ...), custom_call_target="tpu_custom_call" | custom-call | flops 2000000000 | bytes 6291456 | tf_op jit(solution)/shard_map/pallas_call | solution.py:249
  107.4 0.0 collective-permute-done.14.second_ref
  107.4 4.3 %collective-permute-done.13.first_ref = bf16[256,512]{1,0:T(8,128)(2,1)S(1)} collective-permute-done((bf16[256,512]{1,0:T(8,128)(2,1)S(1)}, bf16[256,512]{1,0:T(8,128)(2,1)S(1)}, u32[]{:S(2)}, u32[]{:S(2)}) %collective-permute-start.13) | collective-permute-done | bytes 262176 | tf_op jit(solution)/shard_map/ppermute | solution.py:332
  111.8 0.9 shard_map.92
  (4 shorter events, 0.0 us)
Async XLA Ops:
  0.0 21.3 %copy-start.5 = (f32[2,128,128]{2,1,0:T(8,128)S(1)}, f32[2,128,128]{2,1,0:T(8,128)}, u32[]{:S(2)}) copy-start(f32[2,128,128]{2,1,0:T(8,128)} %constant.11.clone.twist_ref.refs_1_) | copy-start | bytes 393220
  0.0 21.3 %copy-start.6 = (bf16[2,256,128]{2,1,0:T(8,128)(2,1)S(1)}, bf16[2,256,128]{2,1,0:T(8,128)(2,1)}, u32[]{:S(2)}) copy-start(bf16[2,256,128]{2,1,0:T(8,128)(2,1)} %constant.8.clone.fwd1_ref.refs_0_) | copy-start | bytes 393220
  0.0 21.3 %copy-start.4 = (bf16[2,256,256]{2,1,0:T(8,128)(2,1)S(1)}, bf16[2,256,256]{2,1,0:T(8,128)(2,1)}, u32[]{:S(2)}) copy-start(bf16[2,256,256]{2,1,0:T(8,128)(2,1)} %constant.9.clone.fwd2_ref.refs_2_) | copy-start | bytes 786436
  0.0 21.3 %copy-start.3 = (f32[16384,16]{0,1:T(8,128)S(1)}, f32[16384,16]{0,1:T(8,128)}, u32[]{:S(2)}) copy-start(f32[16384,16]{0,1:T(8,128)} %param.10) | copy-start | bytes 3145732
  0.9 5.5 %collective-permute-start = (bf16[3,8,512]{2,1,0:T(8,128)(2,1)S(1)}, bf16[3,8,512]{2,1,0:T(8,128)(2,1)S(1)}, u32[]{:S(2)}, u32[]{:S(2)}) collective-permute-start(bf16[3,8,512]{2,1,0:T(8,128)(2,1)S(1)} %slice.4), channel_id=1, source_target_pairs={{0,8},{8,16},{16,24},{24,32},{32,40},{40,48},{48,56},{56,64},{64,7... | collective-permute-start | bytes 73736 | tf_op jit(solution)/shard_map/ppermute | solution.py:288
  9.4 28.4 %all-to-all-start = ((bf16[32,16,512]{2,1,0:T(8,128)(2,1)}), bf16[32,16,512]{2,1,0:T(8,128)(2,1)S(1)}, u32[]{:S(2)}, u32[]{:S(2)}) async-start(bf16[32,16,512]{2,1,0:T(8,128)(2,1)} %bitcast.1), calls=%async_computation | async-start | bytes 1048576 | tf_op jit(solution)/shard_map/all_to_all | solution.py:296
  23.5 1.4 %copy-start.7 = (f32[16,128,256]{2,1,0:T(8,128)}, f32[16,128,256]{2,1,0:T(8,128)S(1)}, u32[]{:S(2)}) copy-start(f32[16,128,256]{2,1,0:T(8,128)S(1)} %shard_map.84.refs_3_) | copy-start | bytes 6291460
  44.7 34.9 %all-to-all-start.1 = ((bf16[32,16,512]{2,1,0:T(8,128)(2,1)}), bf16[32,16,512]{2,1,0:T(8,128)(2,1)S(1)}, u32[]{:S(2)}, u32[]{:S(2)}) async-start(bf16[32,16,512]{2,1,0:T(8,128)(2,1)} %shard_map.85), calls=%async_computation.1 | async-start | bytes 1048576 | tf_op jit(solution)/shard_map/all_to_all | solution.py:312
  49.5 29.2 %copy-start = (bf16[512,3,512]{2,0,1:T(8,128)(2,1)S(1)}, bf16[512,3,512]{2,0,1:T(8,128)(2,1)}, u32[]{:S(2)}) copy-start(bf16[512,3,512]{2,0,1:T(8,128)(2,1)} %param.8) | copy-start | bytes 4718596
  49.6 29.2 %copy-start.2 = (f32[3,3,512]{2,1,0:T(4,128)S(1)}, f32[3,3,512]{2,1,0:T(4,128)}, u32[]{:S(2)}) copy-start(f32[3,3,512]{2,1,0:T(4,128)} %taps_hbm.1) | copy-start | bytes 55300
  51.5 28.0 %copy-start.1 = (bf16[2,512,512]{2,1,0:T(8,128)(2,1)}, bf16[2,512,512]{2,1,0:T(8,128)(2,1)S(1)}, u32[]{:S(2)}) copy-start(bf16[2,512,512]{2,1,0:T(8,128)(2,1)S(1)} %get-tuple-element.24.refs_0_) | copy-start | bytes 3145732
  51.5 14.8 %collective-permute-start.9 = (bf16[2,256,512]{2,1,0:T(8,128)(2,1)S(1)}, bf16[2,256,512]{2,1,0:T(8,128)(2,1)S(1)}, u32[]{:S(2)}, u32[]{:S(2)}) collective-permute-start(bf16[2,256,512]{2,1,0:T(8,128)(2,1)S(1)} %get-tuple-element.26), channel_id=1, source_target_pairs={{0,2},{1,3},{2,0},{3,1},{4,6},{5,7},{6,4},{7,5},{8,10},{9,11},{10,... | collective-permute-start | bytes 1572872 | tf_op jit(solution)/shard_map/ppermute | solution.py:307
  54.3 23.3 %collective-permute-start.11 = (bf16[2,256,512]{2,1,0:T(8,128)(2,1)S(1)}, bf16[2,256,512]{2,1,0:T(8,128)(2,1)S(1)}, u32[]{:S(2)}, u32[]{:S(2)}) collective-permute-start(bf16[2,256,512]{2,1,0:T(8,128)(2,1)S(1)} %get-tuple-element.27), channel_id=1, source_target_pairs={{0,3},{1,0},{2,1},{3,2},{4,7},{5,4},{6,5},{7,6},{8,11},{9,8},{10,9... | collective-permute-start | bytes 1572872 | tf_op jit(solution)/shard_map/ppermute | solution.py:307
  55.2 24.2 %collective-permute-start.7 = (bf16[2,256,512]{2,1,0:T(8,128)(2,1)S(1)}, bf16[2,256,512]{2,1,0:T(8,128)(2,1)S(1)}, u32[]{:S(2)}, u32[]{:S(2)}) collective-permute-start(bf16[2,256,512]{2,1,0:T(8,128)(2,1)S(1)} %get-tuple-element.25), channel_id=1, source_target_pairs={{0,1},{1,2},{2,3},{3,0},{4,5},{5,6},{6,7},{7,4},{8,9},{9,10},{10,1... | collective-permute-start | bytes 1572872 | tf_op jit(solution)/shard_map/ppermute | solution.py:307
  66.2 13.5 %copy-start.8 = (bf16[2,256,512]{2,1,0:T(8,128)(2,1)}, bf16[2,256,512]{2,1,0:T(8,128)(2,1)S(1)}, u32[]{:S(2)}) copy-start(bf16[2,256,512]{2,1,0:T(8,128)(2,1)S(1)} %collective-permute-done.9.refs_3_) | copy-start | bytes 1572868
  66.2 16.0 %collective-permute-start.10 = (bf16[2,256,512]{2,1,0:T(8,128)(2,1)S(1)}, bf16[2,256,512]{2,1,0:T(8,128)(2,1)}, u32[]{:S(2)}, u32[]{:S(2)}) collective-permute-start(bf16[2,256,512]{2,1,0:T(8,128)(2,1)S(1)} %collective-permute-done.9.refs_3_), channel_id=1, source_target_pairs={{0,8},{8,0},{1,9},{9,1},{2,10},{10,2},{3,11},{11,3},{4,12},{12,4},... | collective-permute-start | bytes 1572872 | tf_op jit(solution)/shard_map/ppermute | solution.py:308
  77.6 2.2 %copy-start.9 = (bf16[2,256,512]{2,1,0:T(8,128)(2,1)}, bf16[2,256,512]{2,1,0:T(8,128)(2,1)S(1)}, u32[]{:S(2)}) copy-start(bf16[2,256,512]{2,1,0:T(8,128)(2,1)S(1)} %collective-permute-done.11.refs_5_) | copy-start | bytes 1572868
  77.6 13.2 %collective-permute-start.12 = (bf16[2,256,512]{2,1,0:T(8,128)(2,1)S(1)}, bf16[2,256,512]{2,1,0:T(8,128)(2,1)}, u32[]{:S(2)}, u32[]{:S(2)}) collective-permute-start(bf16[2,256,512]{2,1,0:T(8,128)(2,1)S(1)} %collective-permute-done.11.refs_5_), channel_id=1, source_target_pairs={{0,8},{8,0},{1,9},{9,1},{2,10},{10,2},{3,11},{11,3},{4,12},{12,4},... | collective-permute-start | bytes 1572872 | tf_op jit(solution)/shard_map/ppermute | solution.py:308
  79.4 12.9 %copy-start.10 = (bf16[2,256,512]{2,1,0:T(8,128)(2,1)}, bf16[2,256,512]{2,1,0:T(8,128)(2,1)S(1)}, u32[]{:S(2)}) copy-start(bf16[2,256,512]{2,1,0:T(8,128)(2,1)S(1)} %collective-permute-done.7.refs_1_) | copy-start | bytes 1572868
  79.4 12.8 %collective-permute-start.8 = (bf16[2,256,512]{2,1,0:T(8,128)(2,1)S(1)}, bf16[2,256,512]{2,1,0:T(8,128)(2,1)}, u32[]{:S(2)}, u32[]{:S(2)}) collective-permute-start(bf16[2,256,512]{2,1,0:T(8,128)(2,1)S(1)} %collective-permute-done.7.refs_1_), channel_id=1, source_target_pairs={{0,8},{8,0},{1,9},{9,1},{2,10},{10,2},{3,11},{11,3},{4,12},{12,4},... | collective-permute-start | bytes 1572872 | tf_op jit(solution)/shard_map/ppermute | solution.py:308
  79.8 7.6 %collective-permute-start.5 = (bf16[256,512]{1,0:T(8,128)(2,1)S(1)}, bf16[256,512]{1,0:T(8,128)(2,1)S(1)}, u32[]{:S(2)}, u32[]{:S(2)}) collective-permute-start(bf16[256,512]{1,0:T(8,128)(2,1)S(1)} %get-tuple-element.22.refs_4_.refs_0_), channel_id=1, source_target_pairs={{0,3},{1,0},{2,1},{3,2},{4,7},{5,4},{6,5},{7,6},{8,11},{9,8},{10,9... | collective-permute-start | bytes 786440 | tf_op jit(solution)/shard_map/ppermute | solution.py:318
  82.2 8.6 %collective-permute-start.1 = (bf16[256,512]{1,0:T(8,128)(2,1)S(1)}, bf16[256,512]{1,0:T(8,128)(2,1)S(1)}, u32[]{:S(2)}, u32[]{:S(2)}) collective-permute-start(bf16[256,512]{1,0:T(8,128)(2,1)S(1)} %get-tuple-element.21.refs_0_), channel_id=1, source_target_pairs={{0,1},{1,2},{2,3},{3,0},{4,5},{5,6},{6,7},{7,4},{8,9},{9,10},{10,1... | collective-permute-start | bytes 786440 | tf_op jit(solution)/shard_map/ppermute | solution.py:318
  82.2 13.9 %collective-permute-start.4 = (bf16[256,512]{1,0:T(8,128)(2,1)S(1)}, bf16[256,512]{1,0:T(8,128)(2,1)S(1)}, u32[]{:S(2)}, u32[]{:S(2)}) collective-permute-start(bf16[256,512]{1,0:T(8,128)(2,1)S(1)} %get-tuple-element.22.refs_4_.refs_0_), channel_id=1, source_target_pairs={{0,1},{1,2},{2,3},{3,0},{4,5},{5,6},{6,7},{7,4},{8,9},{9,10},{10,1... | collective-permute-start | bytes 786440 | tf_op jit(solution)/shard_map/ppermute | solution.py:318
  87.4 8.8 %collective-permute-start.6 = (bf16[256,512]{1,0:T(8,128)(2,1)S(1)}, bf16[256,512]{1,0:T(8,128)(2,1)S(1)}, u32[]{:S(2)}, u32[]{:S(2)}) collective-permute-start(bf16[256,512]{1,0:T(8,128)(2,1)S(1)} %collective-permute-done.5.refs_7_.refs_3_), channel_id=1, source_target_pairs={{0,3},{1,0},{2,1},{3,2},{4,7},{5,4},{6,5},{7,6},{8,11},{9,8},{10,9... | collective-permute-start | bytes 786440 | tf_op jit(solution)/shard_map/ppermute | solution.py:318
  90.8 9.9 %collective-permute-start.3 = (bf16[256,512]{1,0:T(8,128)(2,1)S(1)}, bf16[256,512]{1,0:T(8,128)(2,1)S(1)}, u32[]{:S(2)}, u32[]{:S(2)}) collective-permute-start(bf16[256,512]{1,0:T(8,128)(2,1)S(1)} %get-tuple-element.21.refs_0_), channel_id=1, source_target_pairs={{0,3},{1,0},{2,1},{3,2},{4,7},{5,4},{6,5},{7,6},{8,11},{9,8},{10,9... | collective-permute-start | bytes 786440 | tf_op jit(solution)/shard_map/ppermute | solution.py:318
  90.8 10.9 %collective-permute-start.2 = (bf16[256,512]{1,0:T(8,128)(2,1)S(1)}, bf16[256,512]{1,0:T(8,128)(2,1)S(1)}, u32[]{:S(2)}, u32[]{:S(2)}) collective-permute-start(bf16[256,512]{1,0:T(8,128)(2,1)S(1)} %collective-permute-done.1.refs_1_), channel_id=1, source_target_pairs={{0,1},{1,2},{2,3},{3,0},{4,5},{5,6},{6,7},{7,4},{8,9},{9,10},{10,1... | collective-permute-start | bytes 786440 | tf_op jit(solution)/shard_map/ppermute | solution.py:318
  97.0 10.4 %collective-permute-start.14 = (bf16[256,512]{1,0:T(8,128)(2,1)S(1)}, bf16[256,512]{1,0:T(8,128)(2,1)S(1)}, u32[]{:S(2)}, u32[]{:S(2)}) collective-permute-start(bf16[256,512]{1,0:T(8,128)(2,1)S(1)} %shard_map.91), channel_id=1, source_target_pairs={{0,4},{4,0},{1,5},{5,1},{2,6},{6,2},{3,7},{7,3},{8,12},{12,8},{9,1... | collective-permute-start | bytes 786440 | tf_op jit(solution)/shard_map/ppermute | solution.py:332
  102.7 9.1 %collective-permute-start.13 = (bf16[256,512]{1,0:T(8,128)(2,1)S(1)}, bf16[256,512]{1,0:T(8,128)(2,1)S(1)}, u32[]{:S(2)}, u32[]{:S(2)}) collective-permute-start(bf16[256,512]{1,0:T(8,128)(2,1)S(1)} %shard_map.90), channel_id=1, source_target_pairs={{0,4},{4,0},{1,5},{5,1},{2,6},{6,2},{3,7},{7,3},{8,12},{12,8},{9,1... | collective-permute-start | bytes 786440 | tf_op jit(solution)/shard_map/ppermute | solution.py:332

commit v4 on v3

--- a/solution.py
+++ b/solution.py
@@ -31,7 +31,7 @@
     fwd2 = np.block([[c2, s2], [-s2, c2]])
     inv2 = np.concatenate([c1.T, s1.T], 1) / LENGTH
     twist = np.stack([np.cos(turn), np.sin(turn)]).astype(np.float32)
-    return halves(fwd1), halves(fwd2), halves(inv2), twist
+    return np.concatenate(halves(fwd1), 1), halves(fwd2), halves(inv2), twist
 
 
 def split(x):
@@ -68,7 +68,9 @@
         rows[n * channels : (n + 1) * channels, :] = h_ref[:, n * SIDE : (n + 1) * SIDE]
 
     group = jnp.concatenate([rows[pl.ds(w, SIDE, stride=channels), :] for w in range(channels)], 1)
-    spectra = right3(stacked(left3(fwd1_ref, group), twist_ref), fwd2_ref)
+    high, low = split(group)
+    first = mm(fwd1_ref[...], jnp.concatenate([high, high], 0)) + mm(fwd1_ref[:, :SIDE], low)
+    spectra = right3(stacked(first, twist_ref), fwd2_ref)
     for w in range(channels):
         out_ref[w] = spectra[w * SIDE : (w + 1) * SIDE]
 
@@ -94,7 +96,7 @@
     group = jnp.concatenate([rows[pl.ds(w, SIDE, stride=channels), :] for w in range(channels)], 1).astype(bf16)
     for c in copies[:3]:
         c.wait()
-    first = mm(fwd1_ref[0], group) + mm(fwd1_ref[1], group)
+    first = mm(fwd1_ref[...], jnp.concatenate([group, group], 0))
     spectra = right3(stacked(first, twist_ref), fwd2_ref)
     for c in copies[3:]:
         c.wait()
@@ -125,23 +127,37 @@
         c.wait()
 
 
-def featured(x, edge_ref, taps_ref, ext, s):
+def featured(x, edge_ref, taps_ref, ext, s, cut=slice(None)):
     tokens = x.shape[0]
-    ext[EDGE : EDGE + tokens, :] = x.astype(f32)
-    ext[:EDGE, :] = edge_ref[s].astype(f32)
-    total = taps_ref[s, 0:1, :] * ext[EDGE : EDGE + tokens, :]
+    ext[EDGE : EDGE + tokens, cut] = x.astype(f32)
+    ext[:EDGE, cut] = edge_ref[s, :, cut].astype(f32)
+    total = taps_ref[s, 0:1, cut] * ext[EDGE : EDGE + tokens, cut]
     for j in range(1, taps_ref.shape[1]):
-        total = total + taps_ref[s, j : j + 1, :] * ext[EDGE - j : EDGE - j + tokens, :]
+        total = total + taps_ref[s, j : j + 1, cut] * ext[EDGE - j : EDGE - j + tokens, cut]
     return total
 
 
-def gate_in_kernel(edge_ref, x_hbm, taps_hbm, out_ref, ext, keys, values, taps, sem):
-    copies = fetch((taps_hbm, x_hbm.at[1], x_hbm.at[2]), (taps, keys, values), sem)
+def gate_in_kernel(edge_ref, x_hbm, taps_hbm, out_hbm, ext, keys, values, taps, out_ref, sem, out_sem):
+    parts = 4
+    size = keys.shape[1] // parts
+    cuts = [slice(p * size, (p + 1) * size) for p in range(parts)]
+    sources, targets = [taps_hbm], [taps]
+    for cut in cuts:
+        sources += [x_hbm.at[1, :, cut], x_hbm.at[2, :, cut]]
+        targets += [keys.at[:, cut], values.at[:, cut]]
+    copies = fetch(sources, targets, sem)
     copies[0].wait()
-    copies[1].wait()
-    key = featured(keys[...], edge_ref, taps, ext, 1)
-    copies[2].wait()
-    out_ref[...] = (key * featured(values[...], edge_ref, taps, ext, 2)).T.astype(bf16)
+    outs = []
+    for p, cut in enumerate(cuts):
+        copies[1 + 2 * p].wait()
+        copies[2 + 2 * p].wait()
+        key = featured(keys[:, cut], edge_ref, taps, ext, 1, cut)
+        product = key * featured(values[:, cut], edge_ref, taps, ext, 2, cut)
+        out_ref[cut, :] = product.T.astype(bf16)
+        outs.append(pltpu.make_async_copy(out_ref.at[cut], out_hbm.at[cut], out_sem.at[p]))
+        outs[-1].start()
+    for c in outs:
+        c.wait()
 
 
 def query_kernel(x_ref, edge_ref, taps_ref, out_ref, ext):
@@ -161,71 +177,77 @@
     return pl.ds(pl.multiple_of(block * cols, cols), cols)
 
 
-def columns_kernel(nx, ny, weight_ref, *rest):
-    outs, sem = rest[:nx], rest[nx]
-    cols = outs[0].shape[2]
+def columns_kernel(nx, ny, weight_ref, *refs):
+    along_x, along_y, sem = refs[: nx - 1], refs[nx - 1], refs[nx]
+    cols = along_y.shape[2]
     half = weight_ref.shape[0] // 2
-    first = pl.multiple_of(lax.axis_index("core") * half, half)
-    sources = []
+    rows = pl.ds(pl.multiple_of(lax.axis_index("core") * half, half), half)
+    sources, targets = [], []
+    for s in range(1, nx):
+        for o in range(ny):
+            sources.append(weight_ref.at[rows, block_columns(nx, ny, s, o, cols)])
+            targets.append(along_x[s - 1].at[o])
     for s in range(nx):
-        for o in range(ny):
-            at = block_columns(nx, ny, s, o, cols)
-            sources.append(weight_ref.at[pl.ds(first, half), at] if s else weight_ref.at[:, at])
-    for c in fetch(sources, [out.at[o] for out in outs for o in range(ny)], sem):
-        c.wait()
-
-
-def stage_kernel(*refs):
-    count = len(refs) // 2
-    for c in fetch(refs[:count], refs[count : 2 * count], refs[2 * count]):
-        c.wait()
-
-
-def project_rows(other, at, pieces, weights):
-    width = pieces[0].shape[1]
+        sources.append(weight_ref.at[rows, block_columns(nx, ny, s, 1, cols)])
+        targets.append(along_y.at[s])
+    for c in fetch(sources, targets, sem):
+        c.wait()
+
+
+def stage_kernel(nx, ny, blocks, weight_ref, *refs):
+    count = (len(refs) - 2) // 2
+    came, own_ref, outs, sem = refs[:count], refs[count], refs[count + 1 : -1], refs[-1]
+    cols = own_ref.shape[2]
+    sources = [weight_ref.at[:, block_columns(nx, ny, s, o, cols)] for s, o in blocks]
+    targets = [own_ref.at[i] for i in range(len(blocks))]
+    for c in fetch(sources + list(came), targets + list(outs), sem):
+        c.wait()
+
+
+def core_halves(width):
     half = width // 2
     core = lax.axis_index("core")
-    mine = pl.ds(pl.multiple_of(core * half, half), half)
-    rest = pl.ds(pl.multiple_of((1 - core) * half, half), half)
-    total = mm(pieces[0][at, :], weights[0][other])
+    return [pl.ds(pl.multiple_of(c * half, half), half) for c in (core, 1 - core)]
+
+
+def sums_over_x(other, pieces, weights):
+    mine, rest = core_halves(pieces[0].shape[1])
+    total = mm(pieces[0][...], weights[0][other])
     for s, piece in enumerate(pieces[1:]):
-        total = total + mm(piece[at, mine], weights[1 + 2 * s][other])
-        total = total + mm(piece[at, rest], weights[2 + 2 * s][other])
+        total = total + mm(piece[:, mine], weights[1 + 2 * s][other])
+        total = total + mm(piece[:, rest], weights[2 + 2 * s][other])
     return total
 
 
-def project_other_kernel(*refs):
-    pieces, weights, out_ref = refs[:4], refs[4:11], refs[11]
-    step = 128
-
-    def rows(r, carry):
-        at = pl.ds(pl.multiple_of(r * step, step), step)
-        out_ref[at, :] = project_rows(1, at, pieces, weights).astype(out_ref.dtype)
-        return carry
-
-    lax.fori_loop(0, out_ref.shape[0] // step, rows, 0)
-
-
-def project_own_kernel(*refs):
-    pieces, weights, out_ref = refs[:8], refs[8:15], refs[15]
-    step = 128
-    tokens = pieces[0].shape[0]
-    for part in range(2):
-
-        def rows(r, carry):
-            start = pl.multiple_of(r * step, step)
-            sums = project_rows(0, pl.ds(start, step), pieces[4 * part : 4 * part + 4], weights)
-            out_ref[pl.ds(part * tokens + start, step), :] = sums
-            return carry
-
-        lax.fori_loop(0, tokens // step, rows, 0)
-
-
-def finish_kernel(own_ref, first_ref, second_ref, out_ref):
-    tokens = first_ref.shape[0]
-    for part, came in enumerate((first_ref, second_ref)):
-        at = slice(part * tokens, (part + 1) * tokens)
-        out_ref[at, :] = (own_ref[at, :] + came[...].astype(f32)).astype(out_ref.dtype)
+def sums_over_y(shift, pieces, weights):
+    mine, rest = core_halves(pieces[0].shape[1])
+    total = mm(pieces[0][...], weights[0][shift])
+    return total + (mm(pieces[1][:, mine], weights[1][shift]) + mm(pieces[1][:, rest], weights[2][shift]))
+
+
+def along_x_kernel(*refs):
+    pieces, weights, outs = refs[:2], refs[2:5], refs[5:]
+    for s, out_ref in enumerate(outs):
+        out_ref[...] = sums_over_y(s + 1, pieces, weights).astype(out_ref.dtype)
+
+
+def along_y_kernel(*refs):
+    refs[11][...] = sums_over_x(1, refs[:4], refs[4:11]).astype(refs[11].dtype)
+
+
+def own_kernel(*refs):
+    refs[16][...] = sums_over_x(0, refs[:4], refs[4:11])
+    refs[17][...] = sums_over_y(0, refs[11:13], refs[13:16])
+
+
+def finish_kernel(upper_ref, lower_ref, *refs):
+    along_y, along_x, out_ref = refs[0], refs[1:-1], refs[-1]
+    half = upper_ref.shape[0]
+    out_ref[:half, :] = (upper_ref[...] + along_y[...].astype(f32)).astype(out_ref.dtype)
+    total = lower_ref[...]
+    for came in along_x:
+        total = total + came[...].astype(f32)
+    out_ref[half:, :] = total.astype(out_ref.dtype)
 
 
 def ring(axis, shift):
@@ -289,8 +311,10 @@
     ext = [pltpu.VMEM((tokens + EDGE, width), f32)]
     gated_in = call(
         gate_in_kernel, [((width, tokens), bf16)],
-        ext + held(streams_first[1], streams_first[2], short_filter), 0,
-        edge, streams_first, short_filter, specs=[VM, HBM, HBM],
+        ext
+        + held(streams_first[1], streams_first[2], short_filter)[:-1]
+        + [pltpu.VMEM((width, tokens), bf16), pltpu.SemaphoreType.DMA((9,)), pltpu.SemaphoreType.DMA((4,))],
+        0, edge, streams_first, short_filter, specs=[VM, HBM, HBM], outs_at=HBM,
     )
     gated_in, out_weight = lax.optimization_barrier((gated_in, out_weight))
     signal = lax.all_to_all(gated_in.reshape(ctx, mine, tokens), CTX, 0, 0)
@@ -298,14 +322,20 @@
     def columns(*refs):
         columns_kernel(nx, ny, *refs)
 
-    blocks = call(
-        columns, [((ny, width if s == 0 else width // 2, cols), bf16) for s in range(nx)],
-        [pltpu.SemaphoreType.DMA((ny * nx,))], 0, out_weight, specs=[HBM],
+    *along_x, along_y = call(
+        columns,
+        [((ny, width // 2, cols), bf16)] * (nx - 1) + [((nx, width // 2, cols), bf16)],
+        [pltpu.SemaphoreType.DMA((ny * (nx - 1) + nx,))], 0, out_weight, specs=[HBM],
     )
-    weights = [blocks[0]]
+
+    def swapped(block, axis, route):
+        came = lax.ppermute(block, axis, route)
+        return [came, lax.ppermute(came, "core", ring("core", 1))]
+
+    across = ny * lax.axis_size("yl")
+    for_upper, for_lower = [], swapped(along_y, ("yl", "yh"), [(i, across - 1 - i) for i in range(across)])
     for s in range(1, nx):
-        came = lax.ppermute(blocks[s], "x", ring("x", s))
-        weights += [came, lax.ppermute(came, "core", ring("core", 1))]
+        for_upper += swapped(along_x[s - 1], "x", ring("x", s))
 
     spectrum = transform(long_filter, fwd1, fwd2, twist)
     convolved = convolve(signal, spectrum, fwd1, fwd2, inv2, twist)
@@ -314,24 +344,27 @@
     half = tokens // 2
     upper, lower = call(gate_out_kernel, [((half, width), bf16)] * 2, [], 0, query, returned)
 
-    def send(block, shift):
-        return lax.ppermute(block, "x", ring("x", shift))
-
-    left_upper, right_lower = send(upper, 1), send(lower, -1)
-    right_upper, left_lower = send(upper, -1), send(lower, 1)
-    far_upper, far_lower = send(left_upper, 1), send(right_lower, -1)
-    pieces = [(upper, left_upper, far_upper, right_upper), (lower, left_lower, far_lower, right_lower)]
-
-    weights = call(
-        stage_kernel, [(w.shape, bf16) for w in weights], [pltpu.SemaphoreType.DMA((len(weights),))], 0,
-        *weights, specs=[HBM] * len(weights),
-    )
-    theirs = []
-    for part in range(2):
-        sums = call(project_other_kernel, [((half, cols), bf16)], [], 10**9, *pieces[part], *weights)
-        theirs.append(lax.ppermute(sums, "yh", ring("yh", 1)))
-    own = call(project_own_kernel, [((tokens, cols), f32)], [], 2 * 10**9, *pieces[0], *pieces[1], *weights)
-    return call(finish_kernel, [((tokens, cols), bf16)], [], 0, own, *theirs)
+    def send(block, axis, shift):
+        return lax.ppermute(block, axis, ring(axis, shift))
+
+    def stage(blocks, came):
+        def kernel(*refs):
+            stage_kernel(nx, ny, blocks, *refs)
+
+        shapes = [((len(blocks), width, cols), bf16)] + [(c.shape, bf16) for c in came]
+        sems = [pltpu.SemaphoreType.DMA((len(blocks) + len(came),))]
+        return call(kernel, shapes, sems, 0, out_weight, *came, specs=[HBM] * (1 + len(came)))
+
+    lower_pieces = [lower, send(lower, "yh", 1)]
+    upper_pieces = [upper] + [send(upper, "x", s) for s in range(1, nx)]
+    for_lower = stage([(s, 0) for s in range(nx)], for_lower)
+    sums = call(along_x_kernel, [((half, cols), bf16)] * (nx - 1), [], 10**9, *lower_pieces, *for_lower)
+    summed_x = [send(sums[s - 1], "x", s) for s in range(1, nx)]
+    for_upper = stage([(0, 0), (0, 1)], for_upper)
+    sums = call(along_y_kernel, [((half, cols), bf16)], [], 10**9, *upper_pieces, *for_upper)
+    summed_y = send(sums, "yh", 1)
+    own = call(own_kernel, [((half, cols), f32)] * 2, [], 10**9, *upper_pieces, *for_upper, *lower_pieces, *for_lower)
+    return call(finish_kernel, [((tokens, cols), bf16)], [], 0, *own, summed_y, *summed_x)
 
 
 def solution(mesh):

time: 115 us -> 103 us (0.90); the launches traced: 113 us -> 102 us
  waiting for transfers between devices: 46.3 us -> 26.4 us
  starting transfers between devices: 42.5 us -> 49 us
  Pallas kernels: 21.4 us -> 23.6 us
    ppermute x14 -> x16, waiting for transfers between devices: 32.4 us -> 21.7 us  [the longest x8 12.5 us: send(): return lax.ppermute(block, axis, ring(axis, shift))]
    all_to_all x1, waiting for transfers between devices: 12.9 us -> 2.4 us  [body(): signal = lax.all_to_all(gated_in.reshape(ctx, mine, tokens), CTX, 0, 0)]
    ppermute x14 -> x16, starting transfers between devices: 21.1 us -> 27 us  [the longest x8 14.8 us: send(): return lax.ppermute(block, axis, ring(axis, shift))]
    pallas_call x11 -> x12, Pallas kernels: 21.4 us -> 23.6 us  [call(): pl.pallas_call(kernel, out_shape=shapes, in_specs=specs, out_specs=[outs_...]
    all_to_all x1, waiting for transfers between devices: 0.01 us -> 1.39 us  [body(): returned = lax.all_to_all(convolved, CTX, 0, 0).reshape(width, tokens)]
  transfers between devices with their start and end apart: 17 -> 19, of which waited for: 9 -> 10; matrix products, arithmetic and copies ran while one was open for 0% -> 0% of each run, Pallas kernels for 9% -> 19%
where the time goes in v4:
time: 103 us; the launch traced here: 102 us
  starting transfers between devices  49 us (48%)
  waiting for transfers between devices  26.4 us (26%)
  Pallas kernels  23.6 us (23%)
  local copies, waits for them, and re-layouts  2.92 us (3%)
    pallas_call x12, Pallas kernels, call(): pl.pallas_call(kernel, out_shape=shapes, in_specs=specs, out_specs=[outs_...  23.6 us
    ppermute x8, starting transfers between devices, send(): return lax.ppermute(block, axis, ring(axis, shift))  14.8 us
    ppermute x8, waiting for transfers between devices, send(): return lax.ppermute(block, axis, ring(axis, shift))  12.5 us
    all_to_all x1, starting transfers between devices, body(): signal = lax.all_to_all(gated_in.reshape(ctx, mine, tokens), CTX, 0, 0)  11.9 us
    ppermute x4, waiting for transfers between devices, swapped(): came = lax.ppermute(block, axis, route)  9.14 us
    ppermute x4, starting transfers between devices, swapped(): came = lax.ppermute(block, axis, route)  8.6 us
    all_to_all x1, starting transfers between devices, body(): returned = lax.all_to_all(convolved, CTX, 0, 0).reshape(width, tokens)  5.62 us
    ppermute x1, starting transfers between devices, body(): lax.ppermute(streams_first[:, tokens - EDGE:, :], CTX, [(i, i + 1) for i...  4.57 us
  transfers between devices with their start and end apart: 19, of which 10 were waited for; matrix products, arithmetic and copies ran while one was open for 0% of the time, Pallas kernels for 19%

profile of v4, /device:TPU:1, one launch (start us, length us, event | category | flops | bytes accessed | tf_op | source)
XLA Modules:
  0.0 102.1 jit_solution(17947546357437919210)
XLA Ops:
  0.0 0.7 slice.4
  0.7 4.6 %collective-permute-start = (bf16[3,8,512]{2,1,0:T(8,128)(2,1)S(1)}, bf16[3,8,512]{2,1,0:T(8,128)(2,1)S(1)}, u32[]{:S(2)}, u32[]{:S(2)}) collective-permute-start(bf16[3,8,512]{2,1,0:T(8,128)(2,1)S(1)} %slice.4), channel_id=1, source_target_pairs={{0,8},{8,16},{16,24},{24,32},{32,40},{40,48},{48,56},{56,64},{64,7... | collective-permute-start | bytes 73736 | tf_op jit(solution)/shard_map/ppermute | solution.py:310
  5.3 0.9 collective-permute-done.edge_ref
  6.2 3.0 %shard_map.83 = bf16[512,512]{1,0:T(8,128)(2,1)} custom-call(bf16[3,8,512]{2,1,0:T(8,128)(2,1)S(1)} %collective-permute-done.edge_ref, bf16[3,512,512]{2,1,0:T(8,128)(2,1)} %bitcast.5, f32[3,3,512]{2,1,0:T(4,128)} %taps_hbm.1), custom_call_target="tpu_custom_call" | custom-call | bytes 1615872 | tf_op jit(solution)/shard_map/pallas_call | solution.py:271
  9.2 11.9 %all-to-all-start = ((bf16[32,16,512]{2,1,0:T(8,128)(2,1)}), bf16[32,16,512]{2,1,0:T(8,128)(2,1)S(1)}, u32[]{:S(2)}, u32[]{:S(2)}) async-start(bf16[32,16,512]{2,1,0:T(8,128)(2,1)} %bitcast.1), calls=%async_computation | async-start | bytes 1048576 | tf_op jit(solution)/shard_map/all_to_all | solution.py:320
  21.1 0.0 copy-start.2
  21.1 0.0 copy-start.5
  21.1 0.0 copy-start.6
  21.1 0.0 copy-start.7
  21.1 3.2 %shard_map.87 = (bf16[2,256,512]{2,1,0:T(8,128)(2,1)}, bf16[2,256,512]{2,1,0:T(8,128)(2,1)}, bf16[2,256,512]{2,1,0:T(8,128)(2,1)S(1)}, bf16[4,256,512]{2,1,0:T(8,128)(2,1)}) custom-call(bf16[512,4096]{1,0:T(8,128)(2,1)} %refs_0_.3), custom_call_target="tpu_custom_call" | custom-call | bytes 4194304 | tf_op jit(solution)/shard_map/pallas_call | solution.py:271
  24.4 0.0 copy-start.3
  24.4 0.8 copy-done.3
  25.2 3.1 %collective-permute-start.11 = (bf16[4,256,512]{2,1,0:T(8,128)(2,1)}, bf16[4,256,512]{2,1,0:T(8,128)(2,1)}, u32[]{:S(2)}, u32[]{:S(2)}) collective-permute-start(bf16[4,256,512]{2,1,0:T(8,128)(2,1)} %get-tuple-element.42), channel_id=1, source_target_pairs={{0,20},{4,16},{16,4},{20,0},{1,21},{5,17},{17,5},{21,1},{2,22},{6,... | collective-permute-start | bytes 3145736 | tf_op jit(solution)/shard_map/ppermute | solution.py:332
  28.3 0.0 copy-done.2
  28.3 0.0 copy-done.5
  28.3 0.0 copy-done.6
  28.3 0.0 copy-done.7
  28.3 1.9 %shard_map.84.refs_3_ = f32[16,128,256]{2,1,0:T(8,128)S(1)} custom-call(f32[16,16384]{1,0:T(8,128)S(1)} %bitcast.8, bf16[256,256]{1,0:T(8,128)(2,1)S(1)} %copy-done.6, bf16[2,256,256]{2,1,0:T(8,128)(2,1)S(1)} %copy-done.5, f32[2,128,128]{2,1,0:T(8,128)S(1)} %copy-done.7), custom_call_target="tpu_custom_call" | custom-call | flops 1000000000 | bytes 1572864 | tf_op jit(solution)/shard_map/pallas_call | solution.py:271
  30.2 0.0 copy-start.8
  30.2 1.3 %copy-done.8 = f32[16,128,256]{2,1,0:T(8,128)} copy-done((f32[16,128,256]{2,1,0:T(8,128)}, f32[16,128,256]{2,1,0:T(8,128)S(1)}, u32[]{:S(2)}) %copy-start.8) | copy-done | bytes 2097176
  31.5 1.2 %collective-permute-start.4 = (bf16[2,256,512]{2,1,0:T(8,128)(2,1)}, bf16[2,256,512]{2,1,0:T(8,128)(2,1)}, u32[]{:S(2)}, u32[]{:S(2)}) collective-permute-start(bf16[2,256,512]{2,1,0:T(8,128)(2,1)} %get-tuple-element.31), channel_id=1, source_target_pairs={{0,1},{1,2},{2,3},{3,0},{4,5},{5,6},{6,7},{7,4},{8,9},{9,10},{10,1... | collective-permute-start | bytes 1572872 | tf_op jit(solution)/shard_map/ppermute | solution.py:332
  32.8 2.5 %collective-permute-start.6 = (bf16[2,256,512]{2,1,0:T(8,128)(2,1)}, bf16[2,256,512]{2,1,0:T(8,128)(2,1)}, u32[]{:S(2)}, u32[]{:S(2)}) collective-permute-start(bf16[2,256,512]{2,1,0:T(8,128)(2,1)} %get-tuple-element.32), channel_id=1, source_target_pairs={{0,2},{1,3},{2,0},{3,1},{4,6},{5,7},{6,4},{7,5},{8,10},{9,11},{10,... | collective-permute-start | bytes 1572872 | tf_op jit(solution)/shard_map/ppermute | solution.py:332
  35.2 2.4 %all-to-all-done.u_ref = bf16[32,16,512]{2,1,0:T(8,128)(2,1)S(1)} async-done(((bf16[32,16,512]{2,1,0:T(8,128)(2,1)}), bf16[32,16,512]{2,1,0:T(8,128)(2,1)S(1)}, u32[]{:S(2)}, u32[]{:S(2)}) %all-to-all-start) | async-done | bytes 524320 | tf_op jit(solution)/shard_map/all_to_all | solution.py:320
  37.6 6.5 %shard_map.85 = bf16[32,16,512]{2,1,0:T(8,128)(2,1)} custom-call(bf16[32,16,512]{2,1,0:T(8,128)(2,1)S(1)} %all-to-all-done.u_ref, bf16[256,256]{1,0:T(8,128)(2,1)} %constant.8.clone.fwd1_ref.refs_0_, f32[2,128,128]{2,1,0:T(8,128)} %constant.11.clone.twist_ref.refs_1_, bf16[2,256,256]{2,1,0:T(8,128)(2,1)} %constant.9.clone.fwd2_ref.refs_2_, ...), custom_call_target="tpu_custom_call" | custom-call | flops 3000000000 | bytes 3276800 | tf_op jit(solution)/shard_map/pallas_call | solution.py:271
  44.2 5.6 %all-to-all-start.1 = ((bf16[32,16,512]{2,1,0:T(8,128)(2,1)}), bf16[32,16,512]{2,1,0:T(8,128)(2,1)S(1)}, u32[]{:S(2)}, u32[]{:S(2)}) async-start(bf16[32,16,512]{2,1,0:T(8,128)(2,1)} %shard_map.85), calls=%async_computation.1 | async-start | bytes 1048576 | tf_op jit(solution)/shard_map/all_to_all | solution.py:342
  49.8 1.8 %collective-permute-start.8 = (bf16[2,256,512]{2,1,0:T(8,128)(2,1)S(1)}, bf16[2,256,512]{2,1,0:T(8,128)(2,1)}, u32[]{:S(2)}, u32[]{:S(2)}) collective-permute-start(bf16[2,256,512]{2,1,0:T(8,128)(2,1)S(1)} %copy-done.4), channel_id=1, source_target_pairs={{0,3},{1,0},{2,1},{3,2},{4,7},{5,4},{6,5},{7,6},{8,11},{9,8},{10,9... | collective-permute-start | bytes 1572872 | tf_op jit(solution)/shard_map/ppermute | solution.py:332
  51.7 0.1 collective-permute-done.11.refs_1_
  51.7 1.0 collective-permute-start.12
  52.7 0.0 collective-permute-done.4.refs_1_
  52.7 0.0 collective-permute-start.5
  52.7 5.5 %collective-permute-done.6.refs_3_ = bf16[2,256,512]{2,1,0:T(8,128)(2,1)} collective-permute-done((bf16[2,256,512]{2,1,0:T(8,128)(2,1)}, bf16[2,256,512]{2,1,0:T(8,128)(2,1)}, u32[]{:S(2)}, u32[]{:S(2)}) %collective-permute-start.6) | collective-permute-done | bytes 524320 | tf_op jit(solution)/shard_map/ppermute | solution.py:332
  58.2 1.5 %collective-permute-start.7 = (bf16[2,256,512]{2,1,0:T(8,128)(2,1)}, bf16[2,256,512]{2,1,0:T(8,128)(2,1)}, u32[]{:S(2)}, u32[]{:S(2)}) collective-permute-start(bf16[2,256,512]{2,1,0:T(8,128)(2,1)} %collective-permute-done.6.refs_3_), channel_id=1, source_target_pairs={{0,8},{8,0},{1,9},{9,1},{2,10},{10,2},{3,11},{11,3},{4,12},{12,4},... | collective-permute-start | bytes 1572872 | tf_op jit(solution)/shard_map/ppermute | solution.py:333
  59.7 3.6 %collective-permute-done.8.refs_5_ = bf16[2,256,512]{2,1,0:T(8,128)(2,1)} collective-permute-done((bf16[2,256,512]{2,1,0:T(8,128)(2,1)S(1)}, bf16[2,256,512]{2,1,0:T(8,128)(2,1)}, u32[]{:S(2)}, u32[]{:S(2)}) %collective-permute-start.8) | collective-permute-done | bytes 524320 | tf_op jit(solution)/shard_map/ppermute | solution.py:332
  63.3 1.1 %collective-permute-start.9 = (bf16[2,256,512]{2,1,0:T(8,128)(2,1)}, bf16[2,256,512]{2,1,0:T(8,128)(2,1)}, u32[]{:S(2)}, u32[]{:S(2)}) collective-permute-start(bf16[2,256,512]{2,1,0:T(8,128)(2,1)} %collective-permute-done.8.refs_5_), channel_id=1, source_target_pairs={{0,8},{8,0},{1,9},{9,1},{2,10},{10,2},{3,11},{11,3},{4,12},{12,4},... | collective-permute-start | bytes 1572872 | tf_op jit(solution)/shard_map/ppermute | solution.py:333
  64.4 0.0 copy-done
  64.4 0.6 shard_map.82.query_ref
  65.0 1.4 %all-to-all-done.1 = bf16[32,16,512]{2,1,0:T(8,128)(2,1)S(1)} async-done(((bf16[32,16,512]{2,1,0:T(8,128)(2,1)}), bf16[32,16,512]{2,1,0:T(8,128)(2,1)S(1)}, u32[]{:S(2)}, u32[]{:S(2)}) %all-to-all-start.1) | async-done | bytes 524320 | tf_op jit(solution)/shard_map/all_to_all | solution.py:342
  66.4 0.2 shard_map.86
  66.6 1.0 collective-permute-start.1
  67.6 0.0 collective-permute-done.5.refs_2_
  67.6 2.4 %collective-permute-start.2 = (bf16[256,512]{1,0:T(8,128)(2,1)S(1)}, bf16[256,512]{1,0:T(8,128)(2,1)S(1)}, u32[]{:S(2)}, u32[]{:S(2)}) collective-permute-start(bf16[256,512]{1,0:T(8,128)(2,1)S(1)} %get-tuple-element.29.refs_0_), channel_id=1, source_target_pairs={{0,2},{1,3},{2,0},{3,1},{4,6},{5,7},{6,4},{7,5},{8,10},{9,11},{10,... | collective-permute-start | bytes 786440 | tf_op jit(solution)/shard_map/ppermute | solution.py:348
  70.1 0.0 collective-permute-done.7.refs_4_
  70.1 1.2 %collective-permute-start.3 = (bf16[256,512]{1,0:T(8,128)(2,1)S(1)}, bf16[256,512]{1,0:T(8,128)(2,1)S(1)}, u32[]{:S(2)}, u32[]{:S(2)}) collective-permute-start(bf16[256,512]{1,0:T(8,128)(2,1)S(1)} %get-tuple-element.29.refs_0_), channel_id=1, source_target_pairs={{0,3},{1,0},{2,1},{3,2},{4,7},{5,4},{6,5},{7,6},{8,11},{9,8},{10,9... | collective-permute-start | bytes 786440 | tf_op jit(solution)/shard_map/ppermute | solution.py:348
  71.2 0.0 collective-permute-done.9.refs_6_
  71.2 2.9 %collective-permute-start.10 = (bf16[256,512]{1,0:T(8,128)(2,1)S(1)}, bf16[256,512]{1,0:T(8,128)(2,1)S(1)}, u32[]{:S(2)}, u32[]{:S(2)}) collective-permute-start(bf16[256,512]{1,0:T(8,128)(2,1)S(1)} %get-tuple-element.41.refs_11_.refs_0_), channel_id=1, source_target_pairs={{0,4},{4,0},{1,5},{5,1},{2,6},{6,2},{3,7},{7,3},{8,12},{12,8},{9,1... | collective-permute-start | bytes 786440 | tf_op jit(solution)/shard_map/ppermute | solution.py:348
  74.2 2.2 %shard_map.88 = (bf16[2,512,512]{2,1,0:T(8,128)(2,1)S(1)}, bf16[2,256,512]{2,1,0:T(8,128)(2,1)S(1)}, bf16[2,256,512]{2,1,0:T(8,128)(2,1)S(1)}, bf16[2,256,512]{2...) custom-call(bf16[512,4096]{1,0:T(8,128)(2,1)} %refs_0_.3, ...), custom_call_target="tpu_custom_call" | custom-call | bytes 7340032 | tf_op jit(solution)/shard_map/pallas_call | solution.py:271
  76.4 0.0 collective-permute-done.12.refs_2_
  76.4 2.3 %shard_map.89 = (bf16[4,512,512]{2,1,0:T(8,128)(2,1)S(1)}, bf16[4,256,512]{2,1,0:T(8,128)(2,1)S(1)}, bf16[4,256,512]{2,1,0:T(8,128)(2,1)S(1)}) custom-call(bf16[512,4096]{1,0:T(8,128)(2,1)} %refs_0_.3, bf16[4,256,512]{2,1,0:T(8,128)(2,1)} %collective-permute-done.11.refs_1_, bf16[4,256,512]{2,1,0:T(8,128)(2,1)} %collective-permute-done.12.refs_2_), custom_call_target="tpu_custom_call" | custom-call | bytes 6291456 | tf_op jit(solution)/shard_map/pallas_call | solution.py:271
  78.7 0.0 collective-permute-done.1.refs_1_
  78.7 2.1 %collective-permute-done.2.refs_2_ = bf16[256,512]{1,0:T(8,128)(2,1)S(1)} collective-permute-done((bf16[256,512]{1,0:T(8,128)(2,1)S(1)}, bf16[256,512]{1,0:T(8,128)(2,1)S(1)}, u32[]{:S(2)}, u32[]{:S(2)}) %collective-permute-start.2) | collective-permute-done | bytes 262176 | tf_op jit(solution)/shard_map/ppermute | solution.py:348
  80.8 0.4 collective-permute-done.3.refs_3_
  81.2 0.7 shard_map.91
  81.9 2.6 %collective-permute-start.13 = (bf16[256,512]{1,0:T(8,128)(2,1)S(1)}, bf16[256,512]{1,0:T(8,128)(2,1)S(1)}, u32[]{:S(2)}, u32[]{:S(2)}) collective-permute-start(bf16[256,512]{1,0:T(8,128)(2,1)S(1)} %shard_map.91), channel_id=1, source_target_pairs={{0,4},{4,0},{1,5},{5,1},{2,6},{6,2},{3,7},{7,3},{8,12},{12,8},{9,1... | collective-permute-start | bytes 786440 | tf_op jit(solution)/shard_map/ppermute | solution.py:348
  84.5 0.0 collective-permute-done.10.refs_12_.refs_1_
  84.5 1.0 shard_map.92
  85.5 2.1 %collective-permute-start.14 = (bf16[256,512]{1,0:T(8,128)(2,1)S(1)}, bf16[256,512]{1,0:T(8,128)(2,1)S(1)}, u32[]{:S(2)}, u32[]{:S(2)}) collective-permute-start(bf16[256,512]{1,0:T(8,128)(2,1)S(1)} %get-tuple-element.48), channel_id=1, source_target_pairs={{0,1},{1,2},{2,3},{3,0},{4,5},{5,6},{6,7},{7,4},{8,9},{9,10},{10,1... | collective-permute-start | bytes 786440 | tf_op jit(solution)/shard_map/ppermute | solution.py:348
  87.6 2.5 %collective-permute-start.15 = (bf16[256,512]{1,0:T(8,128)(2,1)S(1)}, bf16[256,512]{1,0:T(8,128)(2,1)S(1)}, u32[]{:S(2)}, u32[]{:S(2)}) collective-permute-start(bf16[256,512]{1,0:T(8,128)(2,1)S(1)} %get-tuple-element.49), channel_id=1, source_target_pairs={{0,2},{1,3},{2,0},{3,1},{4,6},{5,7},{6,4},{7,5},{8,10},{9,11},{10,... | collective-permute-start | bytes 786440 | tf_op jit(solution)/shard_map/ppermute | solution.py:348
  90.2 0.0 collective-permute-start.16
  90.2 1.0 shard_map.90
  91.1 0.0 collective-permute-done.13.refs_0_
  91.2 2.5 %collective-permute-done.14.refs_1_ = bf16[256,512]{1,0:T(8,128)(2,1)S(1)} collective-permute-done((bf16[256,512]{1,0:T(8,128)(2,1)S(1)}, bf16[256,512]{1,0:T(8,128)(2,1)S(1)}, u32[]{:S(2)}, u32[]{:S(2)}) %collective-permute-start.14) | collective-permute-done | bytes 262176 | tf_op jit(solution)/shard_map/ppermute | solution.py:348
  93.7 7.5 %collective-permute-done.15.refs_2_ = bf16[256,512]{1,0:T(8,128)(2,1)S(1)} collective-permute-done((bf16[256,512]{1,0:T(8,128)(2,1)S(1)}, bf16[256,512]{1,0:T(8,128)(2,1)S(1)}, u32[]{:S(2)}, u32[]{:S(2)}) %collective-permute-start.15) | collective-permute-done | bytes 262176 | tf_op jit(solution)/shard_map/ppermute | solution.py:348
  101.2 0.0 collective-permute-done.16.refs_3_
  101.2 0.9 shard_map.93
  (5 shorter events, 0.0 us)
Async XLA Ops:
  0.7 5.5 %collective-permute-start = (bf16[3,8,512]{2,1,0:T(8,128)(2,1)S(1)}, bf16[3,8,512]{2,1,0:T(8,128)(2,1)S(1)}, u32[]{:S(2)}, u32[]{:S(2)}) collective-permute-start(bf16[3,8,512]{2,1,0:T(8,128)(2,1)S(1)} %slice.4), channel_id=1, source_target_pairs={{0,8},{8,16},{16,24},{24,32},{32,40},{40,48},{48,56},{56,64},{64,7... | collective-permute-start | bytes 73736 | tf_op jit(solution)/shard_map/ppermute | solution.py:310
  9.2 28.4 %all-to-all-start = ((bf16[32,16,512]{2,1,0:T(8,128)(2,1)}), bf16[32,16,512]{2,1,0:T(8,128)(2,1)S(1)}, u32[]{:S(2)}, u32[]{:S(2)}) async-start(bf16[32,16,512]{2,1,0:T(8,128)(2,1)} %bitcast.1), calls=%async_computation | async-start | bytes 1048576 | tf_op jit(solution)/shard_map/all_to_all | solution.py:320
  21.1 7.2 %copy-start.2 = (f32[16384,16]{0,1:T(8,128)S(1)}, f32[16384,16]{0,1:T(8,128)}, u32[]{:S(2)}) copy-start(f32[16384,16]{0,1:T(8,128)} %param.10) | copy-start | bytes 3145732
  21.1 7.2 %copy-start.5 = (bf16[2,256,256]{2,1,0:T(8,128)(2,1)S(1)}, bf16[2,256,256]{2,1,0:T(8,128)(2,1)}, u32[]{:S(2)}) copy-start(bf16[2,256,256]{2,1,0:T(8,128)(2,1)} %constant.9.clone.fwd2_ref.refs_2_) | copy-start | bytes 786436
  21.1 7.2 %copy-start.6 = (bf16[256,256]{1,0:T(8,128)(2,1)S(1)}, bf16[256,256]{1,0:T(8,128)(2,1)}, u32[]{:S(2)}) copy-start(bf16[256,256]{1,0:T(8,128)(2,1)} %constant.8.clone.fwd1_ref.refs_0_) | copy-start | bytes 393220
  21.1 7.2 %copy-start.7 = (f32[2,128,128]{2,1,0:T(8,128)S(1)}, f32[2,128,128]{2,1,0:T(8,128)}, u32[]{:S(2)}) copy-start(f32[2,128,128]{2,1,0:T(8,128)} %constant.11.clone.twist_ref.refs_1_) | copy-start | bytes 393220
  24.4 0.8 copy-start.3
  25.2 26.5 %collective-permute-start.11 = (bf16[4,256,512]{2,1,0:T(8,128)(2,1)}, bf16[4,256,512]{2,1,0:T(8,128)(2,1)}, u32[]{:S(2)}, u32[]{:S(2)}) collective-permute-start(bf16[4,256,512]{2,1,0:T(8,128)(2,1)} %get-tuple-element.42), channel_id=1, source_target_pairs={{0,20},{4,16},{16,4},{20,0},{1,21},{5,17},{17,5},{21,1},{2,22},{6,... | collective-permute-start | bytes 3145736 | tf_op jit(solution)/shard_map/ppermute | solution.py:332
  30.2 1.3 %copy-start.8 = (f32[16,128,256]{2,1,0:T(8,128)}, f32[16,128,256]{2,1,0:T(8,128)S(1)}, u32[]{:S(2)}) copy-start(f32[16,128,256]{2,1,0:T(8,128)S(1)} %shard_map.84.refs_3_) | copy-start | bytes 6291460
  31.5 21.2 %collective-permute-start.4 = (bf16[2,256,512]{2,1,0:T(8,128)(2,1)}, bf16[2,256,512]{2,1,0:T(8,128)(2,1)}, u32[]{:S(2)}, u32[]{:S(2)}) collective-permute-start(bf16[2,256,512]{2,1,0:T(8,128)(2,1)} %get-tuple-element.31), channel_id=1, source_target_pairs={{0,1},{1,2},{2,3},{3,0},{4,5},{5,6},{6,7},{7,4},{8,9},{9,10},{10,1... | collective-permute-start | bytes 1572872 | tf_op jit(solution)/shard_map/ppermute | solution.py:332
  32.8 17.0 %copy-start.4 = (bf16[2,256,512]{2,1,0:T(8,128)(2,1)S(1)}, bf16[2,256,512]{2,1,0:T(8,128)(2,1)}, u32[]{:S(2)}) copy-start(bf16[2,256,512]{2,1,0:T(8,128)(2,1)} %copy-done.3) | copy-start | bytes 1572868
  32.8 31.6 %copy-start.1 = (f32[3,3,512]{2,1,0:T(4,128)S(1)}, f32[3,3,512]{2,1,0:T(4,128)}, u32[]{:S(2)}) copy-start(f32[3,3,512]{2,1,0:T(4,128)} %taps_hbm.1) | copy-start | bytes 55300
  32.8 25.4 %collective-permute-start.6 = (bf16[2,256,512]{2,1,0:T(8,128)(2,1)}, bf16[2,256,512]{2,1,0:T(8,128)(2,1)}, u32[]{:S(2)}, u32[]{:S(2)}) collective-permute-start(bf16[2,256,512]{2,1,0:T(8,128)(2,1)} %get-tuple-element.32), channel_id=1, source_target_pairs={{0,2},{1,3},{2,0},{3,1},{4,6},{5,7},{6,4},{7,5},{8,10},{9,11},{10,... | collective-permute-start | bytes 1572872 | tf_op jit(solution)/shard_map/ppermute | solution.py:332
  37.6 26.7 %copy-start = (bf16[512,3,512]{2,0,1:T(8,128)(2,1)S(1)}, bf16[512,3,512]{2,0,1:T(8,128)(2,1)}, u32[]{:S(2)}) copy-start(bf16[512,3,512]{2,0,1:T(8,128)(2,1)} %param.8) | copy-start | bytes 4718596
  44.2 22.2 %all-to-all-start.1 = ((bf16[32,16,512]{2,1,0:T(8,128)(2,1)}), bf16[32,16,512]{2,1,0:T(8,128)(2,1)S(1)}, u32[]{:S(2)}, u32[]{:S(2)}) async-start(bf16[32,16,512]{2,1,0:T(8,128)(2,1)} %shard_map.85), calls=%async_computation.1 | async-start | bytes 1048576 | tf_op jit(solution)/shard_map/all_to_all | solution.py:342
  49.8 13.4 %collective-permute-start.8 = (bf16[2,256,512]{2,1,0:T(8,128)(2,1)S(1)}, bf16[2,256,512]{2,1,0:T(8,128)(2,1)}, u32[]{:S(2)}, u32[]{:S(2)}) collective-permute-start(bf16[2,256,512]{2,1,0:T(8,128)(2,1)S(1)} %copy-done.4), channel_id=1, source_target_pairs={{0,3},{1,0},{2,1},{3,2},{4,7},{5,4},{6,5},{7,6},{8,11},{9,8},{10,9... | collective-permute-start | bytes 1572872 | tf_op jit(solution)/shard_map/ppermute | solution.py:332
  51.7 24.6 %collective-permute-start.12 = (bf16[4,256,512]{2,1,0:T(8,128)(2,1)}, bf16[4,256,512]{2,1,0:T(8,128)(2,1)}, u32[]{:S(2)}, u32[]{:S(2)}) collective-permute-start(bf16[4,256,512]{2,1,0:T(8,128)(2,1)} %collective-permute-done.11.refs_1_), channel_id=1, source_target_pairs={{0,8},{8,0},{1,9},{9,1},{2,10},{10,2},{3,11},{11,3},{4,12},{12,4},... | collective-permute-start | bytes 3145736 | tf_op jit(solution)/shard_map/ppermute | solution.py:333
  52.7 14.9 %collective-permute-start.5 = (bf16[2,256,512]{2,1,0:T(8,128)(2,1)}, bf16[2,256,512]{2,1,0:T(8,128)(2,1)}, u32[]{:S(2)}, u32[]{:S(2)}) collective-permute-start(bf16[2,256,512]{2,1,0:T(8,128)(2,1)} %collective-permute-done.4.refs_1_), channel_id=1, source_target_pairs={{0,8},{8,0},{1,9},{9,1},{2,10},{10,2},{3,11},{11,3},{4,12},{12,4},... | collective-permute-start | bytes 1572872 | tf_op jit(solution)/shard_map/ppermute | solution.py:333
  58.2 11.9 %collective-permute-start.7 = (bf16[2,256,512]{2,1,0:T(8,128)(2,1)}, bf16[2,256,512]{2,1,0:T(8,128)(2,1)}, u32[]{:S(2)}, u32[]{:S(2)}) collective-permute-start(bf16[2,256,512]{2,1,0:T(8,128)(2,1)} %collective-permute-done.6.refs_3_), channel_id=1, source_target_pairs={{0,8},{8,0},{1,9},{9,1},{2,10},{10,2},{3,11},{11,3},{4,12},{12,4},... | collective-permute-start | bytes 1572872 | tf_op jit(solution)/shard_map/ppermute | solution.py:333
  63.3 8.0 %collective-permute-start.9 = (bf16[2,256,512]{2,1,0:T(8,128)(2,1)}, bf16[2,256,512]{2,1,0:T(8,128)(2,1)}, u32[]{:S(2)}, u32[]{:S(2)}) collective-permute-start(bf16[2,256,512]{2,1,0:T(8,128)(2,1)} %collective-permute-done.8.refs_5_), channel_id=1, source_target_pairs={{0,8},{8,0},{1,9},{9,1},{2,10},{10,2},{3,11},{11,3},{4,12},{12,4},... | collective-permute-start | bytes 1572872 | tf_op jit(solution)/shard_map/ppermute | solution.py:333
  66.6 12.1 %collective-permute-start.1 = (bf16[256,512]{1,0:T(8,128)(2,1)S(1)}, bf16[256,512]{1,0:T(8,128)(2,1)S(1)}, u32[]{:S(2)}, u32[]{:S(2)}) collective-permute-start(bf16[256,512]{1,0:T(8,128)(2,1)S(1)} %get-tuple-element.29.refs_0_), channel_id=1, source_target_pairs={{0,1},{1,2},{2,3},{3,0},{4,5},{5,6},{6,7},{7,4},{8,9},{9,10},{10,1... | collective-permute-start | bytes 786440 | tf_op jit(solution)/shard_map/ppermute | solution.py:348
  67.6 13.1 %collective-permute-start.2 = (bf16[256,512]{1,0:T(8,128)(2,1)S(1)}, bf16[256,512]{1,0:T(8,128)(2,1)S(1)}, u32[]{:S(2)}, u32[]{:S(2)}) collective-permute-start(bf16[256,512]{1,0:T(8,128)(2,1)S(1)} %get-tuple-element.29.refs_0_), channel_id=1, source_target_pairs={{0,2},{1,3},{2,0},{3,1},{4,6},{5,7},{6,4},{7,5},{8,10},{9,11},{10,... | collective-permute-start | bytes 786440 | tf_op jit(solution)/shard_map/ppermute | solution.py:348
  70.1 11.1 %collective-permute-start.3 = (bf16[256,512]{1,0:T(8,128)(2,1)S(1)}, bf16[256,512]{1,0:T(8,128)(2,1)S(1)}, u32[]{:S(2)}, u32[]{:S(2)}) collective-permute-start(bf16[256,512]{1,0:T(8,128)(2,1)S(1)} %get-tuple-element.29.refs_0_), channel_id=1, source_target_pairs={{0,3},{1,0},{2,1},{3,2},{4,7},{5,4},{6,5},{7,6},{8,11},{9,8},{10,9... | collective-permute-start | bytes 786440 | tf_op jit(solution)/shard_map/ppermute | solution.py:348
  71.2 13.3 %collective-permute-start.10 = (bf16[256,512]{1,0:T(8,128)(2,1)S(1)}, bf16[256,512]{1,0:T(8,128)(2,1)S(1)}, u32[]{:S(2)}, u32[]{:S(2)}) collective-permute-start(bf16[256,512]{1,0:T(8,128)(2,1)S(1)} %get-tuple-element.41.refs_11_.refs_0_), channel_id=1, source_target_pairs={{0,4},{4,0},{1,5},{5,1},{2,6},{6,2},{3,7},{7,3},{8,12},{12,8},{9,1... | collective-permute-start | bytes 786440 | tf_op jit(solution)/shard_map/ppermute | solution.py:348
  81.9 9.2 %collective-permute-start.13 = (bf16[256,512]{1,0:T(8,128)(2,1)S(1)}, bf16[256,512]{1,0:T(8,128)(2,1)S(1)}, u32[]{:S(2)}, u32[]{:S(2)}) collective-permute-start(bf16[256,512]{1,0:T(8,128)(2,1)S(1)} %shard_map.91), channel_id=1, source_target_pairs={{0,4},{4,0},{1,5},{5,1},{2,6},{6,2},{3,7},{7,3},{8,12},{12,8},{9,1... | collective-permute-start | bytes 786440 | tf_op jit(solution)/shard_map/ppermute | solution.py:348
  85.5 8.2 %collective-permute-start.14 = (bf16[256,512]{1,0:T(8,128)(2,1)S(1)}, bf16[256,512]{1,0:T(8,128)(2,1)S(1)}, u32[]{:S(2)}, u32[]{:S(2)}) collective-permute-start(bf16[256,512]{1,0:T(8,128)(2,1)S(1)} %get-tuple-element.48), channel_id=1, source_target_pairs={{0,1},{1,2},{2,3},{3,0},{4,5},{5,6},{6,7},{7,4},{8,9},{9,10},{10,1... | collective-permute-start | bytes 786440 | tf_op jit(solution)/shard_map/ppermute | solution.py:348
  87.6 13.5 %collective-permute-start.15 = (bf16[256,512]{1,0:T(8,128)(2,1)S(1)}, bf16[256,512]{1,0:T(8,128)(2,1)S(1)}, u32[]{:S(2)}, u32[]{:S(2)}) collective-permute-start(bf16[256,512]{1,0:T(8,128)(2,1)S(1)} %get-tuple-element.49), channel_id=1, source_target_pairs={{0,2},{1,3},{2,0},{3,1},{4,6},{5,7},{6,4},{7,5},{8,10},{9,11},{10,... | collective-permute-start | bytes 786440 | tf_op jit(solution)/shard_map/ppermute | solution.py:348
  90.2 11.0 %collective-permute-start.16 = (bf16[256,512]{1,0:T(8,128)(2,1)S(1)}, bf16[256,512]{1,0:T(8,128)(2,1)S(1)}, u32[]{:S(2)}, u32[]{:S(2)}) collective-permute-start(bf16[256,512]{1,0:T(8,128)(2,1)S(1)} %get-tuple-element.50), channel_id=1, source_target_pairs={{0,3},{1,0},{2,1},{3,2},{4,7},{5,4},{6,5},{7,6},{8,11},{9,8},{10,9... | collective-permute-start | bytes 786440 | tf_op jit(solution)/shard_map/ppermute | solution.py:348

commit v5 on v4

--- a/solution.py
+++ b/solution.py
@@ -137,24 +137,21 @@
     return total
 
 
-def gate_in_kernel(edge_ref, x_hbm, taps_hbm, out_hbm, ext, keys, values, taps, out_ref, sem, out_sem):
+def load_kernel(x_hbm, taps_hbm, keys_ref, values_ref, taps_ref, sem):
+    for c in fetch((taps_hbm, x_hbm.at[1], x_hbm.at[2]), (taps_ref, keys_ref, values_ref), sem):
+        c.wait()
+
+
+def gate_in_kernel(edge_ref, keys_ref, values_ref, taps_ref, out_hbm, ext, out_ref, sem):
     parts = 4
-    size = keys.shape[1] // parts
-    cuts = [slice(p * size, (p + 1) * size) for p in range(parts)]
-    sources, targets = [taps_hbm], [taps]
-    for cut in cuts:
-        sources += [x_hbm.at[1, :, cut], x_hbm.at[2, :, cut]]
-        targets += [keys.at[:, cut], values.at[:, cut]]
-    copies = fetch(sources, targets, sem)
-    copies[0].wait()
+    size = keys_ref.shape[1] // parts
     outs = []
-    for p, cut in enumerate(cuts):
-        copies[1 + 2 * p].wait()
-        copies[2 + 2 * p].wait()
-        key = featured(keys[:, cut], edge_ref, taps, ext, 1, cut)
-        product = key * featured(values[:, cut], edge_ref, taps, ext, 2, cut)
+    for p in range(parts):
+        cut = slice(p * size, (p + 1) * size)
+        key = featured(keys_ref[:, cut], edge_ref, taps_ref, ext, 1, cut)
+        product = key * featured(values_ref[:, cut], edge_ref, taps_ref, ext, 2, cut)
         out_ref[cut, :] = product.T.astype(bf16)
-        outs.append(pltpu.make_async_copy(out_ref.at[cut], out_hbm.at[cut], out_sem.at[p]))
+        outs.append(pltpu.make_async_copy(out_ref.at[cut], out_hbm.at[cut], sem.at[p]))
         outs[-1].start()
     for c in outs:
         c.wait()
@@ -308,13 +305,15 @@
 
     streams_first = jnp.transpose(proj, (1, 0, 2))
     edge = lax.ppermute(streams_first[:, tokens - EDGE :, :], CTX, [(i, i + 1) for i in range(ctx - 1)])
+    loaded = call(
+        load_kernel, [((tokens, width), bf16)] * 2 + [(short_filter.shape, f32)],
+        [pltpu.SemaphoreType.DMA((3,))], 0, streams_first, short_filter, specs=[HBM] * 2,
+    )
     ext = [pltpu.VMEM((tokens + EDGE, width), f32)]
     gated_in = call(
         gate_in_kernel, [((width, tokens), bf16)],
-        ext
-        + held(streams_first[1], streams_first[2], short_filter)[:-1]
-        + [pltpu.VMEM((width, tokens), bf16), pltpu.SemaphoreType.DMA((9,)), pltpu.SemaphoreType.DMA((4,))],
-        0, edge, streams_first, short_filter, specs=[VM, HBM, HBM], outs_at=HBM,
+        ext + [pltpu.VMEM((width, tokens), bf16), pltpu.SemaphoreType.DMA((4,))],
+        0, edge, *loaded, outs_at=HBM,
     )
     gated_in, out_weight = lax.optimization_barrier((gated_in, out_weight))
     signal = lax.all_to_all(gated_in.reshape(ctx, mine, tokens), CTX, 0, 0)

time: 103 us -> 101 us (0.981)
    pallas_call x12 -> x13, Pallas kernels: 23.6 us -> 23.5 us  [call(): pl.pallas_call(kernel, out_shape=shapes, in_specs=specs, out_specs=[outs_...]
  transfers between devices with their start and end apart: 19 -> 19, of which waited for: 10 -> 9; matrix products, arithmetic and copies ran while one was open for 0% -> 0% of each run, Pallas kernels for 19% -> 21%
where the time goes in v5:
time: 101 us
  starting transfers between devices  48.7 us (48%)
  waiting for transfers between devices  25.5 us (25%)
  Pallas kernels  23.5 us (23%)
  local copies, waits for them, and re-layouts  2.91 us (3%)
    pallas_call x13, Pallas kernels, call(): pl.pallas_call(kernel, out_shape=shapes, in_specs=specs, out_specs=[outs_...  23.5 us
    ppermute x8, starting transfers between devices, send(): return lax.ppermute(block, axis, ring(axis, shift))  14.8 us
    ppermute x8, waiting for transfers between devices, send(): return lax.ppermute(block, axis, ring(axis, shift))  12.5 us
    all_to_all x1, starting transfers between devices, body(): signal = lax.all_to_all(gated_in.reshape(ctx, mine, tokens), CTX, 0, 0)  11.5 us
    ppermute x4, waiting for transfers between devices, swapped(): came = lax.ppermute(block, axis, route)  9.12 us
    ppermute x4, starting transfers between devices, swapped(): came = lax.ppermute(block, axis, route)  8.61 us
    all_to_all x1, starting transfers between devices, body(): returned = lax.all_to_all(convolved, CTX, 0, 0).reshape(width, tokens)  5.61 us
    ppermute x1, starting transfers between devices, body(): lax.ppermute(streams_first[:, tokens - EDGE:, :], CTX, [(i, i + 1) for i...  4.57 us
  transfers between devices with their start and end apart: 19, of which 9 were waited for; matrix products, arithmetic and copies ran while one was open for 0% of the time, Pallas kernels for 21%

profile of v5, /device:TPU:1, one launch (start us, length us, event | category | flops | bytes accessed | tf_op | source)
XLA Modules:
  0.0 100.8 jit_solution(8254982188007231984)
XLA Ops:
  0.0 0.7 slice.4
  0.7 4.6 %collective-permute-start = (bf16[3,8,512]{2,1,0:T(8,128)(2,1)S(1)}, bf16[3,8,512]{2,1,0:T(8,128)(2,1)S(1)}, u32[]{:S(2)}, u32[]{:S(2)}) collective-permute-start(bf16[3,8,512]{2,1,0:T(8,128)(2,1)S(1)} %slice.4), channel_id=1, source_target_pairs={{0,8},{8,16},{16,24},{24,32},{32,40},{40,48},{48,56},{56,64},{64,7... | collective-permute-start | bytes 73736 | tf_op jit(solution)/shard_map/ppermute | solution.py:307
  5.3 1.2 %shard_map.83 = (bf16[512,512]{1,0:T(8,128)(2,1)S(1)}, bf16[512,512]{1,0:T(8,128)(2,1)S(1)}, f32[3,3,512]{2,1,0:T(4,128)S(1)}) custom-call(bf16[3,512,512]{2,1,0:T(8,128)(2,1)} %bitcast.5, f32[3,3,512]{2,1,0:T(4,128)} %taps_hbm.1), custom_call_target="tpu_custom_call" | custom-call | bytes 1591296 | tf_op jit(solution)/shard_map/pallas_call | solution.py:268
  6.6 0.0 collective-permute-done.edge_ref
  6.6 1.7 %shard_map.84 = bf16[512,512]{1,0:T(8,128)(2,1)} custom-call(bf16[3,8,512]{2,1,0:T(8,128)(2,1)S(1)} %collective-permute-done.edge_ref, bf16[512,512]{1,0:T(8,128)(2,1)S(1)} %get-tuple-element.31.keys_ref, bf16[512,512]{1,0:T(8,128)(2,1)S(1)} %get-tuple-element.32.values_ref, f32[3,3,512]{2,1,0:T(4,128)S(1)} %get-tuple-element.33.taps_ref), custom_call_target="tpu_custom_call" | custom-call | bytes 1091584 | tf_op jit(solution)/shard_map/pallas_call | solution.py:268
  8.3 11.5 %all-to-all-start = ((bf16[32,16,512]{2,1,0:T(8,128)(2,1)}), bf16[32,16,512]{2,1,0:T(8,128)(2,1)S(1)}, u32[]{:S(2)}, u32[]{:S(2)}) async-start(bf16[32,16,512]{2,1,0:T(8,128)(2,1)} %bitcast.1), calls=%async_computation | async-start | bytes 1048576 | tf_op jit(solution)/shard_map/all_to_all | solution.py:319
  19.8 0.0 copy-start.2
  19.8 0.0 copy-start.5
  19.8 0.0 copy-start.6
  19.8 0.0 copy-start.7
  19.8 3.2 %shard_map.88 = (bf16[2,256,512]{2,1,0:T(8,128)(2,1)}, bf16[2,256,512]{2,1,0:T(8,128)(2,1)}, bf16[2,256,512]{2,1,0:T(8,128)(2,1)S(1)}, bf16[4,256,512]{2,1,0:T(8,128)(2,1)}) custom-call(bf16[512,4096]{1,0:T(8,128)(2,1)} %refs_0_.3), custom_call_target="tpu_custom_call" | custom-call | bytes 4194304 | tf_op jit(solution)/shard_map/pallas_call | solution.py:268
  23.1 0.0 copy-start.3
  23.1 0.8 copy-done.3
  23.9 3.1 %collective-permute-start.11 = (bf16[4,256,512]{2,1,0:T(8,128)(2,1)}, bf16[4,256,512]{2,1,0:T(8,128)(2,1)}, u32[]{:S(2)}, u32[]{:S(2)}) collective-permute-start(bf16[4,256,512]{2,1,0:T(8,128)(2,1)} %get-tuple-element.48), channel_id=1, source_target_pairs={{0,20},{4,16},{16,4},{20,0},{1,21},{5,17},{17,5},{21,1},{2,22},{6,... | collective-permute-start | bytes 3145736 | tf_op jit(solution)/shard_map/ppermute | solution.py:331
  27.0 0.0 copy-done.2
  27.0 0.0 copy-done.5
  27.0 0.0 copy-done.6
  27.0 1.9 %shard_map.85.refs_3_ = f32[16,128,256]{2,1,0:T(8,128)S(1)} custom-call(f32[16,16384]{1,0:T(8,128)S(1)} %bitcast.8, bf16[256,256]{1,0:T(8,128)(2,1)S(1)} %copy-done.6, bf16[2,256,256]{2,1,0:T(8,128)(2,1)S(1)} %copy-done.5, f32[2,128,128]{2,1,0:T(8,128)S(1)} %copy-done.7), custom_call_target="tpu_custom_call" | custom-call | flops 1000000000 | bytes 1572864 | tf_op jit(solution)/shard_map/pallas_call | solution.py:268
  28.9 1.3 %copy-done.8 = f32[16,128,256]{2,1,0:T(8,128)} copy-done((f32[16,128,256]{2,1,0:T(8,128)}, f32[16,128,256]{2,1,0:T(8,128)S(1)}, u32[]{:S(2)}) %copy-start.8) | copy-done | bytes 2097176
  30.2 1.2 %collective-permute-start.4 = (bf16[2,256,512]{2,1,0:T(8,128)(2,1)}, bf16[2,256,512]{2,1,0:T(8,128)(2,1)}, u32[]{:S(2)}, u32[]{:S(2)}) collective-permute-start(bf16[2,256,512]{2,1,0:T(8,128)(2,1)} %get-tuple-element.37), channel_id=1, source_target_pairs={{0,1},{1,2},{2,3},{3,0},{4,5},{5,6},{6,7},{7,4},{8,9},{9,10},{10,1... | collective-permute-start | bytes 1572872 | tf_op jit(solution)/shard_map/ppermute | solution.py:331
  31.5 2.5 %collective-permute-start.6 = (bf16[2,256,512]{2,1,0:T(8,128)(2,1)}, bf16[2,256,512]{2,1,0:T(8,128)(2,1)}, u32[]{:S(2)}, u32[]{:S(2)}) collective-permute-start(bf16[2,256,512]{2,1,0:T(8,128)(2,1)} %get-tuple-element.38), channel_id=1, source_target_pairs={{0,2},{1,3},{2,0},{3,1},{4,6},{5,7},{6,4},{7,5},{8,10},{9,11},{10,... | collective-permute-start | bytes 1572872 | tf_op jit(solution)/shard_map/ppermute | solution.py:331
  33.9 2.4 %all-to-all-done.u_ref = bf16[32,16,512]{2,1,0:T(8,128)(2,1)S(1)} async-done(((bf16[32,16,512]{2,1,0:T(8,128)(2,1)}), bf16[32,16,512]{2,1,0:T(8,128)(2,1)S(1)}, u32[]{:S(2)}, u32[]{:S(2)}) %all-to-all-start) | async-done | bytes 524320 | tf_op jit(solution)/shard_map/all_to_all | solution.py:319
  36.3 6.5 %shard_map.86 = bf16[32,16,512]{2,1,0:T(8,128)(2,1)} custom-call(bf16[32,16,512]{2,1,0:T(8,128)(2,1)S(1)} %all-to-all-done.u_ref, bf16[256,256]{1,0:T(8,128)(2,1)} %constant.8.clone.fwd1_ref.refs_0_, f32[2,128,128]{2,1,0:T(8,128)} %constant.11.clone.twist_ref.refs_1_, bf16[2,256,256]{2,1,0:T(8,128)(2,1)} %constant.9.clone.fwd2_ref.refs_2_, ...), custom_call_target="tpu_custom_call" | custom-call | flops 3000000000 | bytes 3276800 | tf_op jit(solution)/shard_map/pallas_call | solution.py:268
  42.9 5.6 %all-to-all-start.1 = ((bf16[32,16,512]{2,1,0:T(8,128)(2,1)}), bf16[32,16,512]{2,1,0:T(8,128)(2,1)S(1)}, u32[]{:S(2)}, u32[]{:S(2)}) async-start(bf16[32,16,512]{2,1,0:T(8,128)(2,1)} %shard_map.86), calls=%async_computation.1 | async-start | bytes 1048576 | tf_op jit(solution)/shard_map/all_to_all | solution.py:341
  48.5 0.0 copy-done.4
  48.5 1.8 %collective-permute-start.8 = (bf16[2,256,512]{2,1,0:T(8,128)(2,1)S(1)}, bf16[2,256,512]{2,1,0:T(8,128)(2,1)}, u32[]{:S(2)}, u32[]{:S(2)}) collective-permute-start(bf16[2,256,512]{2,1,0:T(8,128)(2,1)S(1)} %copy-done.4), channel_id=1, source_target_pairs={{0,3},{1,0},{2,1},{3,2},{4,7},{5,4},{6,5},{7,6},{8,11},{9,8},{10,9... | collective-permute-start | bytes 1572872 | tf_op jit(solution)/shard_map/ppermute | solution.py:331
  50.4 0.1 collective-permute-done.11.refs_1_
  50.4 1.0 collective-permute-start.12
  51.4 0.0 collective-permute-done.4.refs_1_
  51.4 0.0 collective-permute-start.5
  51.4 5.4 %collective-permute-done.6.refs_3_ = bf16[2,256,512]{2,1,0:T(8,128)(2,1)} collective-permute-done((bf16[2,256,512]{2,1,0:T(8,128)(2,1)}, bf16[2,256,512]{2,1,0:T(8,128)(2,1)}, u32[]{:S(2)}, u32[]{:S(2)}) %collective-permute-start.6) | collective-permute-done | bytes 524320 | tf_op jit(solution)/shard_map/ppermute | solution.py:331
  56.9 1.5 %collective-permute-start.7 = (bf16[2,256,512]{2,1,0:T(8,128)(2,1)}, bf16[2,256,512]{2,1,0:T(8,128)(2,1)}, u32[]{:S(2)}, u32[]{:S(2)}) collective-permute-start(bf16[2,256,512]{2,1,0:T(8,128)(2,1)} %collective-permute-done.6.refs_3_), channel_id=1, source_target_pairs={{0,8},{8,0},{1,9},{9,1},{2,10},{10,2},{3,11},{11,3},{4,12},{12,4},... | collective-permute-start | bytes 1572872 | tf_op jit(solution)/shard_map/ppermute | solution.py:332
  58.3 3.6 %collective-permute-done.8.refs_5_ = bf16[2,256,512]{2,1,0:T(8,128)(2,1)} collective-permute-done((bf16[2,256,512]{2,1,0:T(8,128)(2,1)S(1)}, bf16[2,256,512]{2,1,0:T(8,128)(2,1)}, u32[]{:S(2)}, u32[]{:S(2)}) %collective-permute-start.8) | collective-permute-done | bytes 524320 | tf_op jit(solution)/shard_map/ppermute | solution.py:331
  62.0 1.1 %collective-permute-start.9 = (bf16[2,256,512]{2,1,0:T(8,128)(2,1)}, bf16[2,256,512]{2,1,0:T(8,128)(2,1)}, u32[]{:S(2)}, u32[]{:S(2)}) collective-permute-start(bf16[2,256,512]{2,1,0:T(8,128)(2,1)} %collective-permute-done.8.refs_5_), channel_id=1, source_target_pairs={{0,8},{8,0},{1,9},{9,1},{2,10},{10,2},{3,11},{11,3},{4,12},{12,4},... | collective-permute-start | bytes 1572872 | tf_op jit(solution)/shard_map/ppermute | solution.py:332
  63.1 0.0 copy-done
  63.1 0.6 shard_map.82.query_ref
  63.7 1.4 %all-to-all-done.1 = bf16[32,16,512]{2,1,0:T(8,128)(2,1)S(1)} async-done(((bf16[32,16,512]{2,1,0:T(8,128)(2,1)}), bf16[32,16,512]{2,1,0:T(8,128)(2,1)S(1)}, u32[]{:S(2)}, u32[]{:S(2)}) %all-to-all-start.1) | async-done | bytes 524320 | tf_op jit(solution)/shard_map/all_to_all | solution.py:341
  65.1 0.2 shard_map.87
  65.3 1.0 %collective-permute-start.1 = (bf16[256,512]{1,0:T(8,128)(2,1)S(1)}, bf16[256,512]{1,0:T(8,128)(2,1)S(1)}, u32[]{:S(2)}, u32[]{:S(2)}) collective-permute-start(bf16[256,512]{1,0:T(8,128)(2,1)S(1)} %get-tuple-element.35.refs_0_), channel_id=1, source_target_pairs={{0,1},{1,2},{2,3},{3,0},{4,5},{5,6},{6,7},{7,4},{8,9},{9,10},{10,1... | collective-permute-start | bytes 786440 | tf_op jit(solution)/shard_map/ppermute | solution.py:347
  66.3 0.0 collective-permute-done.5.refs_2_
  66.3 2.5 %collective-permute-start.2 = (bf16[256,512]{1,0:T(8,128)(2,1)S(1)}, bf16[256,512]{1,0:T(8,128)(2,1)S(1)}, u32[]{:S(2)}, u32[]{:S(2)}) collective-permute-start(bf16[256,512]{1,0:T(8,128)(2,1)S(1)} %get-tuple-element.35.refs_0_), channel_id=1, source_target_pairs={{0,2},{1,3},{2,0},{3,1},{4,6},{5,7},{6,4},{7,5},{8,10},{9,11},{10,... | collective-permute-start | bytes 786440 | tf_op jit(solution)/shard_map/ppermute | solution.py:347
  68.8 0.0 collective-permute-done.7.refs_4_
  68.8 1.2 %collective-permute-start.3 = (bf16[256,512]{1,0:T(8,128)(2,1)S(1)}, bf16[256,512]{1,0:T(8,128)(2,1)S(1)}, u32[]{:S(2)}, u32[]{:S(2)}) collective-permute-start(bf16[256,512]{1,0:T(8,128)(2,1)S(1)} %get-tuple-element.35.refs_0_), channel_id=1, source_target_pairs={{0,3},{1,0},{2,1},{3,2},{4,7},{5,4},{6,5},{7,6},{8,11},{9,8},{10,9... | collective-permute-start | bytes 786440 | tf_op jit(solution)/shard_map/ppermute | solution.py:347
  69.9 0.0 collective-permute-done.9.refs_6_
  69.9 2.9 %collective-permute-start.10 = (bf16[256,512]{1,0:T(8,128)(2,1)S(1)}, bf16[256,512]{1,0:T(8,128)(2,1)S(1)}, u32[]{:S(2)}, u32[]{:S(2)}) collective-permute-start(bf16[256,512]{1,0:T(8,128)(2,1)S(1)} %get-tuple-element.47.refs_11_.refs_0_), channel_id=1, source_target_pairs={{0,4},{4,0},{1,5},{5,1},{2,6},{6,2},{3,7},{7,3},{8,12},{12,8},{9,1... | collective-permute-start | bytes 786440 | tf_op jit(solution)/shard_map/ppermute | solution.py:347
  72.8 2.2 %shard_map.89 = (bf16[2,512,512]{2,1,0:T(8,128)(2,1)S(1)}, bf16[2,256,512]{2,1,0:T(8,128)(2,1)S(1)}, bf16[2,256,512]{2,1,0:T(8,128)(2,1)S(1)}, bf16[2,256,512]{2...) custom-call(bf16[512,4096]{1,0:T(8,128)(2,1)} %refs_0_.3, ...), custom_call_target="tpu_custom_call" | custom-call | bytes 7340032 | tf_op jit(solution)/shard_map/pallas_call | solution.py:268
  75.1 0.0 collective-permute-done.12.refs_2_
  75.1 2.3 %shard_map.90 = (bf16[4,512,512]{2,1,0:T(8,128)(2,1)S(1)}, bf16[4,256,512]{2,1,0:T(8,128)(2,1)S(1)}, bf16[4,256,512]{2,1,0:T(8,128)(2,1)S(1)}) custom-call(bf16[512,4096]{1,0:T(8,128)(2,1)} %refs_0_.3, bf16[4,256,512]{2,1,0:T(8,128)(2,1)} %collective-permute-done.11.refs_1_, bf16[4,256,512]{2,1,0:T(8,128)(2,1)} %collective-permute-done.12.refs_2_), custom_call_target="tpu_custom_call" | custom-call | bytes 6291456 | tf_op jit(solution)/shard_map/pallas_call | solution.py:268
  77.4 0.0 collective-permute-done.1.refs_1_
  77.4 2.1 %collective-permute-done.2.refs_2_ = bf16[256,512]{1,0:T(8,128)(2,1)S(1)} collective-permute-done((bf16[256,512]{1,0:T(8,128)(2,1)S(1)}, bf16[256,512]{1,0:T(8,128)(2,1)S(1)}, u32[]{:S(2)}, u32[]{:S(2)}) %collective-permute-start.2) | collective-permute-done | bytes 262176 | tf_op jit(solution)/shard_map/ppermute | solution.py:347
  79.5 0.4 collective-permute-done.3.refs_3_
  79.9 0.7 shard_map.92
  80.6 2.6 %collective-permute-start.13 = (bf16[256,512]{1,0:T(8,128)(2,1)S(1)}, bf16[256,512]{1,0:T(8,128)(2,1)S(1)}, u32[]{:S(2)}, u32[]{:S(2)}) collective-permute-start(bf16[256,512]{1,0:T(8,128)(2,1)S(1)} %shard_map.92), channel_id=1, source_target_pairs={{0,4},{4,0},{1,5},{5,1},{2,6},{6,2},{3,7},{7,3},{8,12},{12,8},{9,1... | collective-permute-start | bytes 786440 | tf_op jit(solution)/shard_map/ppermute | solution.py:347
  83.2 0.0 collective-permute-done.10.refs_12_.refs_1_
  83.2 1.0 shard_map.93
  84.2 2.1 %collective-permute-start.14 = (bf16[256,512]{1,0:T(8,128)(2,1)S(1)}, bf16[256,512]{1,0:T(8,128)(2,1)S(1)}, u32[]{:S(2)}, u32[]{:S(2)}) collective-permute-start(bf16[256,512]{1,0:T(8,128)(2,1)S(1)} %get-tuple-element.54), channel_id=1, source_target_pairs={{0,1},{1,2},{2,3},{3,0},{4,5},{5,6},{6,7},{7,4},{8,9},{9,10},{10,1... | collective-permute-start | bytes 786440 | tf_op jit(solution)/shard_map/ppermute | solution.py:347
  86.3 2.5 %collective-permute-start.15 = (bf16[256,512]{1,0:T(8,128)(2,1)S(1)}, bf16[256,512]{1,0:T(8,128)(2,1)S(1)}, u32[]{:S(2)}, u32[]{:S(2)}) collective-permute-start(bf16[256,512]{1,0:T(8,128)(2,1)S(1)} %get-tuple-element.55), channel_id=1, source_target_pairs={{0,2},{1,3},{2,0},{3,1},{4,6},{5,7},{6,4},{7,5},{8,10},{9,11},{10,... | collective-permute-start | bytes 786440 | tf_op jit(solution)/shard_map/ppermute | solution.py:347
  88.9 0.0 collective-permute-start.16
  88.9 1.0 shard_map.91
  89.8 0.0 collective-permute-done.13.refs_0_
  89.9 2.5 %collective-permute-done.14.refs_1_ = bf16[256,512]{1,0:T(8,128)(2,1)S(1)} collective-permute-done((bf16[256,512]{1,0:T(8,128)(2,1)S(1)}, bf16[256,512]{1,0:T(8,128)(2,1)S(1)}, u32[]{:S(2)}, u32[]{:S(2)}) %collective-permute-start.14) | collective-permute-done | bytes 262176 | tf_op jit(solution)/shard_map/ppermute | solution.py:347
  92.4 7.5 %collective-permute-done.15.refs_2_ = bf16[256,512]{1,0:T(8,128)(2,1)S(1)} collective-permute-done((bf16[256,512]{1,0:T(8,128)(2,1)S(1)}, bf16[256,512]{1,0:T(8,128)(2,1)S(1)}, u32[]{:S(2)}, u32[]{:S(2)}) %collective-permute-start.15) | collective-permute-done | bytes 262176 | tf_op jit(solution)/shard_map/ppermute | solution.py:347
  99.9 0.0 collective-permute-done.16.refs_3_
  99.9 0.9 shard_map.94
  (6 shorter events, 0.0 us)
Async XLA Ops:
  0.7 5.8 %collective-permute-start = (bf16[3,8,512]{2,1,0:T(8,128)(2,1)S(1)}, bf16[3,8,512]{2,1,0:T(8,128)(2,1)S(1)}, u32[]{:S(2)}, u32[]{:S(2)}) collective-permute-start(bf16[3,8,512]{2,1,0:T(8,128)(2,1)S(1)} %slice.4), channel_id=1, source_target_pairs={{0,8},{8,16},{16,24},{24,32},{32,40},{40,48},{48,56},{56,64},{64,7... | collective-permute-start | bytes 73736 | tf_op jit(solution)/shard_map/ppermute | solution.py:307
  8.3 28.1 %all-to-all-start = ((bf16[32,16,512]{2,1,0:T(8,128)(2,1)}), bf16[32,16,512]{2,1,0:T(8,128)(2,1)S(1)}, u32[]{:S(2)}, u32[]{:S(2)}) async-start(bf16[32,16,512]{2,1,0:T(8,128)(2,1)} %bitcast.1), calls=%async_computation | async-start | bytes 1048576 | tf_op jit(solution)/shard_map/all_to_all | solution.py:319
  19.8 7.2 %copy-start.2 = (f32[16384,16]{0,1:T(8,128)S(1)}, f32[16384,16]{0,1:T(8,128)}, u32[]{:S(2)}) copy-start(f32[16384,16]{0,1:T(8,128)} %param.10) | copy-start | bytes 3145732
  19.8 7.2 %copy-start.5 = (bf16[2,256,256]{2,1,0:T(8,128)(2,1)S(1)}, bf16[2,256,256]{2,1,0:T(8,128)(2,1)}, u32[]{:S(2)}) copy-start(bf16[2,256,256]{2,1,0:T(8,128)(2,1)} %constant.9.clone.fwd2_ref.refs_2_) | copy-start | bytes 786436
  19.8 7.2 %copy-start.6 = (bf16[256,256]{1,0:T(8,128)(2,1)S(1)}, bf16[256,256]{1,0:T(8,128)(2,1)}, u32[]{:S(2)}) copy-start(bf16[256,256]{1,0:T(8,128)(2,1)} %constant.8.clone.fwd1_ref.refs_0_) | copy-start | bytes 393220
  19.8 7.2 %copy-start.7 = (f32[2,128,128]{2,1,0:T(8,128)S(1)}, f32[2,128,128]{2,1,0:T(8,128)}, u32[]{:S(2)}) copy-start(f32[2,128,128]{2,1,0:T(8,128)} %constant.11.clone.twist_ref.refs_1_) | copy-start | bytes 393220
  23.1 0.8 copy-start.3
  23.9 26.5 %collective-permute-start.11 = (bf16[4,256,512]{2,1,0:T(8,128)(2,1)}, bf16[4,256,512]{2,1,0:T(8,128)(2,1)}, u32[]{:S(2)}, u32[]{:S(2)}) collective-permute-start(bf16[4,256,512]{2,1,0:T(8,128)(2,1)} %get-tuple-element.48), channel_id=1, source_target_pairs={{0,20},{4,16},{16,4},{20,0},{1,21},{5,17},{17,5},{21,1},{2,22},{6,... | collective-permute-start | bytes 3145736 | tf_op jit(solution)/shard_map/ppermute | solution.py:331
  28.9 1.3 %copy-start.8 = (f32[16,128,256]{2,1,0:T(8,128)}, f32[16,128,256]{2,1,0:T(8,128)S(1)}, u32[]{:S(2)}) copy-start(f32[16,128,256]{2,1,0:T(8,128)S(1)} %shard_map.85.refs_3_) | copy-start | bytes 6291460
  30.2 21.2 %collective-permute-start.4 = (bf16[2,256,512]{2,1,0:T(8,128)(2,1)}, bf16[2,256,512]{2,1,0:T(8,128)(2,1)}, u32[]{:S(2)}, u32[]{:S(2)}) collective-permute-start(bf16[2,256,512]{2,1,0:T(8,128)(2,1)} %get-tuple-element.37), channel_id=1, source_target_pairs={{0,1},{1,2},{2,3},{3,0},{4,5},{5,6},{6,7},{7,4},{8,9},{9,10},{10,1... | collective-permute-start | bytes 1572872 | tf_op jit(solution)/shard_map/ppermute | solution.py:331
  31.5 17.0 %copy-start.4 = (bf16[2,256,512]{2,1,0:T(8,128)(2,1)S(1)}, bf16[2,256,512]{2,1,0:T(8,128)(2,1)}, u32[]{:S(2)}) copy-start(bf16[2,256,512]{2,1,0:T(8,128)(2,1)} %copy-done.3) | copy-start | bytes 1572868
  31.5 31.6 %copy-start.1 = (f32[3,3,512]{2,1,0:T(4,128)S(1)}, f32[3,3,512]{2,1,0:T(4,128)}, u32[]{:S(2)}) copy-start(f32[3,3,512]{2,1,0:T(4,128)} %taps_hbm.1) | copy-start | bytes 55300
  31.5 25.4 %collective-permute-start.6 = (bf16[2,256,512]{2,1,0:T(8,128)(2,1)}, bf16[2,256,512]{2,1,0:T(8,128)(2,1)}, u32[]{:S(2)}, u32[]{:S(2)}) collective-permute-start(bf16[2,256,512]{2,1,0:T(8,128)(2,1)} %get-tuple-element.38), channel_id=1, source_target_pairs={{0,2},{1,3},{2,0},{3,1},{4,6},{5,7},{6,4},{7,5},{8,10},{9,11},{10,... | collective-permute-start | bytes 1572872 | tf_op jit(solution)/shard_map/ppermute | solution.py:331
  36.3 26.7 %copy-start = (bf16[512,3,512]{2,0,1:T(8,128)(2,1)S(1)}, bf16[512,3,512]{2,0,1:T(8,128)(2,1)}, u32[]{:S(2)}) copy-start(bf16[512,3,512]{2,0,1:T(8,128)(2,1)} %param.8) | copy-start | bytes 4718596
  42.9 22.2 %all-to-all-start.1 = ((bf16[32,16,512]{2,1,0:T(8,128)(2,1)}), bf16[32,16,512]{2,1,0:T(8,128)(2,1)S(1)}, u32[]{:S(2)}, u32[]{:S(2)}) async-start(bf16[32,16,512]{2,1,0:T(8,128)(2,1)} %shard_map.86), calls=%async_computation.1 | async-start | bytes 1048576 | tf_op jit(solution)/shard_map/all_to_all | solution.py:341
  48.5 13.4 %collective-permute-start.8 = (bf16[2,256,512]{2,1,0:T(8,128)(2,1)S(1)}, bf16[2,256,512]{2,1,0:T(8,128)(2,1)}, u32[]{:S(2)}, u32[]{:S(2)}) collective-permute-start(bf16[2,256,512]{2,1,0:T(8,128)(2,1)S(1)} %copy-done.4), channel_id=1, source_target_pairs={{0,3},{1,0},{2,1},{3,2},{4,7},{5,4},{6,5},{7,6},{8,11},{9,8},{10,9... | collective-permute-start | bytes 1572872 | tf_op jit(solution)/shard_map/ppermute | solution.py:331
  50.4 24.6 %collective-permute-start.12 = (bf16[4,256,512]{2,1,0:T(8,128)(2,1)}, bf16[4,256,512]{2,1,0:T(8,128)(2,1)}, u32[]{:S(2)}, u32[]{:S(2)}) collective-permute-start(bf16[4,256,512]{2,1,0:T(8,128)(2,1)} %collective-permute-done.11.refs_1_), channel_id=1, source_target_pairs={{0,8},{8,0},{1,9},{9,1},{2,10},{10,2},{3,11},{11,3},{4,12},{12,4},... | collective-permute-start | bytes 3145736 | tf_op jit(solution)/shard_map/ppermute | solution.py:332
  51.4 14.9 %collective-permute-start.5 = (bf16[2,256,512]{2,1,0:T(8,128)(2,1)}, bf16[2,256,512]{2,1,0:T(8,128)(2,1)}, u32[]{:S(2)}, u32[]{:S(2)}) collective-permute-start(bf16[2,256,512]{2,1,0:T(8,128)(2,1)} %collective-permute-done.4.refs_1_), channel_id=1, source_target_pairs={{0,8},{8,0},{1,9},{9,1},{2,10},{10,2},{3,11},{11,3},{4,12},{12,4},... | collective-permute-start | bytes 1572872 | tf_op jit(solution)/shard_map/ppermute | solution.py:332
  56.9 11.9 %collective-permute-start.7 = (bf16[2,256,512]{2,1,0:T(8,128)(2,1)}, bf16[2,256,512]{2,1,0:T(8,128)(2,1)}, u32[]{:S(2)}, u32[]{:S(2)}) collective-permute-start(bf16[2,256,512]{2,1,0:T(8,128)(2,1)} %collective-permute-done.6.refs_3_), channel_id=1, source_target_pairs={{0,8},{8,0},{1,9},{9,1},{2,10},{10,2},{3,11},{11,3},{4,12},{12,4},... | collective-permute-start | bytes 1572872 | tf_op jit(solution)/shard_map/ppermute | solution.py:332
  62.0 8.0 %collective-permute-start.9 = (bf16[2,256,512]{2,1,0:T(8,128)(2,1)}, bf16[2,256,512]{2,1,0:T(8,128)(2,1)}, u32[]{:S(2)}, u32[]{:S(2)}) collective-permute-start(bf16[2,256,512]{2,1,0:T(8,128)(2,1)} %collective-permute-done.8.refs_5_), channel_id=1, source_target_pairs={{0,8},{8,0},{1,9},{9,1},{2,10},{10,2},{3,11},{11,3},{4,12},{12,4},... | collective-permute-start | bytes 1572872 | tf_op jit(solution)/shard_map/ppermute | solution.py:332
  65.3 12.1 %collective-permute-start.1 = (bf16[256,512]{1,0:T(8,128)(2,1)S(1)}, bf16[256,512]{1,0:T(8,128)(2,1)S(1)}, u32[]{:S(2)}, u32[]{:S(2)}) collective-permute-start(bf16[256,512]{1,0:T(8,128)(2,1)S(1)} %get-tuple-element.35.refs_0_), channel_id=1, source_target_pairs={{0,1},{1,2},{2,3},{3,0},{4,5},{5,6},{6,7},{7,4},{8,9},{9,10},{10,1... | collective-permute-start | bytes 786440 | tf_op jit(solution)/shard_map/ppermute | solution.py:347
  66.3 13.1 %collective-permute-start.2 = (bf16[256,512]{1,0:T(8,128)(2,1)S(1)}, bf16[256,512]{1,0:T(8,128)(2,1)S(1)}, u32[]{:S(2)}, u32[]{:S(2)}) collective-permute-start(bf16[256,512]{1,0:T(8,128)(2,1)S(1)} %get-tuple-element.35.refs_0_), channel_id=1, source_target_pairs={{0,2},{1,3},{2,0},{3,1},{4,6},{5,7},{6,4},{7,5},{8,10},{9,11},{10,... | collective-permute-start | bytes 786440 | tf_op jit(solution)/shard_map/ppermute | solution.py:347
  68.8 11.1 %collective-permute-start.3 = (bf16[256,512]{1,0:T(8,128)(2,1)S(1)}, bf16[256,512]{1,0:T(8,128)(2,1)S(1)}, u32[]{:S(2)}, u32[]{:S(2)}) collective-permute-start(bf16[256,512]{1,0:T(8,128)(2,1)S(1)} %get-tuple-element.35.refs_0_), channel_id=1, source_target_pairs={{0,3},{1,0},{2,1},{3,2},{4,7},{5,4},{6,5},{7,6},{8,11},{9,8},{10,9... | collective-permute-start | bytes 786440 | tf_op jit(solution)/shard_map/ppermute | solution.py:347
  69.9 13.3 %collective-permute-start.10 = (bf16[256,512]{1,0:T(8,128)(2,1)S(1)}, bf16[256,512]{1,0:T(8,128)(2,1)S(1)}, u32[]{:S(2)}, u32[]{:S(2)}) collective-permute-start(bf16[256,512]{1,0:T(8,128)(2,1)S(1)} %get-tuple-element.47.refs_11_.refs_0_), channel_id=1, source_target_pairs={{0,4},{4,0},{1,5},{5,1},{2,6},{6,2},{3,7},{7,3},{8,12},{12,8},{9,1... | collective-permute-start | bytes 786440 | tf_op jit(solution)/shard_map/ppermute | solution.py:347
  80.6 9.3 %collective-permute-start.13 = (bf16[256,512]{1,0:T(8,128)(2,1)S(1)}, bf16[256,512]{1,0:T(8,128)(2,1)S(1)}, u32[]{:S(2)}, u32[]{:S(2)}) collective-permute-start(bf16[256,512]{1,0:T(8,128)(2,1)S(1)} %shard_map.92), channel_id=1, source_target_pairs={{0,4},{4,0},{1,5},{5,1},{2,6},{6,2},{3,7},{7,3},{8,12},{12,8},{9,1... | collective-permute-start | bytes 786440 | tf_op jit(solution)/shard_map/ppermute | solution.py:347
  84.2 8.2 %collective-permute-start.14 = (bf16[256,512]{1,0:T(8,128)(2,1)S(1)}, bf16[256,512]{1,0:T(8,128)(2,1)S(1)}, u32[]{:S(2)}, u32[]{:S(2)}) collective-permute-start(bf16[256,512]{1,0:T(8,128)(2,1)S(1)} %get-tuple-element.54), channel_id=1, source_target_pairs={{0,1},{1,2},{2,3},{3,0},{4,5},{5,6},{6,7},{7,4},{8,9},{9,10},{10,1... | collective-permute-start | bytes 786440 | tf_op jit(solution)/shard_map/ppermute | solution.py:347
  86.3 13.5 %collective-permute-start.15 = (bf16[256,512]{1,0:T(8,128)(2,1)S(1)}, bf16[256,512]{1,0:T(8,128)(2,1)S(1)}, u32[]{:S(2)}, u32[]{:S(2)}) collective-permute-start(bf16[256,512]{1,0:T(8,128)(2,1)S(1)} %get-tuple-element.55), channel_id=1, source_target_pairs={{0,2},{1,3},{2,0},{3,1},{4,6},{5,7},{6,4},{7,5},{8,10},{9,11},{10,... | collective-permute-start | bytes 786440 | tf_op jit(solution)/shard_map/ppermute | solution.py:347
  88.9 11.0 %collective-permute-start.16 = (bf16[256,512]{1,0:T(8,128)(2,1)S(1)}, bf16[256,512]{1,0:T(8,128)(2,1)S(1)}, u32[]{:S(2)}, u32[]{:S(2)}) collective-permute-start(bf16[256,512]{1,0:T(8,128)(2,1)S(1)} %get-tuple-element.56), channel_id=1, source_target_pairs={{0,3},{1,0},{2,1},{3,2},{4,7},{5,4},{6,5},{7,6},{8,11},{9,8},{10,9... | collective-permute-start | bytes 786440 | tf_op jit(solution)/shard_map/ppermute | solution.py:347

commit v6 on v5

--- a/solution.py
+++ b/solution.py
@@ -11,6 +11,7 @@
 SIDE = 128
 LENGTH = SIDE * SIDE
 EDGE = 8
+GROUPS = 4
 LIMIT = 16 * 2**20
 f32, bf16 = jnp.float32, jnp.bfloat16
 
@@ -93,27 +94,39 @@
         for q in range(per):
             n = i * per + q
             rows[n * channels : (n + 1) * channels, :] = u_ref[i, :, q * SIDE : (q + 1) * SIDE].astype(f32)
-    group = jnp.concatenate([rows[pl.ds(w, SIDE, stride=channels), :] for w in range(channels)], 1).astype(bf16)
+    size = channels // GROUPS
+    groups = [range(g * size, (g + 1) * size) for g in range(GROUPS)]
+    signals = [
+        jnp.concatenate([rows[pl.ds(w, SIDE, stride=channels), :] for w in group], 1).astype(bf16) for group in groups
+    ]
     for c in copies[:3]:
         c.wait()
-    first = mm(fwd1_ref[...], jnp.concatenate([group, group], 0))
-    spectra = right3(stacked(first, twist_ref), fwd2_ref)
+    firsts = [mm(fwd1_ref[...], jnp.concatenate([x, x], 0)) for x in signals]
+    turned = [stacked(first, twist_ref) for first in firsts]
+    spectra = [right3(x, fwd2_ref) for x in turned]
     for c in copies[3:]:
         c.wait()
     products = []
-    for w in range(channels):
-        s, h = spectra[w * SIDE : (w + 1) * SIDE], h_ref[w]
-        sr, si, hr, hi = s[:, :SIDE], s[:, SIDE:], h[:, :SIDE], h[:, SIDE:]
-        products.append(jnp.concatenate([sr * hr - si * hi, -(sr * hi + si * hr)], 1))
-    b = right3(jnp.concatenate(products, 0), fwd2_ref)
+    for group, spectrum in zip(groups, spectra):
+        parts = []
+        for w, channel in enumerate(group):
+            s, h = spectrum[w * SIDE : (w + 1) * SIDE], h_ref[channel]
+            sr, si, hr, hi = s[:, :SIDE], s[:, SIDE:], h[:, :SIDE], h[:, SIDE:]
+            parts.append(jnp.concatenate([sr * hr - si * hi, -(sr * hi + si * hr)], 1))
+        products.append(jnp.concatenate(parts, 0))
     tc, ts = twist_ref[0], twist_ref[1]
-    turned = []
-    for w in range(channels):
-        br, bi = b[w * SIDE : (w + 1) * SIDE, :SIDE], b[w * SIDE : (w + 1) * SIDE, SIDE:]
-        turned.append(jnp.concatenate([br * tc - bi * ts, -(bi * tc + br * ts)], 0))
-    y = left3(inv2_ref, jnp.concatenate(turned, 1))
-    for w in range(channels):
-        back[pl.ds(w, SIDE, stride=channels), :] = y[:, w * SIDE : (w + 1) * SIDE]
+    backs = [right3(x, fwd2_ref) for x in products]
+    results = []
+    for b in backs:
+        parts = []
+        for w in range(size):
+            br, bi = b[w * SIDE : (w + 1) * SIDE, :SIDE], b[w * SIDE : (w + 1) * SIDE, SIDE:]
+            parts.append(jnp.concatenate([br * tc - bi * ts, -(bi * tc + br * ts)], 0))
+        results.append(jnp.concatenate(parts, 1))
+    results = [left3(inv2_ref, x) for x in results]
+    for group, y in zip(groups, results):
+        for w, channel in enumerate(group):
+            back[pl.ds(channel, SIDE, stride=channels), :] = y[:, w * SIDE : (w + 1) * SIDE]
     outs = []
     for i in range(blocks):
         for q in range(per):

time: 101 us -> 99.9 us (0.989)
  Pallas kernels: 23.5 us -> 22.2 us
    pallas_call x13, Pallas kernels: 23.5 us -> 22.2 us  [call(): pl.pallas_call(kernel, out_shape=shapes, in_specs=specs, out_specs=[outs_...]
  transfers between devices with their start and end apart: 19 -> 19, of which waited for: 9 -> 9; matrix products, arithmetic and copies ran while one was open for 0% -> 0% of each run, Pallas kernels for 21% -> 20%
where the time goes in v6:
time: 99.9 us; the launch traced here: 99.5 us
  starting transfers between devices  48.7 us (49%)
  waiting for transfers between devices  25.5 us (26%)
  Pallas kernels  22.2 us (22%)
  local copies, waits for them, and re-layouts  2.91 us (3%)
    pallas_call x13, Pallas kernels, call(): pl.pallas_call(kernel, out_shape=shapes, in_specs=specs, out_specs=[outs_...  22.2 us
    ppermute x8, starting transfers between devices, send(): return lax.ppermute(block, axis, ring(axis, shift))  14.8 us
    ppermute x8, waiting for transfers between devices, send(): return lax.ppermute(block, axis, ring(axis, shift))  12.5 us
    all_to_all x1, starting transfers between devices, body(): signal = lax.all_to_all(gated_in.reshape(ctx, mine, tokens), CTX, 0, 0)  11.5 us
    ppermute x4, waiting for transfers between devices, swapped(): came = lax.ppermute(block, axis, route)  9.12 us
    ppermute x4, starting transfers between devices, swapped(): came = lax.ppermute(block, axis, route)  8.61 us
    all_to_all x1, starting transfers between devices, body(): returned = lax.all_to_all(convolved, CTX, 0, 0).reshape(width, tokens)  5.61 us
    ppermute x1, starting transfers between devices, body(): lax.ppermute(streams_first[:, tokens - EDGE:, :], CTX, [(i, i + 1) for i...  4.57 us
  transfers between devices with their start and end apart: 19, of which 9 were waited for; matrix products, arithmetic and copies ran while one was open for 0% of the time, Pallas kernels for 20%

profile of v6, /device:TPU:1, one launch (start us, length us, event | category | flops | bytes accessed | tf_op | source)
XLA Modules:
  0.0 99.5 jit_solution(171094039455181509)
XLA Ops:
  0.0 0.7 slice.4
  0.7 4.6 %collective-permute-start = (bf16[3,8,512]{2,1,0:T(8,128)(2,1)S(1)}, bf16[3,8,512]{2,1,0:T(8,128)(2,1)S(1)}, u32[]{:S(2)}, u32[]{:S(2)}) collective-permute-start(bf16[3,8,512]{2,1,0:T(8,128)(2,1)S(1)} %slice.4), channel_id=1, source_target_pairs={{0,8},{8,16},{16,24},{24,32},{32,40},{40,48},{48,56},{56,64},{64,7... | collective-permute-start | bytes 73736 | tf_op jit(solution)/shard_map/ppermute | solution.py:320
  5.3 1.2 %shard_map.83 = (bf16[512,512]{1,0:T(8,128)(2,1)S(1)}, bf16[512,512]{1,0:T(8,128)(2,1)S(1)}, f32[3,3,512]{2,1,0:T(4,128)S(1)}) custom-call(bf16[3,512,512]{2,1,0:T(8,128)(2,1)} %bitcast.5, f32[3,3,512]{2,1,0:T(4,128)} %taps_hbm.1), custom_call_target="tpu_custom_call" | custom-call | bytes 1591296 | tf_op jit(solution)/shard_map/pallas_call | solution.py:281
  6.6 0.0 collective-permute-done.edge_ref
  6.6 1.7 %shard_map.84 = bf16[512,512]{1,0:T(8,128)(2,1)} custom-call(bf16[3,8,512]{2,1,0:T(8,128)(2,1)S(1)} %collective-permute-done.edge_ref, bf16[512,512]{1,0:T(8,128)(2,1)S(1)} %get-tuple-element.31.keys_ref, bf16[512,512]{1,0:T(8,128)(2,1)S(1)} %get-tuple-element.32.values_ref, f32[3,3,512]{2,1,0:T(4,128)S(1)} %get-tuple-element.33.taps_ref), custom_call_target="tpu_custom_call" | custom-call | bytes 1091584 | tf_op jit(solution)/shard_map/pallas_call | solution.py:281
  8.3 11.5 %all-to-all-start = ((bf16[32,16,512]{2,1,0:T(8,128)(2,1)}), bf16[32,16,512]{2,1,0:T(8,128)(2,1)S(1)}, u32[]{:S(2)}, u32[]{:S(2)}) async-start(bf16[32,16,512]{2,1,0:T(8,128)(2,1)} %bitcast.1), calls=%async_computation | async-start | bytes 1048576 | tf_op jit(solution)/shard_map/all_to_all | solution.py:332
  19.8 0.0 copy-start.2
  19.8 0.0 copy-start.5
  19.8 0.0 copy-start.6
  19.8 0.0 copy-start.7
  19.8 3.2 %shard_map.88 = (bf16[2,256,512]{2,1,0:T(8,128)(2,1)}, bf16[2,256,512]{2,1,0:T(8,128)(2,1)}, bf16[2,256,512]{2,1,0:T(8,128)(2,1)S(1)}, bf16[4,256,512]{2,1,0:T(8,128)(2,1)}) custom-call(bf16[512,4096]{1,0:T(8,128)(2,1)} %refs_0_.3), custom_call_target="tpu_custom_call" | custom-call | bytes 4194304 | tf_op jit(solution)/shard_map/pallas_call | solution.py:281
  23.1 0.0 copy-start.3
  23.1 0.8 copy-done.3
  23.9 3.1 %collective-permute-start.11 = (bf16[4,256,512]{2,1,0:T(8,128)(2,1)}, bf16[4,256,512]{2,1,0:T(8,128)(2,1)}, u32[]{:S(2)}, u32[]{:S(2)}) collective-permute-start(bf16[4,256,512]{2,1,0:T(8,128)(2,1)} %get-tuple-element.48), channel_id=1, source_target_pairs={{0,20},{4,16},{16,4},{20,0},{1,21},{5,17},{17,5},{21,1},{2,22},{6,... | collective-permute-start | bytes 3145736 | tf_op jit(solution)/shard_map/ppermute | solution.py:344
  27.0 0.0 copy-done.2
  27.0 0.0 copy-done.5
  27.0 0.0 copy-done.6
  27.0 0.0 copy-done.7
  27.0 1.9 %shard_map.85.refs_3_ = f32[16,128,256]{2,1,0:T(8,128)S(1)} custom-call(f32[16,16384]{1,0:T(8,128)S(1)} %bitcast.8, bf16[256,256]{1,0:T(8,128)(2,1)S(1)} %copy-done.6, bf16[2,256,256]{2,1,0:T(8,128)(2,1)S(1)} %copy-done.5, f32[2,128,128]{2,1,0:T(8,128)S(1)} %copy-done.7), custom_call_target="tpu_custom_call" | custom-call | flops 1000000000 | bytes 1572864 | tf_op jit(solution)/shard_map/pallas_call | solution.py:281
  28.9 0.0 copy-start.8
  28.9 1.3 %copy-done.8 = f32[16,128,256]{2,1,0:T(8,128)} copy-done((f32[16,128,256]{2,1,0:T(8,128)}, f32[16,128,256]{2,1,0:T(8,128)S(1)}, u32[]{:S(2)}) %copy-start.8) | copy-done | bytes 2097176
  30.2 1.2 %collective-permute-start.4 = (bf16[2,256,512]{2,1,0:T(8,128)(2,1)}, bf16[2,256,512]{2,1,0:T(8,128)(2,1)}, u32[]{:S(2)}, u32[]{:S(2)}) collective-permute-start(bf16[2,256,512]{2,1,0:T(8,128)(2,1)} %get-tuple-element.37), channel_id=1, source_target_pairs={{0,1},{1,2},{2,3},{3,0},{4,5},{5,6},{6,7},{7,4},{8,9},{9,10},{10,1... | collective-permute-start | bytes 1572872 | tf_op jit(solution)/shard_map/ppermute | solution.py:344
  31.5 2.5 %collective-permute-start.6 = (bf16[2,256,512]{2,1,0:T(8,128)(2,1)}, bf16[2,256,512]{2,1,0:T(8,128)(2,1)}, u32[]{:S(2)}, u32[]{:S(2)}) collective-permute-start(bf16[2,256,512]{2,1,0:T(8,128)(2,1)} %get-tuple-element.38), channel_id=1, source_target_pairs={{0,2},{1,3},{2,0},{3,1},{4,6},{5,7},{6,4},{7,5},{8,10},{9,11},{10,... | collective-permute-start | bytes 1572872 | tf_op jit(solution)/shard_map/ppermute | solution.py:344
  33.9 2.4 %all-to-all-done.u_ref = bf16[32,16,512]{2,1,0:T(8,128)(2,1)S(1)} async-done(((bf16[32,16,512]{2,1,0:T(8,128)(2,1)}), bf16[32,16,512]{2,1,0:T(8,128)(2,1)S(1)}, u32[]{:S(2)}, u32[]{:S(2)}) %all-to-all-start) | async-done | bytes 524320 | tf_op jit(solution)/shard_map/all_to_all | solution.py:332
  36.3 5.3 %shard_map.86 = bf16[32,16,512]{2,1,0:T(8,128)(2,1)} custom-call(bf16[32,16,512]{2,1,0:T(8,128)(2,1)S(1)} %all-to-all-done.u_ref, bf16[256,256]{1,0:T(8,128)(2,1)} %constant.8.clone.fwd1_ref.refs_0_, f32[2,128,128]{2,1,0:T(8,128)} %constant.11.clone.twist_ref.refs_1_, bf16[2,256,256]{2,1,0:T(8,128)(2,1)} %constant.9.clone.fwd2_ref.refs_2_, ...), custom_call_target="tpu_custom_call" | custom-call | flops 3000000000 | bytes 3276800 | tf_op jit(solution)/shard_map/pallas_call | solution.py:281
  41.6 5.6 %all-to-all-start.1 = ((bf16[32,16,512]{2,1,0:T(8,128)(2,1)}), bf16[32,16,512]{2,1,0:T(8,128)(2,1)S(1)}, u32[]{:S(2)}, u32[]{:S(2)}) async-start(bf16[32,16,512]{2,1,0:T(8,128)(2,1)} %shard_map.86), calls=%async_computation.1 | async-start | bytes 1048576 | tf_op jit(solution)/shard_map/all_to_all | solution.py:354
  47.2 1.8 %collective-permute-start.8 = (bf16[2,256,512]{2,1,0:T(8,128)(2,1)S(1)}, bf16[2,256,512]{2,1,0:T(8,128)(2,1)}, u32[]{:S(2)}, u32[]{:S(2)}) collective-permute-start(bf16[2,256,512]{2,1,0:T(8,128)(2,1)S(1)} %copy-done.4), channel_id=1, source_target_pairs={{0,3},{1,0},{2,1},{3,2},{4,7},{5,4},{6,5},{7,6},{8,11},{9,8},{10,9... | collective-permute-start | bytes 1572872 | tf_op jit(solution)/shard_map/ppermute | solution.py:344
  49.1 1.4 %collective-permute-done.11.refs_1_ = bf16[4,256,512]{2,1,0:T(8,128)(2,1)} collective-permute-done((bf16[4,256,512]{2,1,0:T(8,128)(2,1)}, bf16[4,256,512]{2,1,0:T(8,128)(2,1)}, u32[]{:S(2)}, u32[]{:S(2)}) %collective-permute-start.11) | collective-permute-done | bytes 1048608 | tf_op jit(solution)/shard_map/ppermute | solution.py:344
  50.4 1.0 collective-permute-start.12
  51.4 0.0 collective-permute-done.4.refs_1_
  51.4 0.0 collective-permute-start.5
  51.4 5.4 %collective-permute-done.6.refs_3_ = bf16[2,256,512]{2,1,0:T(8,128)(2,1)} collective-permute-done((bf16[2,256,512]{2,1,0:T(8,128)(2,1)}, bf16[2,256,512]{2,1,0:T(8,128)(2,1)}, u32[]{:S(2)}, u32[]{:S(2)}) %collective-permute-start.6) | collective-permute-done | bytes 524320 | tf_op jit(solution)/shard_map/ppermute | solution.py:344
  56.9 1.5 %collective-permute-start.7 = (bf16[2,256,512]{2,1,0:T(8,128)(2,1)}, bf16[2,256,512]{2,1,0:T(8,128)(2,1)}, u32[]{:S(2)}, u32[]{:S(2)}) collective-permute-start(bf16[2,256,512]{2,1,0:T(8,128)(2,1)} %collective-permute-done.6.refs_3_), channel_id=1, source_target_pairs={{0,8},{8,0},{1,9},{9,1},{2,10},{10,2},{3,11},{11,3},{4,12},{12,4},... | collective-permute-start | bytes 1572872 | tf_op jit(solution)/shard_map/ppermute | solution.py:345
  58.3 2.3 %collective-permute-done.8.refs_5_ = bf16[2,256,512]{2,1,0:T(8,128)(2,1)} collective-permute-done((bf16[2,256,512]{2,1,0:T(8,128)(2,1)S(1)}, bf16[2,256,512]{2,1,0:T(8,128)(2,1)}, u32[]{:S(2)}, u32[]{:S(2)}) %collective-permute-start.8) | collective-permute-done | bytes 524320 | tf_op jit(solution)/shard_map/ppermute | solution.py:344
  60.7 1.1 %collective-permute-start.9 = (bf16[2,256,512]{2,1,0:T(8,128)(2,1)}, bf16[2,256,512]{2,1,0:T(8,128)(2,1)}, u32[]{:S(2)}, u32[]{:S(2)}) collective-permute-start(bf16[2,256,512]{2,1,0:T(8,128)(2,1)} %collective-permute-done.8.refs_5_), channel_id=1, source_target_pairs={{0,8},{8,0},{1,9},{9,1},{2,10},{10,2},{3,11},{11,3},{4,12},{12,4},... | collective-permute-start | bytes 1572872 | tf_op jit(solution)/shard_map/ppermute | solution.py:345
  61.8 0.6 shard_map.82.query_ref
  62.4 1.4 %all-to-all-done.1 = bf16[32,16,512]{2,1,0:T(8,128)(2,1)S(1)} async-done(((bf16[32,16,512]{2,1,0:T(8,128)(2,1)}), bf16[32,16,512]{2,1,0:T(8,128)(2,1)S(1)}, u32[]{:S(2)}, u32[]{:S(2)}) %all-to-all-start.1) | async-done | bytes 524320 | tf_op jit(solution)/shard_map/all_to_all | solution.py:354
  63.8 0.2 shard_map.87
  64.0 1.0 %collective-permute-start.1 = (bf16[256,512]{1,0:T(8,128)(2,1)S(1)}, bf16[256,512]{1,0:T(8,128)(2,1)S(1)}, u32[]{:S(2)}, u32[]{:S(2)}) collective-permute-start(bf16[256,512]{1,0:T(8,128)(2,1)S(1)} %get-tuple-element.35.refs_0_), channel_id=1, source_target_pairs={{0,1},{1,2},{2,3},{3,0},{4,5},{5,6},{6,7},{7,4},{8,9},{9,10},{10,1... | collective-permute-start | bytes 786440 | tf_op jit(solution)/shard_map/ppermute | solution.py:360
  65.0 0.0 collective-permute-done.5.refs_2_
  65.0 2.5 %collective-permute-start.2 = (bf16[256,512]{1,0:T(8,128)(2,1)S(1)}, bf16[256,512]{1,0:T(8,128)(2,1)S(1)}, u32[]{:S(2)}, u32[]{:S(2)}) collective-permute-start(bf16[256,512]{1,0:T(8,128)(2,1)S(1)} %get-tuple-element.35.refs_0_), channel_id=1, source_target_pairs={{0,2},{1,3},{2,0},{3,1},{4,6},{5,7},{6,4},{7,5},{8,10},{9,11},{10,... | collective-permute-start | bytes 786440 | tf_op jit(solution)/shard_map/ppermute | solution.py:360
  67.5 0.0 collective-permute-done.7.refs_4_
  67.5 1.2 %collective-permute-start.3 = (bf16[256,512]{1,0:T(8,128)(2,1)S(1)}, bf16[256,512]{1,0:T(8,128)(2,1)S(1)}, u32[]{:S(2)}, u32[]{:S(2)}) collective-permute-start(bf16[256,512]{1,0:T(8,128)(2,1)S(1)} %get-tuple-element.35.refs_0_), channel_id=1, source_target_pairs={{0,3},{1,0},{2,1},{3,2},{4,7},{5,4},{6,5},{7,6},{8,11},{9,8},{10,9... | collective-permute-start | bytes 786440 | tf_op jit(solution)/shard_map/ppermute | solution.py:360
  68.6 0.0 collective-permute-done.9.refs_6_
  68.6 2.9 %collective-permute-start.10 = (bf16[256,512]{1,0:T(8,128)(2,1)S(1)}, bf16[256,512]{1,0:T(8,128)(2,1)S(1)}, u32[]{:S(2)}, u32[]{:S(2)}) collective-permute-start(bf16[256,512]{1,0:T(8,128)(2,1)S(1)} %get-tuple-element.47.refs_11_.refs_0_), channel_id=1, source_target_pairs={{0,4},{4,0},{1,5},{5,1},{2,6},{6,2},{3,7},{7,3},{8,12},{12,8},{9,1... | collective-permute-start | bytes 786440 | tf_op jit(solution)/shard_map/ppermute | solution.py:360
  71.6 2.2 %shard_map.89 = (bf16[2,512,512]{2,1,0:T(8,128)(2,1)S(1)}, bf16[2,256,512]{2,1,0:T(8,128)(2,1)S(1)}, bf16[2,256,512]{2,1,0:T(8,128)(2,1)S(1)}, bf16[2,256,512]{2...) custom-call(bf16[512,4096]{1,0:T(8,128)(2,1)} %refs_0_.3, ...), custom_call_target="tpu_custom_call" | custom-call | bytes 7340032 | tf_op jit(solution)/shard_map/pallas_call | solution.py:281
  73.8 0.0 collective-permute-done.12.refs_2_
  73.8 2.3 %shard_map.90 = (bf16[4,512,512]{2,1,0:T(8,128)(2,1)S(1)}, bf16[4,256,512]{2,1,0:T(8,128)(2,1)S(1)}, bf16[4,256,512]{2,1,0:T(8,128)(2,1)S(1)}) custom-call(bf16[512,4096]{1,0:T(8,128)(2,1)} %refs_0_.3, bf16[4,256,512]{2,1,0:T(8,128)(2,1)} %collective-permute-done.11.refs_1_, bf16[4,256,512]{2,1,0:T(8,128)(2,1)} %collective-permute-done.12.refs_2_), custom_call_target="tpu_custom_call" | custom-call | bytes 6291456 | tf_op jit(solution)/shard_map/pallas_call | solution.py:281
  76.1 0.0 collective-permute-done.1.refs_1_
  76.1 2.1 %collective-permute-done.2.refs_2_ = bf16[256,512]{1,0:T(8,128)(2,1)S(1)} collective-permute-done((bf16[256,512]{1,0:T(8,128)(2,1)S(1)}, bf16[256,512]{1,0:T(8,128)(2,1)S(1)}, u32[]{:S(2)}, u32[]{:S(2)}) %collective-permute-start.2) | collective-permute-done | bytes 262176 | tf_op jit(solution)/shard_map/ppermute | solution.py:360
  78.2 0.4 collective-permute-done.3.refs_3_
  78.6 0.7 shard_map.92
  79.3 2.6 %collective-permute-start.13 = (bf16[256,512]{1,0:T(8,128)(2,1)S(1)}, bf16[256,512]{1,0:T(8,128)(2,1)S(1)}, u32[]{:S(2)}, u32[]{:S(2)}) collective-permute-start(bf16[256,512]{1,0:T(8,128)(2,1)S(1)} %shard_map.92), channel_id=1, source_target_pairs={{0,4},{4,0},{1,5},{5,1},{2,6},{6,2},{3,7},{7,3},{8,12},{12,8},{9,1... | collective-permute-start | bytes 786440 | tf_op jit(solution)/shard_map/ppermute | solution.py:360
  81.9 0.0 collective-permute-done.10.refs_12_.refs_1_
  81.9 1.0 shard_map.93
  82.9 2.1 %collective-permute-start.14 = (bf16[256,512]{1,0:T(8,128)(2,1)S(1)}, bf16[256,512]{1,0:T(8,128)(2,1)S(1)}, u32[]{:S(2)}, u32[]{:S(2)}) collective-permute-start(bf16[256,512]{1,0:T(8,128)(2,1)S(1)} %get-tuple-element.54), channel_id=1, source_target_pairs={{0,1},{1,2},{2,3},{3,0},{4,5},{5,6},{6,7},{7,4},{8,9},{9,10},{10,1... | collective-permute-start | bytes 786440 | tf_op jit(solution)/shard_map/ppermute | solution.py:360
  85.0 2.5 %collective-permute-start.15 = (bf16[256,512]{1,0:T(8,128)(2,1)S(1)}, bf16[256,512]{1,0:T(8,128)(2,1)S(1)}, u32[]{:S(2)}, u32[]{:S(2)}) collective-permute-start(bf16[256,512]{1,0:T(8,128)(2,1)S(1)} %get-tuple-element.55), channel_id=1, source_target_pairs={{0,2},{1,3},{2,0},{3,1},{4,6},{5,7},{6,4},{7,5},{8,10},{9,11},{10,... | collective-permute-start | bytes 786440 | tf_op jit(solution)/shard_map/ppermute | solution.py:360
  87.6 0.0 collective-permute-start.16
  87.6 1.0 shard_map.91
  88.6 0.0 collective-permute-done.13.refs_0_
  88.6 2.5 %collective-permute-done.14.refs_1_ = bf16[256,512]{1,0:T(8,128)(2,1)S(1)} collective-permute-done((bf16[256,512]{1,0:T(8,128)(2,1)S(1)}, bf16[256,512]{1,0:T(8,128)(2,1)S(1)}, u32[]{:S(2)}, u32[]{:S(2)}) %collective-permute-start.14) | collective-permute-done | bytes 262176 | tf_op jit(solution)/shard_map/ppermute | solution.py:360
  91.1 7.5 %collective-permute-done.15.refs_2_ = bf16[256,512]{1,0:T(8,128)(2,1)S(1)} collective-permute-done((bf16[256,512]{1,0:T(8,128)(2,1)S(1)}, bf16[256,512]{1,0:T(8,128)(2,1)S(1)}, u32[]{:S(2)}, u32[]{:S(2)}) %collective-permute-start.15) | collective-permute-done | bytes 262176 | tf_op jit(solution)/shard_map/ppermute | solution.py:360
  98.6 0.0 collective-permute-done.16.refs_3_
  98.6 0.9 shard_map.94
  (6 shorter events, 0.0 us)
Async XLA Ops:
  0.7 5.8 %collective-permute-start = (bf16[3,8,512]{2,1,0:T(8,128)(2,1)S(1)}, bf16[3,8,512]{2,1,0:T(8,128)(2,1)S(1)}, u32[]{:S(2)}, u32[]{:S(2)}) collective-permute-start(bf16[3,8,512]{2,1,0:T(8,128)(2,1)S(1)} %slice.4), channel_id=1, source_target_pairs={{0,8},{8,16},{16,24},{24,32},{32,40},{40,48},{48,56},{56,64},{64,7... | collective-permute-start | bytes 73736 | tf_op jit(solution)/shard_map/ppermute | solution.py:320
  8.3 28.1 %all-to-all-start = ((bf16[32,16,512]{2,1,0:T(8,128)(2,1)}), bf16[32,16,512]{2,1,0:T(8,128)(2,1)S(1)}, u32[]{:S(2)}, u32[]{:S(2)}) async-start(bf16[32,16,512]{2,1,0:T(8,128)(2,1)} %bitcast.1), calls=%async_computation | async-start | bytes 1048576 | tf_op jit(solution)/shard_map/all_to_all | solution.py:332
  19.8 7.2 %copy-start.2 = (f32[16384,16]{0,1:T(8,128)S(1)}, f32[16384,16]{0,1:T(8,128)}, u32[]{:S(2)}) copy-start(f32[16384,16]{0,1:T(8,128)} %param.10) | copy-start | bytes 3145732
  19.8 7.2 %copy-start.5 = (bf16[2,256,256]{2,1,0:T(8,128)(2,1)S(1)}, bf16[2,256,256]{2,1,0:T(8,128)(2,1)}, u32[]{:S(2)}) copy-start(bf16[2,256,256]{2,1,0:T(8,128)(2,1)} %constant.9.clone.fwd2_ref.refs_2_) | copy-start | bytes 786436
  19.8 7.2 %copy-start.6 = (bf16[256,256]{1,0:T(8,128)(2,1)S(1)}, bf16[256,256]{1,0:T(8,128)(2,1)}, u32[]{:S(2)}) copy-start(bf16[256,256]{1,0:T(8,128)(2,1)} %constant.8.clone.fwd1_ref.refs_0_) | copy-start | bytes 393220
  19.8 7.2 %copy-start.7 = (f32[2,128,128]{2,1,0:T(8,128)S(1)}, f32[2,128,128]{2,1,0:T(8,128)}, u32[]{:S(2)}) copy-start(f32[2,128,128]{2,1,0:T(8,128)} %constant.11.clone.twist_ref.refs_1_) | copy-start | bytes 393220
  23.1 0.8 copy-start.3
  23.9 26.5 %collective-permute-start.11 = (bf16[4,256,512]{2,1,0:T(8,128)(2,1)}, bf16[4,256,512]{2,1,0:T(8,128)(2,1)}, u32[]{:S(2)}, u32[]{:S(2)}) collective-permute-start(bf16[4,256,512]{2,1,0:T(8,128)(2,1)} %get-tuple-element.48), channel_id=1, source_target_pairs={{0,20},{4,16},{16,4},{20,0},{1,21},{5,17},{17,5},{21,1},{2,22},{6,... | collective-permute-start | bytes 3145736 | tf_op jit(solution)/shard_map/ppermute | solution.py:344
  28.9 1.3 %copy-start.8 = (f32[16,128,256]{2,1,0:T(8,128)}, f32[16,128,256]{2,1,0:T(8,128)S(1)}, u32[]{:S(2)}) copy-start(f32[16,128,256]{2,1,0:T(8,128)S(1)} %shard_map.85.refs_3_) | copy-start | bytes 6291460
  30.2 21.2 %collective-permute-start.4 = (bf16[2,256,512]{2,1,0:T(8,128)(2,1)}, bf16[2,256,512]{2,1,0:T(8,128)(2,1)}, u32[]{:S(2)}, u32[]{:S(2)}) collective-permute-start(bf16[2,256,512]{2,1,0:T(8,128)(2,1)} %get-tuple-element.37), channel_id=1, source_target_pairs={{0,1},{1,2},{2,3},{3,0},{4,5},{5,6},{6,7},{7,4},{8,9},{9,10},{10,1... | collective-permute-start | bytes 1572872 | tf_op jit(solution)/shard_map/ppermute | solution.py:344
  31.5 15.8 %copy-start.4 = (bf16[2,256,512]{2,1,0:T(8,128)(2,1)S(1)}, bf16[2,256,512]{2,1,0:T(8,128)(2,1)}, u32[]{:S(2)}) copy-start(bf16[2,256,512]{2,1,0:T(8,128)(2,1)} %copy-done.3) | copy-start | bytes 1572868
  31.5 30.3 %copy-start.1 = (f32[3,3,512]{2,1,0:T(4,128)S(1)}, f32[3,3,512]{2,1,0:T(4,128)}, u32[]{:S(2)}) copy-start(f32[3,3,512]{2,1,0:T(4,128)} %taps_hbm.1) | copy-start | bytes 55300
  31.5 25.4 %collective-permute-start.6 = (bf16[2,256,512]{2,1,0:T(8,128)(2,1)}, bf16[2,256,512]{2,1,0:T(8,128)(2,1)}, u32[]{:S(2)}, u32[]{:S(2)}) collective-permute-start(bf16[2,256,512]{2,1,0:T(8,128)(2,1)} %get-tuple-element.38), channel_id=1, source_target_pairs={{0,2},{1,3},{2,0},{3,1},{4,6},{5,7},{6,4},{7,5},{8,10},{9,11},{10,... | collective-permute-start | bytes 1572872 | tf_op jit(solution)/shard_map/ppermute | solution.py:344
  36.3 25.4 %copy-start = (bf16[512,3,512]{2,0,1:T(8,128)(2,1)S(1)}, bf16[512,3,512]{2,0,1:T(8,128)(2,1)}, u32[]{:S(2)}) copy-start(bf16[512,3,512]{2,0,1:T(8,128)(2,1)} %param.8) | copy-start | bytes 4718596
  41.6 22.2 %all-to-all-start.1 = ((bf16[32,16,512]{2,1,0:T(8,128)(2,1)}), bf16[32,16,512]{2,1,0:T(8,128)(2,1)S(1)}, u32[]{:S(2)}, u32[]{:S(2)}) async-start(bf16[32,16,512]{2,1,0:T(8,128)(2,1)} %shard_map.86), calls=%async_computation.1 | async-start | bytes 1048576 | tf_op jit(solution)/shard_map/all_to_all | solution.py:354
  47.2 13.4 %collective-permute-start.8 = (bf16[2,256,512]{2,1,0:T(8,128)(2,1)S(1)}, bf16[2,256,512]{2,1,0:T(8,128)(2,1)}, u32[]{:S(2)}, u32[]{:S(2)}) collective-permute-start(bf16[2,256,512]{2,1,0:T(8,128)(2,1)S(1)} %copy-done.4), channel_id=1, source_target_pairs={{0,3},{1,0},{2,1},{3,2},{4,7},{5,4},{6,5},{7,6},{8,11},{9,8},{10,9... | collective-permute-start | bytes 1572872 | tf_op jit(solution)/shard_map/ppermute | solution.py:344
  50.4 23.4 %collective-permute-start.12 = (bf16[4,256,512]{2,1,0:T(8,128)(2,1)}, bf16[4,256,512]{2,1,0:T(8,128)(2,1)}, u32[]{:S(2)}, u32[]{:S(2)}) collective-permute-start(bf16[4,256,512]{2,1,0:T(8,128)(2,1)} %collective-permute-done.11.refs_1_), channel_id=1, source_target_pairs={{0,8},{8,0},{1,9},{9,1},{2,10},{10,2},{3,11},{11,3},{4,12},{12,4},... | collective-permute-start | bytes 3145736 | tf_op jit(solution)/shard_map/ppermute | solution.py:345
  51.4 13.6 %collective-permute-start.5 = (bf16[2,256,512]{2,1,0:T(8,128)(2,1)}, bf16[2,256,512]{2,1,0:T(8,128)(2,1)}, u32[]{:S(2)}, u32[]{:S(2)}) collective-permute-start(bf16[2,256,512]{2,1,0:T(8,128)(2,1)} %collective-permute-done.4.refs_1_), channel_id=1, source_target_pairs={{0,8},{8,0},{1,9},{9,1},{2,10},{10,2},{3,11},{11,3},{4,12},{12,4},... | collective-permute-start | bytes 1572872 | tf_op jit(solution)/shard_map/ppermute | solution.py:345
  56.9 10.6 %collective-permute-start.7 = (bf16[2,256,512]{2,1,0:T(8,128)(2,1)}, bf16[2,256,512]{2,1,0:T(8,128)(2,1)}, u32[]{:S(2)}, u32[]{:S(2)}) collective-permute-start(bf16[2,256,512]{2,1,0:T(8,128)(2,1)} %collective-permute-done.6.refs_3_), channel_id=1, source_target_pairs={{0,8},{8,0},{1,9},{9,1},{2,10},{10,2},{3,11},{11,3},{4,12},{12,4},... | collective-permute-start | bytes 1572872 | tf_op jit(solution)/shard_map/ppermute | solution.py:345
  60.7 8.0 %collective-permute-start.9 = (bf16[2,256,512]{2,1,0:T(8,128)(2,1)}, bf16[2,256,512]{2,1,0:T(8,128)(2,1)}, u32[]{:S(2)}, u32[]{:S(2)}) collective-permute-start(bf16[2,256,512]{2,1,0:T(8,128)(2,1)} %collective-permute-done.8.refs_5_), channel_id=1, source_target_pairs={{0,8},{8,0},{1,9},{9,1},{2,10},{10,2},{3,11},{11,3},{4,12},{12,4},... | collective-permute-start | bytes 1572872 | tf_op jit(solution)/shard_map/ppermute | solution.py:345
  64.0 12.1 %collective-permute-start.1 = (bf16[256,512]{1,0:T(8,128)(2,1)S(1)}, bf16[256,512]{1,0:T(8,128)(2,1)S(1)}, u32[]{:S(2)}, u32[]{:S(2)}) collective-permute-start(bf16[256,512]{1,0:T(8,128)(2,1)S(1)} %get-tuple-element.35.refs_0_), channel_id=1, source_target_pairs={{0,1},{1,2},{2,3},{3,0},{4,5},{5,6},{6,7},{7,4},{8,9},{9,10},{10,1... | collective-permute-start | bytes 786440 | tf_op jit(solution)/shard_map/ppermute | solution.py:360
  65.0 13.1 %collective-permute-start.2 = (bf16[256,512]{1,0:T(8,128)(2,1)S(1)}, bf16[256,512]{1,0:T(8,128)(2,1)S(1)}, u32[]{:S(2)}, u32[]{:S(2)}) collective-permute-start(bf16[256,512]{1,0:T(8,128)(2,1)S(1)} %get-tuple-element.35.refs_0_), channel_id=1, source_target_pairs={{0,2},{1,3},{2,0},{3,1},{4,6},{5,7},{6,4},{7,5},{8,10},{9,11},{10,... | collective-permute-start | bytes 786440 | tf_op jit(solution)/shard_map/ppermute | solution.py:360
  67.5 11.1 %collective-permute-start.3 = (bf16[256,512]{1,0:T(8,128)(2,1)S(1)}, bf16[256,512]{1,0:T(8,128)(2,1)S(1)}, u32[]{:S(2)}, u32[]{:S(2)}) collective-permute-start(bf16[256,512]{1,0:T(8,128)(2,1)S(1)} %get-tuple-element.35.refs_0_), channel_id=1, source_target_pairs={{0,3},{1,0},{2,1},{3,2},{4,7},{5,4},{6,5},{7,6},{8,11},{9,8},{10,9... | collective-permute-start | bytes 786440 | tf_op jit(solution)/shard_map/ppermute | solution.py:360
  68.6 13.3 %collective-permute-start.10 = (bf16[256,512]{1,0:T(8,128)(2,1)S(1)}, bf16[256,512]{1,0:T(8,128)(2,1)S(1)}, u32[]{:S(2)}, u32[]{:S(2)}) collective-permute-start(bf16[256,512]{1,0:T(8,128)(2,1)S(1)} %get-tuple-element.47.refs_11_.refs_0_), channel_id=1, source_target_pairs={{0,4},{4,0},{1,5},{5,1},{2,6},{6,2},{3,7},{7,3},{8,12},{12,8},{9,1... | collective-permute-start | bytes 786440 | tf_op jit(solution)/shard_map/ppermute | solution.py:360
  79.3 9.3 %collective-permute-start.13 = (bf16[256,512]{1,0:T(8,128)(2,1)S(1)}, bf16[256,512]{1,0:T(8,128)(2,1)S(1)}, u32[]{:S(2)}, u32[]{:S(2)}) collective-permute-start(bf16[256,512]{1,0:T(8,128)(2,1)S(1)} %shard_map.92), channel_id=1, source_target_pairs={{0,4},{4,0},{1,5},{5,1},{2,6},{6,2},{3,7},{7,3},{8,12},{12,8},{9,1... | collective-permute-start | bytes 786440 | tf_op jit(solution)/shard_map/ppermute | solution.py:360
  82.9 8.2 %collective-permute-start.14 = (bf16[256,512]{1,0:T(8,128)(2,1)S(1)}, bf16[256,512]{1,0:T(8,128)(2,1)S(1)}, u32[]{:S(2)}, u32[]{:S(2)}) collective-permute-start(bf16[256,512]{1,0:T(8,128)(2,1)S(1)} %get-tuple-element.54), channel_id=1, source_target_pairs={{0,1},{1,2},{2,3},{3,0},{4,5},{5,6},{6,7},{7,4},{8,9},{9,10},{10,1... | collective-permute-start | bytes 786440 | tf_op jit(solution)/shard_map/ppermute | solution.py:360
  85.0 13.5 %collective-permute-start.15 = (bf16[256,512]{1,0:T(8,128)(2,1)S(1)}, bf16[256,512]{1,0:T(8,128)(2,1)S(1)}, u32[]{:S(2)}, u32[]{:S(2)}) collective-permute-start(bf16[256,512]{1,0:T(8,128)(2,1)S(1)} %get-tuple-element.55), channel_id=1, source_target_pairs={{0,2},{1,3},{2,0},{3,1},{4,6},{5,7},{6,4},{7,5},{8,10},{9,11},{10,... | collective-permute-start | bytes 786440 | tf_op jit(solution)/shard_map/ppermute | solution.py:360
  87.6 11.0 %collective-permute-start.16 = (bf16[256,512]{1,0:T(8,128)(2,1)S(1)}, bf16[256,512]{1,0:T(8,128)(2,1)S(1)}, u32[]{:S(2)}, u32[]{:S(2)}) collective-permute-start(bf16[256,512]{1,0:T(8,128)(2,1)S(1)} %get-tuple-element.56), channel_id=1, source_target_pairs={{0,3},{1,0},{2,1},{3,2},{4,7},{5,4},{6,5},{7,6},{8,11},{9,8},{10,9... | collective-permute-start | bytes 786440 | tf_op jit(solution)/shard_map/ppermute | solution.py:360

commit v7 on v6

--- a/solution.py
+++ b/solution.py
@@ -140,13 +140,11 @@
         c.wait()
 
 
-def featured(x, edge_ref, taps_ref, ext, s, cut=slice(None)):
-    tokens = x.shape[0]
-    ext[EDGE : EDGE + tokens, cut] = x.astype(f32)
-    ext[:EDGE, cut] = edge_ref[s, :, cut].astype(f32)
-    total = taps_ref[s, 0:1, cut] * ext[EDGE : EDGE + tokens, cut]
+def featured(x, edge_ref, taps_ref, s, cut=slice(None)):
+    whole = jnp.concatenate([edge_ref[s, :, cut].astype(f32), x.astype(f32)], 0)
+    total = taps_ref[s, 0:1, cut] * whole[EDGE:]
     for j in range(1, taps_ref.shape[1]):
-        total = total + taps_ref[s, j : j + 1, cut] * ext[EDGE - j : EDGE - j + tokens, cut]
+        total = total + taps_ref[s, j : j + 1, cut] * pltpu.roll(whole, j, 0)[EDGE:]
     return total
 
 
@@ -155,14 +153,14 @@
         c.wait()
 
 
-def gate_in_kernel(edge_ref, keys_ref, values_ref, taps_ref, out_hbm, ext, out_ref, sem):
+def gate_in_kernel(edge_ref, keys_ref, values_ref, taps_ref, out_hbm, out_ref, sem):
     parts = 4
     size = keys_ref.shape[1] // parts
     outs = []
     for p in range(parts):
         cut = slice(p * size, (p + 1) * size)
-        key = featured(keys_ref[:, cut], edge_ref, taps_ref, ext, 1, cut)
-        product = key * featured(values_ref[:, cut], edge_ref, taps_ref, ext, 2, cut)
+        key = featured(keys_ref[:, cut], edge_ref, taps_ref, 1, cut)
+        product = key * featured(values_ref[:, cut], edge_ref, taps_ref, 2, cut)
         out_ref[cut, :] = product.T.astype(bf16)
         outs.append(pltpu.make_async_copy(out_ref.at[cut], out_hbm.at[cut], sem.at[p]))
         outs[-1].start()
@@ -170,8 +168,8 @@
         c.wait()
 
 
-def query_kernel(x_ref, edge_ref, taps_ref, out_ref, ext):
-    out_ref[...] = featured(x_ref[0], edge_ref, taps_ref, ext, 0)
+def query_kernel(x_ref, edge_ref, taps_ref, out_ref):
+    out_ref[...] = featured(x_ref[0], edge_ref, taps_ref, 0)
 
 
 def gate_out_kernel(query_ref, conv_ref, upper_ref, lower_ref):
@@ -322,10 +320,9 @@
         load_kernel, [((tokens, width), bf16)] * 2 + [(short_filter.shape, f32)],
         [pltpu.SemaphoreType.DMA((3,))], 0, streams_first, short_filter, specs=[HBM] * 2,
     )
-    ext = [pltpu.VMEM((tokens + EDGE, width), f32)]
     gated_in = call(
         gate_in_kernel, [((width, tokens), bf16)],
-        ext + [pltpu.VMEM((width, tokens), bf16), pltpu.SemaphoreType.DMA((4,))],
+        [pltpu.VMEM((width, tokens), bf16), pltpu.SemaphoreType.DMA((4,))],
         0, edge, *loaded, outs_at=HBM,
     )
     gated_in, out_weight = lax.optimization_barrier((gated_in, out_weight))
@@ -352,7 +349,7 @@
     spectrum = transform(long_filter, fwd1, fwd2, twist)
     convolved = convolve(signal, spectrum, fwd1, fwd2, inv2, twist)
     returned = lax.all_to_all(convolved, CTX, 0, 0).reshape(width, tokens)
-    query = call(query_kernel, [((tokens, width), f32)], ext, 0, streams_first, edge, short_filter)
+    query = call(query_kernel, [((tokens, width), f32)], [], 0, streams_first, edge, short_filter)
     half = tokens // 2
     upper, lower = call(gate_out_kernel, [((half, width), bf16)] * 2, [], 0, query, returned)
 

time: 99.9 us -> 99.8 us (level)
  transfers between devices with their start and end apart: 19 -> 19, of which waited for: 9 -> 9; matrix products, arithmetic and copies ran while one was open for 0% -> 0% of each run, Pallas kernels for 20% -> 19%
where the time goes in v7:
time: 99.8 us; the launch traced here: 99.4 us
  starting transfers between devices  48.7 us (49%)
  waiting for transfers between devices  25.7 us (26%)
  Pallas kernels  21.8 us (22%)
  local copies, waits for them, and re-layouts  2.91 us (3%)
    pallas_call x13, Pallas kernels, call(): pl.pallas_call(kernel, out_shape=shapes, in_specs=specs, out_specs=[outs_...  21.8 us
    ppermute x8, starting transfers between devices, send(): return lax.ppermute(block, axis, ring(axis, shift))  14.8 us
    ppermute x8, waiting for transfers between devices, send(): return lax.ppermute(block, axis, ring(axis, shift))  12.5 us
    all_to_all x1, starting transfers between devices, body(): signal = lax.all_to_all(gated_in.reshape(ctx, mine, tokens), CTX, 0, 0)  11.5 us
    ppermute x4, waiting for transfers between devices, swapped(): came = lax.ppermute(block, axis, route)  9.12 us
    ppermute x4, starting transfers between devices, swapped(): came = lax.ppermute(block, axis, route)  8.61 us
    all_to_all x1, starting transfers between devices, body(): returned = lax.all_to_all(convolved, CTX, 0, 0).reshape(width, tokens)  5.61 us
    ppermute x1, starting transfers between devices, body(): lax.ppermute(streams_first[:, tokens - EDGE:, :], CTX, [(i, i + 1) for i...  4.57 us
  transfers between devices with their start and end apart: 19, of which 9 were waited for; matrix products, arithmetic and copies ran while one was open for 0% of the time, Pallas kernels for 19%

profile of v7, /device:TPU:1, one launch (start us, length us, event | category | flops | bytes accessed | tf_op | source)
XLA Modules:
  0.0 99.4 jit_solution(15966214205247939349)
XLA Ops:
  0.0 0.7 slice.4
  0.7 4.6 %collective-permute-start = (bf16[3,8,512]{2,1,0:T(8,128)(2,1)S(1)}, bf16[3,8,512]{2,1,0:T(8,128)(2,1)S(1)}, u32[]{:S(2)}, u32[]{:S(2)}) collective-permute-start(bf16[3,8,512]{2,1,0:T(8,128)(2,1)S(1)} %slice.4), channel_id=1, source_target_pairs={{0,8},{8,16},{16,24},{24,32},{32,40},{40,48},{48,56},{56,64},{64,7... | collective-permute-start | bytes 73736 | tf_op jit(solution)/shard_map/ppermute | solution.py:318
  5.3 1.2 %shard_map.83 = (bf16[512,512]{1,0:T(8,128)(2,1)S(1)}, bf16[512,512]{1,0:T(8,128)(2,1)S(1)}, f32[3,3,512]{2,1,0:T(4,128)S(1)}) custom-call(bf16[3,512,512]{2,1,0:T(8,128)(2,1)} %bitcast.5, f32[3,3,512]{2,1,0:T(4,128)} %taps_hbm.1), custom_call_target="tpu_custom_call" | custom-call | bytes 1591296 | tf_op jit(solution)/shard_map/pallas_call | solution.py:279
  6.6 0.0 collective-permute-done.edge_ref
  6.6 1.5 %shard_map.84 = bf16[512,512]{1,0:T(8,128)(2,1)} custom-call(bf16[3,8,512]{2,1,0:T(8,128)(2,1)S(1)} %collective-permute-done.edge_ref, bf16[512,512]{1,0:T(8,128)(2,1)S(1)} %get-tuple-element.31.keys_ref, bf16[512,512]{1,0:T(8,128)(2,1)S(1)} %get-tuple-element.32.values_ref, f32[3,3,512]{2,1,0:T(4,128)S(1)} %get-tuple-element.33.taps_ref), custom_call_target="tpu_custom_call" | custom-call | bytes 1091584 | tf_op jit(solution)/shard_map/pallas_call | solution.py:279
  8.1 11.5 %all-to-all-start = ((bf16[32,16,512]{2,1,0:T(8,128)(2,1)}), bf16[32,16,512]{2,1,0:T(8,128)(2,1)S(1)}, u32[]{:S(2)}, u32[]{:S(2)}) async-start(bf16[32,16,512]{2,1,0:T(8,128)(2,1)} %bitcast.1), calls=%async_computation | async-start | bytes 1048576 | tf_op jit(solution)/shard_map/all_to_all | solution.py:329
  19.7 0.0 copy-start.2
  19.7 0.0 copy-start.5
  19.7 0.0 copy-start.6
  19.7 0.0 copy-start.7
  19.7 3.2 %shard_map.88 = (bf16[2,256,512]{2,1,0:T(8,128)(2,1)}, bf16[2,256,512]{2,1,0:T(8,128)(2,1)}, bf16[2,256,512]{2,1,0:T(8,128)(2,1)S(1)}, bf16[4,256,512]{2,1,0:T(8,128)(2,1)}) custom-call(bf16[512,4096]{1,0:T(8,128)(2,1)} %refs_0_.3), custom_call_target="tpu_custom_call" | custom-call | bytes 4194304 | tf_op jit(solution)/shard_map/pallas_call | solution.py:279
  23.0 0.0 copy-start.3
  23.0 0.8 copy-done.3
  23.8 3.1 %collective-permute-start.11 = (bf16[4,256,512]{2,1,0:T(8,128)(2,1)}, bf16[4,256,512]{2,1,0:T(8,128)(2,1)}, u32[]{:S(2)}, u32[]{:S(2)}) collective-permute-start(bf16[4,256,512]{2,1,0:T(8,128)(2,1)} %get-tuple-element.48), channel_id=1, source_target_pairs={{0,20},{4,16},{16,4},{20,0},{1,21},{5,17},{17,5},{21,1},{2,22},{6,... | collective-permute-start | bytes 3145736 | tf_op jit(solution)/shard_map/ppermute | solution.py:341
  26.9 0.0 copy-done.2
  26.9 0.0 copy-done.5
  26.9 0.0 copy-done.6
  26.9 0.0 copy-done.7
  26.9 1.9 %shard_map.85.refs_3_ = f32[16,128,256]{2,1,0:T(8,128)S(1)} custom-call(f32[16,16384]{1,0:T(8,128)S(1)} %bitcast.8, bf16[256,256]{1,0:T(8,128)(2,1)S(1)} %copy-done.6, bf16[2,256,256]{2,1,0:T(8,128)(2,1)S(1)} %copy-done.5, f32[2,128,128]{2,1,0:T(8,128)S(1)} %copy-done.7), custom_call_target="tpu_custom_call" | custom-call | flops 1000000000 | bytes 1572864 | tf_op jit(solution)/shard_map/pallas_call | solution.py:279
  28.8 0.0 copy-start.8
  28.8 1.3 %copy-done.8 = f32[16,128,256]{2,1,0:T(8,128)} copy-done((f32[16,128,256]{2,1,0:T(8,128)}, f32[16,128,256]{2,1,0:T(8,128)S(1)}, u32[]{:S(2)}) %copy-start.8) | copy-done | bytes 2097176
  30.1 1.2 %collective-permute-start.4 = (bf16[2,256,512]{2,1,0:T(8,128)(2,1)}, bf16[2,256,512]{2,1,0:T(8,128)(2,1)}, u32[]{:S(2)}, u32[]{:S(2)}) collective-permute-start(bf16[2,256,512]{2,1,0:T(8,128)(2,1)} %get-tuple-element.37), channel_id=1, source_target_pairs={{0,1},{1,2},{2,3},{3,0},{4,5},{5,6},{6,7},{7,4},{8,9},{9,10},{10,1... | collective-permute-start | bytes 1572872 | tf_op jit(solution)/shard_map/ppermute | solution.py:341
  31.4 2.4 %collective-permute-start.6 = (bf16[2,256,512]{2,1,0:T(8,128)(2,1)}, bf16[2,256,512]{2,1,0:T(8,128)(2,1)}, u32[]{:S(2)}, u32[]{:S(2)}) collective-permute-start(bf16[2,256,512]{2,1,0:T(8,128)(2,1)} %get-tuple-element.38), channel_id=1, source_target_pairs={{0,2},{1,3},{2,0},{3,1},{4,6},{5,7},{6,4},{7,5},{8,10},{9,11},{10,... | collective-permute-start | bytes 1572872 | tf_op jit(solution)/shard_map/ppermute | solution.py:341
  33.8 2.4 %all-to-all-done.u_ref = bf16[32,16,512]{2,1,0:T(8,128)(2,1)S(1)} async-done(((bf16[32,16,512]{2,1,0:T(8,128)(2,1)}), bf16[32,16,512]{2,1,0:T(8,128)(2,1)S(1)}, u32[]{:S(2)}, u32[]{:S(2)}) %all-to-all-start) | async-done | bytes 524320 | tf_op jit(solution)/shard_map/all_to_all | solution.py:329
  36.2 5.3 %shard_map.86 = bf16[32,16,512]{2,1,0:T(8,128)(2,1)} custom-call(bf16[32,16,512]{2,1,0:T(8,128)(2,1)S(1)} %all-to-all-done.u_ref, bf16[256,256]{1,0:T(8,128)(2,1)} %constant.8.clone.fwd1_ref.refs_0_, f32[2,128,128]{2,1,0:T(8,128)} %constant.11.clone.twist_ref.refs_1_, bf16[2,256,256]{2,1,0:T(8,128)(2,1)} %constant.9.clone.fwd2_ref.refs_2_, ...), custom_call_target="tpu_custom_call" | custom-call | flops 3000000000 | bytes 3276800 | tf_op jit(solution)/shard_map/pallas_call | solution.py:279
  41.5 5.6 %all-to-all-start.1 = ((bf16[32,16,512]{2,1,0:T(8,128)(2,1)}), bf16[32,16,512]{2,1,0:T(8,128)(2,1)S(1)}, u32[]{:S(2)}, u32[]{:S(2)}) async-start(bf16[32,16,512]{2,1,0:T(8,128)(2,1)} %shard_map.86), calls=%async_computation.1 | async-start | bytes 1048576 | tf_op jit(solution)/shard_map/all_to_all | solution.py:351
  47.1 1.8 %collective-permute-start.8 = (bf16[2,256,512]{2,1,0:T(8,128)(2,1)S(1)}, bf16[2,256,512]{2,1,0:T(8,128)(2,1)}, u32[]{:S(2)}, u32[]{:S(2)}) collective-permute-start(bf16[2,256,512]{2,1,0:T(8,128)(2,1)S(1)} %copy-done.4), channel_id=1, source_target_pairs={{0,3},{1,0},{2,1},{3,2},{4,7},{5,4},{6,5},{7,6},{8,11},{9,8},{10,9... | collective-permute-start | bytes 1572872 | tf_op jit(solution)/shard_map/ppermute | solution.py:341
  49.0 1.4 %collective-permute-done.11.refs_1_ = bf16[4,256,512]{2,1,0:T(8,128)(2,1)} collective-permute-done((bf16[4,256,512]{2,1,0:T(8,128)(2,1)}, bf16[4,256,512]{2,1,0:T(8,128)(2,1)}, u32[]{:S(2)}, u32[]{:S(2)}) %collective-permute-start.11) | collective-permute-done | bytes 1048608 | tf_op jit(solution)/shard_map/ppermute | solution.py:341
  50.3 1.0 collective-permute-start.12
  51.3 0.0 collective-permute-done.4.refs_1_
  51.3 0.0 collective-permute-start.5
  51.3 5.4 %collective-permute-done.6.refs_3_ = bf16[2,256,512]{2,1,0:T(8,128)(2,1)} collective-permute-done((bf16[2,256,512]{2,1,0:T(8,128)(2,1)}, bf16[2,256,512]{2,1,0:T(8,128)(2,1)}, u32[]{:S(2)}, u32[]{:S(2)}) %collective-permute-start.6) | collective-permute-done | bytes 524320 | tf_op jit(solution)/shard_map/ppermute | solution.py:341
  56.7 1.5 %collective-permute-start.7 = (bf16[2,256,512]{2,1,0:T(8,128)(2,1)}, bf16[2,256,512]{2,1,0:T(8,128)(2,1)}, u32[]{:S(2)}, u32[]{:S(2)}) collective-permute-start(bf16[2,256,512]{2,1,0:T(8,128)(2,1)} %collective-permute-done.6.refs_3_), channel_id=1, source_target_pairs={{0,8},{8,0},{1,9},{9,1},{2,10},{10,2},{3,11},{11,3},{4,12},{12,4},... | collective-permute-start | bytes 1572872 | tf_op jit(solution)/shard_map/ppermute | solution.py:342
  58.2 2.3 %collective-permute-done.8.refs_5_ = bf16[2,256,512]{2,1,0:T(8,128)(2,1)} collective-permute-done((bf16[2,256,512]{2,1,0:T(8,128)(2,1)S(1)}, bf16[2,256,512]{2,1,0:T(8,128)(2,1)}, u32[]{:S(2)}, u32[]{:S(2)}) %collective-permute-start.8) | collective-permute-done | bytes 524320 | tf_op jit(solution)/shard_map/ppermute | solution.py:341
  60.6 1.1 %collective-permute-start.9 = (bf16[2,256,512]{2,1,0:T(8,128)(2,1)}, bf16[2,256,512]{2,1,0:T(8,128)(2,1)}, u32[]{:S(2)}, u32[]{:S(2)}) collective-permute-start(bf16[2,256,512]{2,1,0:T(8,128)(2,1)} %collective-permute-done.8.refs_5_), channel_id=1, source_target_pairs={{0,8},{8,0},{1,9},{9,1},{2,10},{10,2},{3,11},{11,3},{4,12},{12,4},... | collective-permute-start | bytes 1572872 | tf_op jit(solution)/shard_map/ppermute | solution.py:342
  61.7 0.3 shard_map.82.query_ref
  62.0 1.7 %all-to-all-done.1 = bf16[32,16,512]{2,1,0:T(8,128)(2,1)S(1)} async-done(((bf16[32,16,512]{2,1,0:T(8,128)(2,1)}), bf16[32,16,512]{2,1,0:T(8,128)(2,1)S(1)}, u32[]{:S(2)}, u32[]{:S(2)}) %all-to-all-start.1) | async-done | bytes 524320 | tf_op jit(solution)/shard_map/all_to_all | solution.py:351
  63.7 0.2 shard_map.87
  63.9 1.0 %collective-permute-start.1 = (bf16[256,512]{1,0:T(8,128)(2,1)S(1)}, bf16[256,512]{1,0:T(8,128)(2,1)S(1)}, u32[]{:S(2)}, u32[]{:S(2)}) collective-permute-start(bf16[256,512]{1,0:T(8,128)(2,1)S(1)} %get-tuple-element.35.refs_0_), channel_id=1, source_target_pairs={{0,1},{1,2},{2,3},{3,0},{4,5},{5,6},{6,7},{7,4},{8,9},{9,10},{10,1... | collective-permute-start | bytes 786440 | tf_op jit(solution)/shard_map/ppermute | solution.py:357
  64.9 0.0 collective-permute-done.5.refs_2_
  64.9 2.4 %collective-permute-start.2 = (bf16[256,512]{1,0:T(8,128)(2,1)S(1)}, bf16[256,512]{1,0:T(8,128)(2,1)S(1)}, u32[]{:S(2)}, u32[]{:S(2)}) collective-permute-start(bf16[256,512]{1,0:T(8,128)(2,1)S(1)} %get-tuple-element.35.refs_0_), channel_id=1, source_target_pairs={{0,2},{1,3},{2,0},{3,1},{4,6},{5,7},{6,4},{7,5},{8,10},{9,11},{10,... | collective-permute-start | bytes 786440 | tf_op jit(solution)/shard_map/ppermute | solution.py:357
  67.4 0.0 collective-permute-done.7.refs_4_
  67.4 1.2 %collective-permute-start.3 = (bf16[256,512]{1,0:T(8,128)(2,1)S(1)}, bf16[256,512]{1,0:T(8,128)(2,1)S(1)}, u32[]{:S(2)}, u32[]{:S(2)}) collective-permute-start(bf16[256,512]{1,0:T(8,128)(2,1)S(1)} %get-tuple-element.35.refs_0_), channel_id=1, source_target_pairs={{0,3},{1,0},{2,1},{3,2},{4,7},{5,4},{6,5},{7,6},{8,11},{9,8},{10,9... | collective-permute-start | bytes 786440 | tf_op jit(solution)/shard_map/ppermute | solution.py:357
  68.5 0.0 collective-permute-done.9.refs_6_
  68.5 2.9 %collective-permute-start.10 = (bf16[256,512]{1,0:T(8,128)(2,1)S(1)}, bf16[256,512]{1,0:T(8,128)(2,1)S(1)}, u32[]{:S(2)}, u32[]{:S(2)}) collective-permute-start(bf16[256,512]{1,0:T(8,128)(2,1)S(1)} %get-tuple-element.47.refs_11_.refs_0_), channel_id=1, source_target_pairs={{0,4},{4,0},{1,5},{5,1},{2,6},{6,2},{3,7},{7,3},{8,12},{12,8},{9,1... | collective-permute-start | bytes 786440 | tf_op jit(solution)/shard_map/ppermute | solution.py:357
  71.4 2.2 %shard_map.89 = (bf16[2,512,512]{2,1,0:T(8,128)(2,1)S(1)}, bf16[2,256,512]{2,1,0:T(8,128)(2,1)S(1)}, bf16[2,256,512]{2,1,0:T(8,128)(2,1)S(1)}, bf16[2,256,512]{2...) custom-call(bf16[512,4096]{1,0:T(8,128)(2,1)} %refs_0_.3, ...), custom_call_target="tpu_custom_call" | custom-call | bytes 7340032 | tf_op jit(solution)/shard_map/pallas_call | solution.py:279
  73.7 0.0 collective-permute-done.12.refs_2_
  73.7 2.3 %shard_map.90 = (bf16[4,512,512]{2,1,0:T(8,128)(2,1)S(1)}, bf16[4,256,512]{2,1,0:T(8,128)(2,1)S(1)}, bf16[4,256,512]{2,1,0:T(8,128)(2,1)S(1)}) custom-call(bf16[512,4096]{1,0:T(8,128)(2,1)} %refs_0_.3, bf16[4,256,512]{2,1,0:T(8,128)(2,1)} %collective-permute-done.11.refs_1_, bf16[4,256,512]{2,1,0:T(8,128)(2,1)} %collective-permute-done.12.refs_2_), custom_call_target="tpu_custom_call" | custom-call | bytes 6291456 | tf_op jit(solution)/shard_map/pallas_call | solution.py:279
  76.0 0.0 collective-permute-done.1.refs_1_
  76.0 2.1 %collective-permute-done.2.refs_2_ = bf16[256,512]{1,0:T(8,128)(2,1)S(1)} collective-permute-done((bf16[256,512]{1,0:T(8,128)(2,1)S(1)}, bf16[256,512]{1,0:T(8,128)(2,1)S(1)}, u32[]{:S(2)}, u32[]{:S(2)}) %collective-permute-start.2) | collective-permute-done | bytes 262176 | tf_op jit(solution)/shard_map/ppermute | solution.py:357
  78.1 0.4 collective-permute-done.3.refs_3_
  78.5 0.7 shard_map.92
  79.2 2.6 %collective-permute-start.13 = (bf16[256,512]{1,0:T(8,128)(2,1)S(1)}, bf16[256,512]{1,0:T(8,128)(2,1)S(1)}, u32[]{:S(2)}, u32[]{:S(2)}) collective-permute-start(bf16[256,512]{1,0:T(8,128)(2,1)S(1)} %shard_map.92), channel_id=1, source_target_pairs={{0,4},{4,0},{1,5},{5,1},{2,6},{6,2},{3,7},{7,3},{8,12},{12,8},{9,1... | collective-permute-start | bytes 786440 | tf_op jit(solution)/shard_map/ppermute | solution.py:357
  81.8 0.0 collective-permute-done.10.refs_12_.refs_1_
  81.8 1.0 shard_map.93
  82.8 2.1 %collective-permute-start.14 = (bf16[256,512]{1,0:T(8,128)(2,1)S(1)}, bf16[256,512]{1,0:T(8,128)(2,1)S(1)}, u32[]{:S(2)}, u32[]{:S(2)}) collective-permute-start(bf16[256,512]{1,0:T(8,128)(2,1)S(1)} %get-tuple-element.54), channel_id=1, source_target_pairs={{0,1},{1,2},{2,3},{3,0},{4,5},{5,6},{6,7},{7,4},{8,9},{9,10},{10,1... | collective-permute-start | bytes 786440 | tf_op jit(solution)/shard_map/ppermute | solution.py:357
  84.9 2.5 %collective-permute-start.15 = (bf16[256,512]{1,0:T(8,128)(2,1)S(1)}, bf16[256,512]{1,0:T(8,128)(2,1)S(1)}, u32[]{:S(2)}, u32[]{:S(2)}) collective-permute-start(bf16[256,512]{1,0:T(8,128)(2,1)S(1)} %get-tuple-element.55), channel_id=1, source_target_pairs={{0,2},{1,3},{2,0},{3,1},{4,6},{5,7},{6,4},{7,5},{8,10},{9,11},{10,... | collective-permute-start | bytes 786440 | tf_op jit(solution)/shard_map/ppermute | solution.py:357
  87.5 0.0 collective-permute-start.16
  87.5 1.0 shard_map.91
  88.4 0.0 collective-permute-done.13.refs_0_
  88.4 2.5 %collective-permute-done.14.refs_1_ = bf16[256,512]{1,0:T(8,128)(2,1)S(1)} collective-permute-done((bf16[256,512]{1,0:T(8,128)(2,1)S(1)}, bf16[256,512]{1,0:T(8,128)(2,1)S(1)}, u32[]{:S(2)}, u32[]{:S(2)}) %collective-permute-start.14) | collective-permute-done | bytes 262176 | tf_op jit(solution)/shard_map/ppermute | solution.py:357
  91.0 7.5 %collective-permute-done.15.refs_2_ = bf16[256,512]{1,0:T(8,128)(2,1)S(1)} collective-permute-done((bf16[256,512]{1,0:T(8,128)(2,1)S(1)}, bf16[256,512]{1,0:T(8,128)(2,1)S(1)}, u32[]{:S(2)}, u32[]{:S(2)}) %collective-permute-start.15) | collective-permute-done | bytes 262176 | tf_op jit(solution)/shard_map/ppermute | solution.py:357
  98.5 0.0 collective-permute-done.16.refs_3_
  98.5 0.9 shard_map.94
  (6 shorter events, 0.0 us)
Async XLA Ops:
  0.7 5.8 %collective-permute-start = (bf16[3,8,512]{2,1,0:T(8,128)(2,1)S(1)}, bf16[3,8,512]{2,1,0:T(8,128)(2,1)S(1)}, u32[]{:S(2)}, u32[]{:S(2)}) collective-permute-start(bf16[3,8,512]{2,1,0:T(8,128)(2,1)S(1)} %slice.4), channel_id=1, source_target_pairs={{0,8},{8,16},{16,24},{24,32},{32,40},{40,48},{48,56},{56,64},{64,7... | collective-permute-start | bytes 73736 | tf_op jit(solution)/shard_map/ppermute | solution.py:318
  8.1 28.1 %all-to-all-start = ((bf16[32,16,512]{2,1,0:T(8,128)(2,1)}), bf16[32,16,512]{2,1,0:T(8,128)(2,1)S(1)}, u32[]{:S(2)}, u32[]{:S(2)}) async-start(bf16[32,16,512]{2,1,0:T(8,128)(2,1)} %bitcast.1), calls=%async_computation | async-start | bytes 1048576 | tf_op jit(solution)/shard_map/all_to_all | solution.py:329
  19.7 7.2 %copy-start.2 = (f32[16384,16]{0,1:T(8,128)S(1)}, f32[16384,16]{0,1:T(8,128)}, u32[]{:S(2)}) copy-start(f32[16384,16]{0,1:T(8,128)} %param.10) | copy-start | bytes 3145732
  19.7 7.2 %copy-start.5 = (bf16[2,256,256]{2,1,0:T(8,128)(2,1)S(1)}, bf16[2,256,256]{2,1,0:T(8,128)(2,1)}, u32[]{:S(2)}) copy-start(bf16[2,256,256]{2,1,0:T(8,128)(2,1)} %constant.9.clone.fwd2_ref.refs_2_) | copy-start | bytes 786436
  19.7 7.2 %copy-start.6 = (bf16[256,256]{1,0:T(8,128)(2,1)S(1)}, bf16[256,256]{1,0:T(8,128)(2,1)}, u32[]{:S(2)}) copy-start(bf16[256,256]{1,0:T(8,128)(2,1)} %constant.8.clone.fwd1_ref.refs_0_) | copy-start | bytes 393220
  19.7 7.2 %copy-start.7 = (f32[2,128,128]{2,1,0:T(8,128)S(1)}, f32[2,128,128]{2,1,0:T(8,128)}, u32[]{:S(2)}) copy-start(f32[2,128,128]{2,1,0:T(8,128)} %constant.11.clone.twist_ref.refs_1_) | copy-start | bytes 393220
  23.0 0.8 copy-start.3
  23.8 26.5 %collective-permute-start.11 = (bf16[4,256,512]{2,1,0:T(8,128)(2,1)}, bf16[4,256,512]{2,1,0:T(8,128)(2,1)}, u32[]{:S(2)}, u32[]{:S(2)}) collective-permute-start(bf16[4,256,512]{2,1,0:T(8,128)(2,1)} %get-tuple-element.48), channel_id=1, source_target_pairs={{0,20},{4,16},{16,4},{20,0},{1,21},{5,17},{17,5},{21,1},{2,22},{6,... | collective-permute-start | bytes 3145736 | tf_op jit(solution)/shard_map/ppermute | solution.py:341
  28.8 1.3 %copy-start.8 = (f32[16,128,256]{2,1,0:T(8,128)}, f32[16,128,256]{2,1,0:T(8,128)S(1)}, u32[]{:S(2)}) copy-start(f32[16,128,256]{2,1,0:T(8,128)S(1)} %shard_map.85.refs_3_) | copy-start | bytes 6291460
  30.1 21.2 %collective-permute-start.4 = (bf16[2,256,512]{2,1,0:T(8,128)(2,1)}, bf16[2,256,512]{2,1,0:T(8,128)(2,1)}, u32[]{:S(2)}, u32[]{:S(2)}) collective-permute-start(bf16[2,256,512]{2,1,0:T(8,128)(2,1)} %get-tuple-element.37), channel_id=1, source_target_pairs={{0,1},{1,2},{2,3},{3,0},{4,5},{5,6},{6,7},{7,4},{8,9},{9,10},{10,1... | collective-permute-start | bytes 1572872 | tf_op jit(solution)/shard_map/ppermute | solution.py:341
  31.4 15.8 %copy-start.4 = (bf16[2,256,512]{2,1,0:T(8,128)(2,1)S(1)}, bf16[2,256,512]{2,1,0:T(8,128)(2,1)}, u32[]{:S(2)}) copy-start(bf16[2,256,512]{2,1,0:T(8,128)(2,1)} %copy-done.3) | copy-start | bytes 1572868
  31.4 30.3 %copy-start.1 = (f32[3,3,512]{2,1,0:T(4,128)S(1)}, f32[3,3,512]{2,1,0:T(4,128)}, u32[]{:S(2)}) copy-start(f32[3,3,512]{2,1,0:T(4,128)} %taps_hbm.1) | copy-start | bytes 55300
  31.4 25.4 %collective-permute-start.6 = (bf16[2,256,512]{2,1,0:T(8,128)(2,1)}, bf16[2,256,512]{2,1,0:T(8,128)(2,1)}, u32[]{:S(2)}, u32[]{:S(2)}) collective-permute-start(bf16[2,256,512]{2,1,0:T(8,128)(2,1)} %get-tuple-element.38), channel_id=1, source_target_pairs={{0,2},{1,3},{2,0},{3,1},{4,6},{5,7},{6,4},{7,5},{8,10},{9,11},{10,... | collective-permute-start | bytes 1572872 | tf_op jit(solution)/shard_map/ppermute | solution.py:341
  36.2 25.4 %copy-start = (bf16[512,3,512]{2,0,1:T(8,128)(2,1)S(1)}, bf16[512,3,512]{2,0,1:T(8,128)(2,1)}, u32[]{:S(2)}) copy-start(bf16[512,3,512]{2,0,1:T(8,128)(2,1)} %param.8) | copy-start | bytes 4718596
  41.5 22.2 %all-to-all-start.1 = ((bf16[32,16,512]{2,1,0:T(8,128)(2,1)}), bf16[32,16,512]{2,1,0:T(8,128)(2,1)S(1)}, u32[]{:S(2)}, u32[]{:S(2)}) async-start(bf16[32,16,512]{2,1,0:T(8,128)(2,1)} %shard_map.86), calls=%async_computation.1 | async-start | bytes 1048576 | tf_op jit(solution)/shard_map/all_to_all | solution.py:351
  47.1 13.4 %collective-permute-start.8 = (bf16[2,256,512]{2,1,0:T(8,128)(2,1)S(1)}, bf16[2,256,512]{2,1,0:T(8,128)(2,1)}, u32[]{:S(2)}, u32[]{:S(2)}) collective-permute-start(bf16[2,256,512]{2,1,0:T(8,128)(2,1)S(1)} %copy-done.4), channel_id=1, source_target_pairs={{0,3},{1,0},{2,1},{3,2},{4,7},{5,4},{6,5},{7,6},{8,11},{9,8},{10,9... | collective-permute-start | bytes 1572872 | tf_op jit(solution)/shard_map/ppermute | solution.py:341
  50.3 23.4 %collective-permute-start.12 = (bf16[4,256,512]{2,1,0:T(8,128)(2,1)}, bf16[4,256,512]{2,1,0:T(8,128)(2,1)}, u32[]{:S(2)}, u32[]{:S(2)}) collective-permute-start(bf16[4,256,512]{2,1,0:T(8,128)(2,1)} %collective-permute-done.11.refs_1_), channel_id=1, source_target_pairs={{0,8},{8,0},{1,9},{9,1},{2,10},{10,2},{3,11},{11,3},{4,12},{12,4},... | collective-permute-start | bytes 3145736 | tf_op jit(solution)/shard_map/ppermute | solution.py:342
  51.3 13.6 %collective-permute-start.5 = (bf16[2,256,512]{2,1,0:T(8,128)(2,1)}, bf16[2,256,512]{2,1,0:T(8,128)(2,1)}, u32[]{:S(2)}, u32[]{:S(2)}) collective-permute-start(bf16[2,256,512]{2,1,0:T(8,128)(2,1)} %collective-permute-done.4.refs_1_), channel_id=1, source_target_pairs={{0,8},{8,0},{1,9},{9,1},{2,10},{10,2},{3,11},{11,3},{4,12},{12,4},... | collective-permute-start | bytes 1572872 | tf_op jit(solution)/shard_map/ppermute | solution.py:342
  56.7 10.6 %collective-permute-start.7 = (bf16[2,256,512]{2,1,0:T(8,128)(2,1)}, bf16[2,256,512]{2,1,0:T(8,128)(2,1)}, u32[]{:S(2)}, u32[]{:S(2)}) collective-permute-start(bf16[2,256,512]{2,1,0:T(8,128)(2,1)} %collective-permute-done.6.refs_3_), channel_id=1, source_target_pairs={{0,8},{8,0},{1,9},{9,1},{2,10},{10,2},{3,11},{11,3},{4,12},{12,4},... | collective-permute-start | bytes 1572872 | tf_op jit(solution)/shard_map/ppermute | solution.py:342
  60.6 8.0 %collective-permute-start.9 = (bf16[2,256,512]{2,1,0:T(8,128)(2,1)}, bf16[2,256,512]{2,1,0:T(8,128)(2,1)}, u32[]{:S(2)}, u32[]{:S(2)}) collective-permute-start(bf16[2,256,512]{2,1,0:T(8,128)(2,1)} %collective-permute-done.8.refs_5_), channel_id=1, source_target_pairs={{0,8},{8,0},{1,9},{9,1},{2,10},{10,2},{3,11},{11,3},{4,12},{12,4},... | collective-permute-start | bytes 1572872 | tf_op jit(solution)/shard_map/ppermute | solution.py:342
  63.9 12.1 %collective-permute-start.1 = (bf16[256,512]{1,0:T(8,128)(2,1)S(1)}, bf16[256,512]{1,0:T(8,128)(2,1)S(1)}, u32[]{:S(2)}, u32[]{:S(2)}) collective-permute-start(bf16[256,512]{1,0:T(8,128)(2,1)S(1)} %get-tuple-element.35.refs_0_), channel_id=1, source_target_pairs={{0,1},{1,2},{2,3},{3,0},{4,5},{5,6},{6,7},{7,4},{8,9},{9,10},{10,1... | collective-permute-start | bytes 786440 | tf_op jit(solution)/shard_map/ppermute | solution.py:357
  64.9 13.1 %collective-permute-start.2 = (bf16[256,512]{1,0:T(8,128)(2,1)S(1)}, bf16[256,512]{1,0:T(8,128)(2,1)S(1)}, u32[]{:S(2)}, u32[]{:S(2)}) collective-permute-start(bf16[256,512]{1,0:T(8,128)(2,1)S(1)} %get-tuple-element.35.refs_0_), channel_id=1, source_target_pairs={{0,2},{1,3},{2,0},{3,1},{4,6},{5,7},{6,4},{7,5},{8,10},{9,11},{10,... | collective-permute-start | bytes 786440 | tf_op jit(solution)/shard_map/ppermute | solution.py:357
  67.4 11.1 %collective-permute-start.3 = (bf16[256,512]{1,0:T(8,128)(2,1)S(1)}, bf16[256,512]{1,0:T(8,128)(2,1)S(1)}, u32[]{:S(2)}, u32[]{:S(2)}) collective-permute-start(bf16[256,512]{1,0:T(8,128)(2,1)S(1)} %get-tuple-element.35.refs_0_), channel_id=1, source_target_pairs={{0,3},{1,0},{2,1},{3,2},{4,7},{5,4},{6,5},{7,6},{8,11},{9,8},{10,9... | collective-permute-start | bytes 786440 | tf_op jit(solution)/shard_map/ppermute | solution.py:357
  68.5 13.3 %collective-permute-start.10 = (bf16[256,512]{1,0:T(8,128)(2,1)S(1)}, bf16[256,512]{1,0:T(8,128)(2,1)S(1)}, u32[]{:S(2)}, u32[]{:S(2)}) collective-permute-start(bf16[256,512]{1,0:T(8,128)(2,1)S(1)} %get-tuple-element.47.refs_11_.refs_0_), channel_id=1, source_target_pairs={{0,4},{4,0},{1,5},{5,1},{2,6},{6,2},{3,7},{7,3},{8,12},{12,8},{9,1... | collective-permute-start | bytes 786440 | tf_op jit(solution)/shard_map/ppermute | solution.py:357
  79.2 9.3 %collective-permute-start.13 = (bf16[256,512]{1,0:T(8,128)(2,1)S(1)}, bf16[256,512]{1,0:T(8,128)(2,1)S(1)}, u32[]{:S(2)}, u32[]{:S(2)}) collective-permute-start(bf16[256,512]{1,0:T(8,128)(2,1)S(1)} %shard_map.92), channel_id=1, source_target_pairs={{0,4},{4,0},{1,5},{5,1},{2,6},{6,2},{3,7},{7,3},{8,12},{12,8},{9,1... | collective-permute-start | bytes 786440 | tf_op jit(solution)/shard_map/ppermute | solution.py:357
  82.8 8.2 %collective-permute-start.14 = (bf16[256,512]{1,0:T(8,128)(2,1)S(1)}, bf16[256,512]{1,0:T(8,128)(2,1)S(1)}, u32[]{:S(2)}, u32[]{:S(2)}) collective-permute-start(bf16[256,512]{1,0:T(8,128)(2,1)S(1)} %get-tuple-element.54), channel_id=1, source_target_pairs={{0,1},{1,2},{2,3},{3,0},{4,5},{5,6},{6,7},{7,4},{8,9},{9,10},{10,1... | collective-permute-start | bytes 786440 | tf_op jit(solution)/shard_map/ppermute | solution.py:357
  84.9 13.6 %collective-permute-start.15 = (bf16[256,512]{1,0:T(8,128)(2,1)S(1)}, bf16[256,512]{1,0:T(8,128)(2,1)S(1)}, u32[]{:S(2)}, u32[]{:S(2)}) collective-permute-start(bf16[256,512]{1,0:T(8,128)(2,1)S(1)} %get-tuple-element.55), channel_id=1, source_target_pairs={{0,2},{1,3},{2,0},{3,1},{4,6},{5,7},{6,4},{7,5},{8,10},{9,11},{10,... | collective-permute-start | bytes 786440 | tf_op jit(solution)/shard_map/ppermute | solution.py:357
  87.5 11.0 %collective-permute-start.16 = (bf16[256,512]{1,0:T(8,128)(2,1)S(1)}, bf16[256,512]{1,0:T(8,128)(2,1)S(1)}, u32[]{:S(2)}, u32[]{:S(2)}) collective-permute-start(bf16[256,512]{1,0:T(8,128)(2,1)S(1)} %get-tuple-element.56), channel_id=1, source_target_pairs={{0,3},{1,0},{2,1},{3,2},{4,7},{5,4},{6,5},{7,6},{8,11},{9,8},{10,9... | collective-permute-start | bytes 786440 | tf_op jit(solution)/shard_map/ppermute | solution.py:357
